TPU v7x, 32 devices: a whole 2x2x4 slice. The times are simulated.
32 devices in a mesh: grp: 4 (over z), frac: 8 (over y, x, core).
Axes of the slice: x: 2, y: 2, z: 4, core: 2. Of those that a mesh axis runs over, the one named last changes fastest.
Arguments:
- matrix_state: float32 [2, 512, 2048], P(None, 'grp', 'frac'), may hold values from 0 to 1
- matrix_perm: float32 [512, 2048], P('grp', 'frac'), may hold values from 0.1 to 10
- frac_state: float32 [2, 4, 65536], P(None, 'grp', 'frac'), may hold values from 0 to 1
- frac_aperture: float32 [4, 65536], P('grp', 'frac'), may hold values from 0.5 to 4
- link_cell: int32 [4, 8, 8, 256], P('grp', 'frac'), may hold values from 0 to 32767
- link_seg: int32 [4, 8, 8, 256], P('grp', 'frac'), may hold values from 0 to 8191
- link_trans: float32 [4, 8, 8, 256], P('grp', 'frac'), may hold values from 0.1 to 2
- link_count: int32 [4, 8, 8], P('grp', 'frac'), may hold values from 32 to 256, as said below
- link_upwind: int32 [3, 4, 8, 8, 256], P(None, 'grp', 'frac'), may hold values from 0 to 1
Outputs:
- matrix_out: float32 [2, 512, 2048], P(None, 'grp', 'frac')
- frac_out: float32 [2, 4, 65536], P(None, 'grp', 'frac')
Inputs may be any that keep to these rules, and one draw needn't show every extreme that they name: `link_count`: in each source device's list at least one owner block holds exactly 256 live slots; slots at or beyond a block's count are padding. `link_cell`: A live slot's cell index lies within the source device's 128 x 256 block. `link_seg`: A slot's segment index counts within the owner's 8192 segments. `link_upwind`: 1 takes the upwind saturation from the matrix cell, 0 from the fracture segment.
All inputs are finite; a program needn't handle non-finite values.
Results may differ from a plain program's by a relative error of at most 0.00002.
Values sent between devices are 32-bit elements; how exact they have to be, the bound alone decides.
No kernel may reach another device: no remote copies, remote signals or barrier semaphores. Data moves between devices by JAX's collectives and lax.ppermute only.
A program may use at most 128 MiB of HBM per device.

v0:
```python
import jax
import jax.numpy as jnp
from jax import lax
from jax.sharding import PartitionSpec as P

ITERS = 3
SWEEPS = 4


LOW_BOUND = 0.02
HIGH_BOUND = 1.98
TAU_STEP = 0.5
MOBILITY_FLOOR = 0.2


def extended(cells, sides, width):
    for axis, dim in sides:
        count = lax.axis_size(axis)
        ends = count - 1
        head = lax.slice_in_dim(cells, 0, width, axis=dim)
        tail = lax.slice_in_dim(cells, cells.shape[dim] - width, cells.shape[dim], axis=dim)
        cells = jnp.concatenate(
            [
                lax.ppermute(tail, axis, [(i, (i + 1) % count) for i in range(ends)]),
                cells,
                lax.ppermute(head, axis, [((i + 1) % count, i) for i in range(ends)]),
            ],
            axis=dim,
        )
    return cells


def apply_margin(values, diagonal):
    padded = jnp.pad(values, 1)
    beside = padded[2:, 1:-1] + padded[:-2, 1:-1] + padded[1:-1, 2:] + padded[1:-1, :-2]
    return diagonal * values - beside


def chebyshev_margin(start_field, right_side, diagonal):
    depth = SWEEPS
    stacked = extended(
        jnp.stack([start_field, right_side, diagonal]), (("grp", 1), ("frac", 2)), depth
    )
    field_ext = stacked[0]
    right_ext = stacked[1]
    diag_ext = stacked[2]
    inside = diag_ext > 0.0
    inverse = jnp.where(inside, 1.0 / jnp.where(inside, diag_ext, 1.0), 0.0)
    centre = 0.5 * (HIGH_BOUND + LOW_BOUND)
    half_width = 0.5 * (HIGH_BOUND - LOW_BOUND)
    scale_ratio = centre / half_width
    ratio_now = 1.0 / scale_ratio
    residual = inverse * (right_ext - apply_margin(field_ext, diag_ext))
    update = residual / centre
    iterate = field_ext
    for sweep_index in range(SWEEPS):
        iterate = iterate + update
        if sweep_index + 1 < SWEEPS:
            residual = inverse * (right_ext - apply_margin(iterate, diag_ext))
            ratio_next = 1.0 / (2.0 * scale_ratio - ratio_now)
            update = ratio_next * ratio_now * update + 2.0 * ratio_next / half_width * residual
            ratio_now = ratio_next
    return iterate[depth:-depth, depth:-depth]


def owner_lists(local_segment):
    return lax.all_to_all(local_segment, "frac", split_axis=0, concat_axis=0, tiled=True)


def on_device(
    matrix_state,
    matrix_perm,
    frac_state,
    frac_aperture,
    link_cell,
    link_seg,
    link_trans,
    link_count,
    link_upwind,
):
    members = lax.axis_size("frac")
    position = lax.axis_index("frac")
    cell_index = link_cell[0, 0]
    local_segment = link_seg[0, 0]
    transmit = link_trans[0, 0].reshape(-1)
    block_count = link_count[0, 0]
    upwind_all = link_upwind[:, 0, 0]
    capacity = cell_index.shape[1]
    seg_dev = frac_state.shape[2]
    row_count, column_count = matrix_perm.shape
    live_slots = (
        (jnp.arange(capacity, dtype=jnp.int32)[None, :] < block_count[:, None])
        .astype(jnp.int32)
        .reshape(-1)
    )
    cell_flat = cell_index.reshape(-1)
    global_segment = (
        jnp.arange(members, dtype=jnp.int32)[:, None] * seg_dev + local_segment
    ).reshape(-1)
    pressure = matrix_state[0]
    saturation = matrix_state[1]
    frac_pressure = frac_state[0, 0]
    frac_saturation = frac_state[1, 0]
    aperture = frac_aperture[0]
    targets = None
    targets = owner_lists(local_segment)
    for outer in range(ITERS):
        group_states = lax.all_gather(
            jnp.stack([frac_pressure, frac_saturation]), "frac", axis=1, tiled=True
        )
        seg_pressure = group_states[0][global_segment]
        seg_saturation = group_states[1][global_segment]
        group_length = group_states.shape[1]
        first_segment = position * seg_dev
        before = lax.dynamic_slice_in_dim(group_states[0], jnp.maximum(first_segment - 1, 0), 1) * (
            position > 0
        ).astype(jnp.float32)
        after = lax.dynamic_slice_in_dim(
            group_states[0], jnp.minimum(first_segment + seg_dev, group_length - 1), 1
        ) * (position < members - 1).astype(jnp.float32)
        left_values = jnp.concatenate([before, frac_pressure[:-1]])
        right_values = jnp.concatenate([frac_pressure[1:], after])
        cell_pressure = pressure.reshape(-1)[cell_flat]
        cell_saturation = saturation.reshape(-1)[cell_flat]
        upwind_now = upwind_all[outer].reshape(-1)
        upwind_sat = jnp.where(upwind_now == 1, cell_saturation, seg_saturation)
        weight = jnp.where(
            live_slots == 1, transmit * (MOBILITY_FLOOR + upwind_sat * upwind_sat), jnp.float32(0.0)
        )
        water_flux = weight * (cell_pressure - seg_pressure) * upwind_sat
        cell_terms = jnp.stack([weight, weight * seg_pressure, water_flux])
        cell_totals = (
            jnp.zeros((3, row_count * column_count), jnp.float32).at[:, cell_flat].add(cell_terms)
        )
        couple = cell_totals[0].reshape(row_count, column_count)
        source_term = cell_totals[1].reshape(row_count, column_count)
        water_lost = cell_totals[2].reshape(row_count, column_count)
        owner_terms = jnp.stack([weight * cell_pressure, weight, water_flux])
        arrived = lax.all_to_all(
            owner_terms.reshape(3, members, capacity),
            "frac",
            split_axis=1,
            concat_axis=1,
            tiled=True,
        )
        segment_totals = (
            jnp.zeros((3, seg_dev), jnp.float32)
            .at[:, targets.reshape(-1)]
            .add(arrived.reshape(3, -1))
        )
        diagonal = 4.0 + matrix_perm + couple
        right_side = matrix_perm * pressure + source_term
        new_pressure = chebyshev_margin(pressure, right_side, diagonal)
        new_saturation = saturation - TAU_STEP * water_lost / (matrix_perm + couple)
        inflow = segment_totals[0]
        weight_total = segment_totals[1]
        gained = segment_totals[2]
        new_frac_pressure = (aperture * frac_pressure + inflow + left_values + right_values) / (
            aperture + weight_total + 2.0
        )
        new_frac_saturation = frac_saturation + TAU_STEP * gained / (aperture + weight_total)
        pressure = new_pressure
        saturation = new_saturation
        frac_pressure = new_frac_pressure
        frac_saturation = new_frac_saturation
    matrix_out = jnp.stack([pressure, saturation])
    frac_out = jnp.stack([frac_pressure, frac_saturation])[:, None, :]
    return (matrix_out, frac_out)


def solution(mesh):
    return jax.shard_map(
        on_device,
        mesh=mesh,
        in_specs=(
            P(None, "grp", "frac"),
            P("grp", "frac"),
            P(None, "grp", "frac"),
            P("grp", "frac"),
            P("grp", "frac", None, None),
            P("grp", "frac", None, None),
            P("grp", "frac", None, None),
            P("grp", "frac", None),
            P(None, "grp", "frac", None, None),
        ),
        out_specs=(P(None, "grp", "frac"), P(None, "grp", "frac")),
        check_vma=False,
    )
```

profile of v0, /device:TPU:0, one launch (start us, length us, event | category | flops | bytes accessed | tf_op | source)
XLA Modules:
  0.0 508.6 jit_solution(1301443026736918211)
XLA Ops:
  12.1 11.8 %gather_fusion.3 = f32[2048]{0:T(1024)S(1)} fusion(f32[32768]{0:T(1024)S(1)} %bitcast.279, s32[2048]{0:T(1024)S(1)} %broadcast_clamp_fusion.1), kind=kCustom, calls=%fused_computation.3 | custom fusion | bytes 24576 | tf_op jit(solution)/shard_map/gather | solution.py:123
  23.9 11.8 %gather_fusion = f32[2048]{0:T(1024)S(1)} fusion(f32[32768]{0:T(1024)S(1)} %bitcast.280, s32[2048]{0:T(1024)S(1)} %broadcast_clamp_fusion.1), kind=kCustom, calls=%fused_computation | custom fusion | bytes 24576 | tf_op jit(solution)/shard_map/gather | solution.py:124
  46.6 11.8 %gather_fusion.1 = f32[2048]{0:T(1024)S(1)} fusion(f32[65536]{0:T(1024)S(1)} %bitcast.288, s32[2048]{0:T(1024)S(1)} %broadcast_clamp_fusion), kind=kCustom, calls=%fused_computation.1 | custom fusion | bytes 24576 | tf_op jit(solution)/shard_map/gather | solution.py:112
  58.4 11.8 %gather_fusion.2 = f32[2048]{0:T(1024)S(1)} fusion(f32[65536]{0:T(1024)S(1)} %bitcast.285, s32[2048]{0:T(1024)S(1)} %broadcast_clamp_fusion), kind=kCustom, calls=%fused_computation.2 | custom fusion | bytes 24576 | tf_op jit(solution)/shard_map/gather | solution.py:111
  70.8 18.4 %scatter_custom_fusion = f32[3,32768]{0,1:T(8,128)} fusion(s32[2048]{0:T(1024)S(1)} %bitcast.344, f32[2048,3]{1,0:T(8,128)S(1)} %copy.114, f32[]{:T(128)} %constant.22.clone.1), kind=kCustom, calls=%fused_computation.34 | custom fusion | flops 6144 | bytes 393220 | tf_op jit(solution)/shard_map/scatter-add | solution.py:133
  89.3 30.3 %slice_reduce_fusion.5 = (f32[32768]{0:T(1024)S(1)}, f32[32768]{0:T(1024)S(1)}, f32[32768]{0:T(1024)S(1)}) fusion(f32[3,32768]{0,1:T(8,128)} %scatter_custom_fusion), kind=kLoop, calls=%fused_computation.29 | loop fusion | flops 32768 | bytes 786432 | tf_op jit(solution)/shard_map/slice | solution.py:136
  125.5 11.8 %gather_fusion.4 = f32[2048]{0:T(1024)S(1)} fusion(f32[32768]{0:T(1024)S(1)} %bitcast.283, s32[2048]{0:T(1024)S(1)} %broadcast_clamp_fusion.1), kind=kCustom, calls=%fused_computation.4 | custom fusion | bytes 24576 | tf_op jit(solution)/shard_map/gather | solution.py:124
  150.3 11.8 %gather_fusion.7 = f32[2048]{0:T(1024)S(1)} fusion(f32[32768]{0:T(1024)S(1)} %bitcast.284, s32[2048]{0:T(1024)S(1)} %broadcast_clamp_fusion.1), kind=kCustom, calls=%fused_computation.7 | custom fusion | bytes 24576 | tf_op jit(solution)/shard_map/gather | solution.py:123
  162.5 14.0 %scatter_custom_fusion.1 = f32[3,8192]{0,1:T(8,128)} fusion(s32[2048]{0:T(1024)S(1)} %bitcast.356, f32[2048,3]{1,0:T(8,128)S(1)} %copy.116, f32[]{:T(128)} %constant.22.clone.1), kind=kCustom, calls=%fused_computation.40 | custom fusion | flops 6144 | bytes 98308 | tf_op jit(solution)/shard_map/scatter-add | solution.py:149
  176.6 11.5 %fusion.68 = (f32[1,8192]{0,1:T(8,128)}, f32[1,8192]{0,1:T(8,128)}, f32[1,8192]{0,1:T(8,128)}) fusion(f32[3,8192]{0,1:T(8,128)} %scatter_custom_fusion.1), kind=kLoop, calls=%fused_computation.236 | loop fusion | bytes 196608 | tf_op jit(solution)/shard_map/slice | solution.py:155
  208.3 11.8 %gather_fusion.5 = f32[2048]{0:T(1024)S(1)} fusion(f32[65536]{0:T(1024)S(1)} %bitcast.289, s32[2048]{0:T(1024)S(1)} %broadcast_clamp_fusion), kind=kCustom, calls=%fused_computation.5 | custom fusion | bytes 24576 | tf_op jit(solution)/shard_map/gather | solution.py:112
  220.1 11.8 %gather_fusion.6 = f32[2048]{0:T(1024)S(1)} fusion(f32[65536]{0:T(1024)S(1)} %bitcast.287, s32[2048]{0:T(1024)S(1)} %broadcast_clamp_fusion), kind=kCustom, calls=%fused_computation.6 | custom fusion | bytes 24576 | tf_op jit(solution)/shard_map/gather | solution.py:111
  232.5 18.4 %scatter_custom_fusion.2 = f32[3,32768]{0,1:T(8,128)} fusion(s32[2048]{0:T(1024)S(1)} %bitcast.345, f32[2048,3]{1,0:T(8,128)S(1)} %copy.120, f32[]{:T(128)} %constant.22.clone.1), kind=kCustom, calls=%fused_computation.32 | custom fusion | flops 6144 | bytes 393220 | tf_op jit(solution)/shard_map/scatter-add | solution.py:133
  250.8 30.3 %slice_reduce_fusion.3 = (f32[32768]{0:T(1024)S(1)}, f32[32768]{0:T(1024)S(1)}, f32[32768]{0:T(1024)S(1)}) fusion(f32[3,32768]{0,1:T(8,128)} %scatter_custom_fusion.2), kind=kLoop, calls=%fused_computation.25 | loop fusion | flops 32768 | bytes 786432 | tf_op jit(solution)/shard_map/slice | solution.py:136
  303.1 11.8 %gather_fusion.8 = f32[2048]{0:T(1024)S(1)} fusion(f32[32768]{0:T(1024)S(1)} %bitcast.281, s32[2048]{0:T(1024)S(1)} %broadcast_clamp_fusion.1), kind=kCustom, calls=%fused_computation.8 | custom fusion | bytes 24576 | tf_op jit(solution)/shard_map/gather | solution.py:124
  316.7 11.8 %gather_fusion.11 = f32[2048]{0:T(1024)S(1)} fusion(f32[32768]{0:T(1024)S(1)} %bitcast.282, s32[2048]{0:T(1024)S(1)} %broadcast_clamp_fusion.1), kind=kCustom, calls=%fused_computation.11 | custom fusion | bytes 24576 | tf_op jit(solution)/shard_map/gather | solution.py:123
  328.9 13.8 %scatter_custom_fusion.3 = f32[3,8192]{0,1:T(8,128)} fusion(s32[2048]{0:T(1024)S(1)} %bitcast.357, f32[2048,3]{1,0:T(8,128)S(1)} %copy.122, f32[]{:T(128)} %constant.22.clone.1), kind=kCustom, calls=%fused_computation.38 | custom fusion | flops 6144 | bytes 98308 | tf_op jit(solution)/shard_map/scatter-add | solution.py:149
  342.7 11.5 %fusion.67 = (f32[1,8192]{0,1:T(8,128)}, f32[1,8192]{0,1:T(8,128)}, f32[1,8192]{0,1:T(8,128)}) fusion(f32[3,8192]{0,1:T(8,128)} %scatter_custom_fusion.3), kind=kLoop, calls=%fused_computation.235 | loop fusion | bytes 196608 | tf_op jit(solution)/shard_map/slice | solution.py:155
  373.9 11.8 %gather_fusion.9 = f32[2048]{0:T(1024)S(1)} fusion(f32[65536]{0:T(1024)S(1)} %bitcast.290, s32[2048]{0:T(1024)S(1)} %broadcast_clamp_fusion), kind=kCustom, calls=%fused_computation.9 | custom fusion | bytes 24576 | tf_op jit(solution)/shard_map/gather | solution.py:112
  385.7 11.8 %gather_fusion.10 = f32[2048]{0:T(1024)S(1)} fusion(f32[65536]{0:T(1024)S(1)} %bitcast.286, s32[2048]{0:T(1024)S(1)} %broadcast_clamp_fusion), kind=kCustom, calls=%fused_computation.10 | custom fusion | bytes 24576 | tf_op jit(solution)/shard_map/gather | solution.py:111
  398.1 18.4 %scatter_custom_fusion.4 = f32[3,32768]{0,1:T(8,128)} fusion(s32[2048]{0:T(1024)S(1)} %bitcast.346, f32[2048,3]{1,0:T(8,128)S(1)} %copy.126, f32[]{:T(128)} %constant.22.clone.1), kind=kCustom, calls=%fused_computation.30 | custom fusion | flops 6144 | bytes 393220 | tf_op jit(solution)/shard_map/scatter-add | solution.py:133
  416.5 30.3 %slice_reduce_fusion.1 = (f32[32768]{0:T(1024)S(1)}, f32[32768]{0:T(1024)S(1)}, f32[32768]{0:T(1024)S(1)}) fusion(f32[3,32768]{0,1:T(8,128)} %scatter_custom_fusion.4), kind=kLoop, calls=%fused_computation.21 | loop fusion | flops 32768 | bytes 786432 | tf_op jit(solution)/shard_map/slice | solution.py:136
  473.3 13.9 %scatter_custom_fusion.5 = f32[3,8192]{0,1:T(8,128)} fusion(s32[2048]{0:T(1024)S(1)} %bitcast.358, f32[2048,3]{1,0:T(8,128)S(1)} %copy.128, f32[]{:T(128)} %constant.22.clone.1), kind=kCustom, calls=%fused_computation.36 | custom fusion | flops 6144 | bytes 98308 | tf_op jit(solution)/shard_map/scatter-add | solution.py:149
  487.2 11.5 %fusion.66 = (f32[1,8192]{0,1:T(8,128)}, f32[1,8192]{0,1:T(8,128)}, f32[1,8192]{0,1:T(8,128)}) fusion(f32[3,8192]{0,1:T(8,128)} %scatter_custom_fusion.5), kind=kLoop, calls=%fused_computation.234 | loop fusion | bytes 196608 | tf_op jit(solution)/shard_map/slice | solution.py:155
  (184 shorter events, 138.8 us)
Async XLA Ops:
  1.9 140.7 %all-to-all-start = ((s32[8,1,256]{2,1,0:T(1,128)}), s32[8,1,256]{2,1,0:T(1,128)S(1)}, u32[]{:S(2)}, u32[]{:S(2)}) async-start(s32[8,1,256]{2,1,0:T(1,128)} %all_to_all.15), calls=%async_computation | async-start | bytes 16384 | tf_op jit(solution)/shard_map/all_to_all | solution.py:67
  58.4 11.8 %copy-start.4 = (f32[1,1,8,256]{3,2,1,0:T(8,128)S(1)}, f32[1,1,8,256]{3,2,1,0:T(8,128)}, u32[]{:S(2)}) copy-start(f32[1,1,8,256]{3,2,1,0:T(8,128)} %param.15) | copy-start | bytes 24580
  58.4 11.8 %copy-start.5 = (s32[3,1,1,8,256]{4,3,2,1,0:T(8,128)S(1)}, s32[3,1,1,8,256]{4,3,2,1,0:T(8,128)}, u32[]{:S(2)}) copy-start(s32[3,1,1,8,256]{4,3,2,1,0:T(8,128)} %param.17) | copy-start | bytes 73732
  58.4 11.8 %copy-start.6 = (s32[1,1,8]{2,1,0:T(1,128)S(1)}, s32[1,1,8]{2,1,0:T(1,128)}, u32[]{:S(2)}) copy-start(s32[1,1,8]{2,1,0:T(1,128)} %param.16) | copy-start | bytes 100
  89.2 30.5 %copy-start = (f32[128,256]{1,0:T(8,128)S(1)}, f32[128,256]{1,0:T(8,128)}, u32[]{:S(2)}) copy-start(f32[128,256]{1,0:T(8,128)} %param.10) | copy-start | bytes 393220
  89.2 30.5 %copy-start.1 = (f32[2,128,256]{2,1,0:T(8,128)S(1)}, f32[2,128,256]{2,1,0:T(8,128)}, u32[]{:S(2)}) copy-start(f32[2,128,256]{2,1,0:T(8,128)} %param.9) | copy-start | bytes 786436
  89.3 35.3 %copy-start.3 = (f32[2,1,8192]{2,1,0:T(1,128)S(1)}, f32[2,1,8192]{2,1,0:T(1,128)}, u32[]{:S(2)}) copy-start(f32[2,1,8192]{2,1,0:T(1,128)} %param.11) | copy-start | bytes 196612
  119.8 19.4 %collective-permute-start = (f32[3,4,256]{2,1,0:T(4,128)S(1)}, f32[3,4,256]{2,1,0:T(4,128)S(1)}, u32[]{:S(2)}, u32[]{:S(2)}) collective-permute-start(f32[3,4,256]{2,1,0:T(4,128)S(1)} %get-tuple-element.93), channel_id=1, source_target_pairs={{0,8},{8,16},{16,24},{1,9},{9,17},{17,25},{2,10},{10,18},{18,26},{... | collective-permute-start | bytes 36872 | tf_op jit(solution)/shard_map/ppermute | solution.py:24
  123.3 15.9 %collective-permute-start.1 = (f32[3,4,256]{2,1,0:T(4,128)S(1)}, f32[3,4,256]{2,1,0:T(4,128)S(1)}, u32[]{:S(2)}, u32[]{:S(2)}) collective-permute-start(f32[3,4,256]{2,1,0:T(4,128)S(1)} %get-tuple-element.94), channel_id=1, source_target_pairs={{8,0},{16,8},{24,16},{9,1},{17,9},{25,17},{10,2},{18,10},{26,18},{... | collective-permute-start | bytes 36872 | tf_op jit(solution)/shard_map/ppermute | solution.py:26
  139.4 9.3 %collective-permute-start.2 = (f32[3,136,4]{2,1,0:T(8,128)S(1)}, f32[3,136,4]{2,1,0:T(8,128)S(1)}, u32[]{:S(2)}, u32[]{:S(2)}) collective-permute-start(f32[3,136,4]{2,1,0:T(8,128)S(1)} %get-tuple-element.85), channel_id=1, source_target_pairs={{0,1},{1,2},{2,3},{3,4},{4,5},{5,6},{6,7},{8,9},{9,10},{10,11},{11... | collective-permute-start | bytes 19592 | tf_op jit(solution)/shard_map/ppermute | solution.py:24
  141.4 7.3 %collective-permute-start.3 = (f32[3,136,4]{2,1,0:T(8,128)S(1)}, f32[3,136,4]{2,1,0:T(8,128)S(1)}, u32[]{:S(2)}, u32[]{:S(2)}) collective-permute-start(f32[3,136,4]{2,1,0:T(8,128)S(1)} %get-tuple-element.86), channel_id=1, source_target_pairs={{1,0},{2,1},{3,2},{4,3},{5,4},{6,5},{7,6},{9,8},{10,9},{11,10},{12... | collective-permute-start | bytes 19592 | tf_op jit(solution)/shard_map/ppermute | solution.py:26
  142.7 19.5 %all-to-all-start.1 = ((f32[3,8,256]{2,0,1:T(4,128)}), f32[3,8,256]{2,0,1:T(4,128)S(1)}, u32[]{:S(2)}, u32[]{:S(2)}) async-start(f32[3,8,256]{2,0,1:T(4,128)} %copy.115), calls=%async_computation.1 | async-start | bytes 65536 | tf_op jit(solution)/shard_map/all_to_all | solution.py:139
  190.9 5.7 %copy-start.2 = (f32[1,8192]{1,0:T(1,128)S(1)}, f32[1,8192]{1,0:T(1,128)}, u32[]{:S(2)}) copy-start(f32[1,8192]{1,0:T(1,128)} %param.12) | copy-start | bytes 98308
  281.4 5.9 %collective-permute-start.4 = (f32[3,4,256]{2,1,0:T(4,128)S(1)}, f32[3,4,256]{2,1,0:T(4,128)S(1)}, u32[]{:S(2)}, u32[]{:S(2)}) collective-permute-start(f32[3,4,256]{2,1,0:T(4,128)S(1)} %get-tuple-element.89), channel_id=1, source_target_pairs={{0,8},{8,16},{16,24},{1,9},{9,17},{17,25},{2,10},{10,18},{18,26},{... | collective-permute-start | bytes 36872 | tf_op jit(solution)/shard_map/ppermute | solution.py:24
  285.9 5.6 %collective-permute-start.5 = (f32[3,4,256]{2,1,0:T(4,128)S(1)}, f32[3,4,256]{2,1,0:T(4,128)S(1)}, u32[]{:S(2)}, u32[]{:S(2)}) collective-permute-start(f32[3,4,256]{2,1,0:T(4,128)S(1)} %get-tuple-element.90), channel_id=1, source_target_pairs={{8,0},{16,8},{24,16},{9,1},{17,9},{25,17},{10,2},{18,10},{26,18},{... | collective-permute-start | bytes 36872 | tf_op jit(solution)/shard_map/ppermute | solution.py:26
  291.7 23.3 %collective-permute-start.6 = (f32[3,136,4]{2,1,0:T(8,128)S(1)}, f32[3,136,4]{2,1,0:T(8,128)S(1)}, u32[]{:S(2)}, u32[]{:S(2)}) collective-permute-start(f32[3,136,4]{2,1,0:T(8,128)S(1)} %get-tuple-element.83), channel_id=1, source_target_pairs={{0,1},{1,2},{2,3},{3,4},{4,5},{5,6},{6,7},{8,9},{9,10},{10,11},{11... | collective-permute-start | bytes 19592 | tf_op jit(solution)/shard_map/ppermute | solution.py:24
  293.0 22.0 %collective-permute-start.7 = (f32[3,136,4]{2,1,0:T(8,128)S(1)}, f32[3,136,4]{2,1,0:T(8,128)S(1)}, u32[]{:S(2)}, u32[]{:S(2)}) collective-permute-start(f32[3,136,4]{2,1,0:T(8,128)S(1)} %get-tuple-element.84), channel_id=1, source_target_pairs={{1,0},{2,1},{3,2},{4,3},{5,4},{6,5},{7,6},{9,8},{10,9},{11,10},{12... | collective-permute-start | bytes 19592 | tf_op jit(solution)/shard_map/ppermute | solution.py:26
  296.8 31.7 %all-to-all-start.2 = ((f32[3,8,256]{2,0,1:T(4,128)}), f32[3,8,256]{2,0,1:T(4,128)S(1)}, u32[]{:S(2)}, u32[]{:S(2)}) async-start(f32[3,8,256]{2,0,1:T(4,128)} %copy.121), calls=%async_computation.2 | async-start | bytes 65536 | tf_op jit(solution)/shard_map/all_to_all | solution.py:139
  447.1 4.9 collective-permute-start.8
  450.6 5.6 %collective-permute-start.9 = (f32[3,4,256]{2,1,0:T(4,128)S(1)}, f32[3,4,256]{2,1,0:T(4,128)S(1)}, u32[]{:S(2)}, u32[]{:S(2)}) collective-permute-start(f32[3,4,256]{2,1,0:T(4,128)S(1)} %get-tuple-element.88), channel_id=1, source_target_pairs={{8,0},{16,8},{24,16},{9,1},{17,9},{25,17},{10,2},{18,10},{26,18},{... | collective-permute-start | bytes 36872 | tf_op jit(solution)/shard_map/ppermute | solution.py:26
  456.3 11.8 %collective-permute-start.10 = (f32[3,136,4]{2,1,0:T(8,128)S(1)}, f32[3,136,4]{2,1,0:T(8,128)S(1)}, u32[]{:S(2)}, u32[]{:S(2)}) collective-permute-start(f32[3,136,4]{2,1,0:T(8,128)S(1)} %get-tuple-element.81), channel_id=1, source_target_pairs={{0,1},{1,2},{2,3},{3,4},{4,5},{5,6},{6,7},{8,9},{9,10},{10,11},{11... | collective-permute-start | bytes 19592 | tf_op jit(solution)/shard_map/ppermute | solution.py:24
  457.6 10.4 %collective-permute-start.11 = (f32[3,136,4]{2,1,0:T(8,128)S(1)}, f32[3,136,4]{2,1,0:T(8,128)S(1)}, u32[]{:S(2)}, u32[]{:S(2)}) collective-permute-start(f32[3,136,4]{2,1,0:T(8,128)S(1)} %get-tuple-element.82), channel_id=1, source_target_pairs={{1,0},{2,1},{3,2},{4,3},{5,4},{6,5},{7,6},{9,8},{10,9},{11,10},{12... | collective-permute-start | bytes 19592 | tf_op jit(solution)/shard_map/ppermute | solution.py:26
  461.4 11.4 %all-to-all-start.3 = ((f32[3,8,256]{2,0,1:T(4,128)}), f32[3,8,256]{2,0,1:T(4,128)S(1)}, u32[]{:S(2)}, u32[]{:S(2)}) async-start(f32[3,8,256]{2,0,1:T(4,128)} %copy.127), calls=%async_computation.3 | async-start | bytes 65536 | tf_op jit(solution)/shard_map/all_to_all | solution.py:139
where the time goes:
time: 515 us; the launch traced here: 509 us
  local copies, waits for them, and re-layouts  216 us (42%)
  other arithmetic  196 us (38%)
  starting transfers between devices  47.9 us (9%)
  blocking collectives  31.6 us (6%)
  waiting for transfers between devices  11 us (2%)
  between operations  6.17 us (1%)
    slice x3, other arithmetic, on_device(): source_term = cell_totals[1].reshape(row_count, column_count)  90.8 us
    scatter-add x3, other arithmetic, on_device(): jnp.zeros((3, row_count * column_count), jnp.float32).at[:, cell_flat]  55.2 us
    scatter-add x3, other arithmetic, on_device(): segment_totals = jnp.zeros((3, seg_dev), jnp.float32).at[:, targets.resha...  41.8 us
    gather x6, local copies, waits for them, and re-layouts, on_device(): seg_saturation = group_states[1][global_segment]  35.4 us
    gather x6, local copies, waits for them, and re-layouts, on_device(): seg_pressure = group_states[0][global_segment]  35.4 us
    gather x6, local copies, waits for them, and re-layouts, on_device(): cell_pressure = pressure.reshape(-1)[cell_flat]  35.4 us
    gather x6, local copies, waits for them, and re-layouts, on_device(): cell_saturation = saturation.reshape(-1)[cell_flat]  35.4 us
    slice x3, local copies, waits for them, and re-layouts, on_device(): inflow = segment_totals[0]  34.4 us
  transfers between devices with their start and end apart: 16, of which 5 were waited for; matrix products, arithmetic and copies ran while one was open for 31% of the time, Pallas kernels for 0%

commit v1 on v0

v1 whole, which is shorter than its diff:
```python
import functools

import jax
import jax.numpy as jnp
from jax import lax
from jax.experimental import pallas as pl
from jax.experimental.pallas import tpu as pltpu
from jax.sharding import PartitionSpec as P

ITERS = 3
SWEEPS = 4

LOW_BOUND = 0.02
HIGH_BOUND = 1.98
TAU_STEP = 0.5
MOBILITY_FLOOR = 0.2

F32 = jnp.float32
BF16 = jnp.bfloat16
LANES = 128
SUB = 8
DEPTH = SWEEPS - 1


def iota(shape, dim):
    return lax.broadcasted_iota(jnp.int32, shape, dim)


def parts_of(x):
    high = x.astype(BF16).astype(F32)
    rest = x - high
    mid = rest.astype(BF16).astype(F32)
    low = rest - mid
    return high, mid, low


def table_of(fields):
    split = [parts_of(f) for f in fields]
    return jnp.concatenate([s[p] for p in range(3) for s in split], axis=0).astype(BF16)


def one_hot(index_row, count):
    hit = iota((count, index_row.shape[1]), 0) == index_row
    return jnp.where(hit, 1.0, 0.0).astype(BF16)


def pick(table, fields, rows, row_index, hot):
    wide = jnp.dot(table, hot, preferred_element_type=F32)
    hit = iota((rows, row_index.shape[1]), 0) == row_index
    found = []
    for f in range(fields):
        total = sum(wide[(p * fields + f) * rows : (p * fields + f + 1) * rows] for p in range(3))
        found.append(jnp.sum(jnp.where(hit, total, 0.0), axis=0, keepdims=True))
    return found


def spread(left_ref, block, width, rows, row_index, values):
    hit = iota((rows, row_index.shape[1]), 0) == row_index
    at = slice(block * width, (block + 1) * width)
    for f, value in enumerate(values):
        for p, part in enumerate(parts_of(value)):
            row = (p * len(values) + f) * rows
            left_ref[row : row + rows, at] = jnp.where(hit, part, 0.0).astype(BF16)


def gathered_sum(left_ref, hot_ref, fields, rows):
    wide = lax.dot_general(
        left_ref[...], hot_ref[...], (((1,), (1,)), ((), ())), preferred_element_type=F32
    )
    return [
        sum(wide[(p * fields + f) * rows : (p * fields + f + 1) * rows] for p in range(3))
        for f in range(fields)
    ]


def flow(trans, upwind, cell_p, cell_s, seg_p, seg_s):
    u = jnp.where(upwind > 0.5, cell_s, seg_s)
    weight = trans * (MOBILITY_FLOOR + u * u)
    water = weight * (cell_p - seg_p) * u
    return weight, water


def cell_parts(cell_row, columns):
    return cell_row // columns, cell_row % columns


def ends_of(frac):
    rows = frac.shape[0]
    return jnp.concatenate([frac[0:1], frac[rows - 1 : rows]], axis=1)


def frac_step(frac, sat, aperture, before, after, inflow, total, gained):
    rows, lanes = frac.shape
    row, lane = iota((rows, lanes), 0), iota((rows, lanes), 1)
    back = pltpu.roll(frac, 1, 1)
    left = jnp.where(lane == 0, pltpu.roll(back, 1, 0), back)
    left = jnp.where((lane == 0) & (row == 0), before, left)
    ahead = pltpu.roll(frac, lanes - 1, 1)
    right = jnp.where(lane == lanes - 1, pltpu.roll(ahead, rows - 1, 0), ahead)
    right = jnp.where((lane == lanes - 1) & (row == rows - 1), after, right)
    new_frac = (aperture * frac + inflow + left + right) / (aperture + total + 2.0)
    new_sat = sat + TAU_STEP * gained / (aperture + total)
    return new_frac, new_sat


def chain_ends(ends_ref, row, members):
    me = lax.axis_index("frac")
    lanes = ends_ref.shape[2]
    prior = ends_ref[jnp.maximum(me - 1, 0), row : row + 1, :]
    later = ends_ref[jnp.minimum(me + 1, members - 1), row : row + 1, :]
    before = jnp.where(me > 0, prior[:, lanes - 1 :], 0.0)
    after = jnp.where(me < members - 1, later[:, 0:1], 0.0)
    return before, after


def partial_residual(pressure, couple, source, inverse):
    rows, columns = pressure.shape
    row, col = iota((rows, columns), 0), iota((rows, columns), 1)
    beside = jnp.where(row == 0, 0.0, pltpu.roll(pressure, 1, 0))
    beside += jnp.where(row == rows - 1, 0.0, pltpu.roll(pressure, rows - 1, 0))
    beside += jnp.where(col == 0, 0.0, pltpu.roll(pressure, 1, 1))
    beside += jnp.where(col == columns - 1, 0.0, pltpu.roll(pressure, columns - 1, 1))
    return inverse * (source - (4.0 + couple) * pressure + beside)


def pack_low(q, inv, p, at, axis):
    return jnp.where(
        at < DEPTH, q, jnp.where(at < 2 * DEPTH, pltpu.roll(inv, DEPTH, axis), pltpu.roll(p, 2 * DEPTH, axis))
    )


def pack_high(q, inv, p, at, axis):
    size = q.shape[axis]
    return jnp.where(
        at >= size - DEPTH,
        q,
        jnp.where(
            at >= size - 2 * DEPTH,
            pltpu.roll(inv, size - DEPTH, axis),
            pltpu.roll(p, size - 2 * DEPTH, axis),
        ),
    )


def send_halo(out_ref, q, inv, p, groups, members):
    rows, columns = q.shape
    g, f = lax.axis_index("grp"), lax.axis_index("frac")
    here = g * members + f
    sub = iota((SUB, columns), 0)
    top = pack_low(q[:SUB], inv[:SUB], p[:SUB], sub, 0)
    bottom = pack_high(q[rows - SUB :], inv[rows - SUB :], p[rows - SUB :], sub, 0)
    lane = iota((rows, LANES), 1)
    low = pack_low(q[:, :LANES], inv[:, :LANES], p[:, :LANES], lane, 1)
    high = pack_high(q[:, columns - LANES :], inv[:, columns - LANES :], p[:, columns - LANES :], lane, 1)
    turned = jnp.transpose(jnp.where(lane < LANES // 2, low, high))
    left, right = turned[:SUB], turned[LANES - SUB :]
    p_top, p_bottom = p[:SUB], p[rows - SUB :]

    for step, strip, p_strip in ((-1, top, p_top), (1, bottom, p_bottom)):
        inside = (g + step >= 0) & (g + step < groups)
        base = here + step * members

        @pl.when(inside)
        def _():
            out_ref[base] = strip

        @pl.when(inside & (f > 0))
        def _():
            out_ref[base - 1, :, 0:LANES] = strip[:, :LANES]
            out_ref[base - 1, :, LANES : 2 * LANES] = p_strip[:, :LANES]

        @pl.when(inside & (f < members - 1))
        def _():
            out_ref[base + 1, :, 0:LANES] = strip[:, columns - LANES :]
            out_ref[base + 1, :, LANES : 2 * LANES] = p_strip[:, columns - LANES :]

    @pl.when(f > 0)
    def _():
        out_ref[here - 1, :, 0:LANES] = left

    @pl.when(f < members - 1)
    def _():
        out_ref[here + 1, :, 0:LANES] = right


def chebyshev(in_ref, q, inv, p, q_ext, inv_ext, p_ext, groups, members):
    rows, columns = q.shape
    g, f = lax.axis_index("grp"), lax.axis_index("frac")
    here = g * members + f
    last = groups * members - 1

    def block(dg, df):
        ok = (g + dg >= 0) & (g + dg < groups) & (f + df >= 0) & (f + df < members)
        at = jnp.clip(here + dg * members + df, 0, last)
        return jnp.where(ok, in_ref[at], 0.0)

    sub = iota((SUB, columns), 0)
    below, above = block(1, 0), block(-1, 0)

    def both(low, high, at, count, size):
        return jnp.where(at < count, low, jnp.where(at >= size - count, high, 0.0))

    q_ext[0:rows, 0:columns] = q
    inv_ext[0:rows, 0:columns] = inv
    p_ext[0:rows, 0:columns] = p
    q_ext[rows : rows + SUB, 0:columns] = both(below, above, sub, DEPTH, SUB)
    inv_ext[rows : rows + SUB, 0:columns] = both(
        pltpu.roll(below, SUB - DEPTH, 0), pltpu.roll(above, DEPTH, 0), sub, DEPTH, SUB
    )
    p_ext[rows : rows + SUB, 0:columns] = both(
        pltpu.roll(below, SUB - 2 * DEPTH, 0), pltpu.roll(above, 2 * DEPTH, 0), sub, 2, SUB
    )
    right, left = block(0, 1)[:, :LANES], block(0, -1)[:, :LANES]
    turned = jnp.transpose(
        jnp.concatenate([right, jnp.zeros((LANES - 2 * SUB, rows), F32), left], axis=0)
    )
    lane = iota((rows, LANES), 1)
    side = slice(columns, columns + LANES)
    q_ext[0:rows, side] = both(turned, turned, lane, DEPTH, LANES)
    inv_ext[0:rows, side] = both(
        pltpu.roll(turned, LANES - DEPTH, 1), pltpu.roll(turned, DEPTH, 1), lane, DEPTH, LANES
    )
    p_ext[0:rows, side] = both(
        pltpu.roll(turned, LANES - 2 * DEPTH, 1), pltpu.roll(turned, 2 * DEPTH, 1), lane, 2, LANES
    )
    sub = iota((SUB, LANES), 0)
    lane = iota((SUB, LANES), 1)
    low_right, low_left = block(1, 1), block(1, -1)
    high_right, high_left = block(-1, 1), block(-1, -1)
    low = both(low_right, low_left, iota((SUB, 2 * LANES), 1) % LANES, DEPTH, LANES)
    high = both(high_right, high_left, iota((SUB, 2 * LANES), 1) % LANES, DEPTH, LANES)
    corner = slice(rows, rows + SUB)
    q_ext[corner, side] = both(low[:, :LANES], high[:, :LANES], sub, DEPTH, SUB)
    inv_ext[corner, side] = both(
        pltpu.roll(low[:, :LANES], SUB - DEPTH, 0), pltpu.roll(high[:, :LANES], DEPTH, 0), sub, DEPTH, SUB
    )
    p_ext[corner, side] = both(low[:, LANES:], high[:, LANES:], sub, DEPTH, SUB)

    shape = (rows + SUB, columns + LANES)
    row, col = iota(shape, 0), iota(shape, 1)
    field = p_ext[...]
    missing = jnp.where((row == 0) | (row == rows), pltpu.roll(field, 1, 0), 0.0)
    missing += jnp.where((row == rows - 1) | (row == rows + SUB - 1), pltpu.roll(field, shape[0] - 1, 0), 0.0)
    missing += jnp.where((col == 0) | (col == columns), pltpu.roll(field, 1, 1), 0.0)
    missing += jnp.where(
        (col == columns - 1) | (col == columns + LANES - 1), pltpu.roll(field, shape[1] - 1, 1), 0.0
    )
    inverse = inv_ext[...]
    start = q_ext[...] + inverse * missing

    centre = 0.5 * (HIGH_BOUND + LOW_BOUND)
    half_width = 0.5 * (HIGH_BOUND - LOW_BOUND)
    scale_ratio = centre / half_width
    ratio_now = 1.0 / scale_ratio
    update = start / centre if centre != 1.0 else start
    change = update
    for _ in range(SWEEPS - 1):
        beside = (
            pltpu.roll(change, 1, 0)
            + pltpu.roll(change, shape[0] - 1, 0)
            + pltpu.roll(change, 1, 1)
            + pltpu.roll(change, shape[1] - 1, 1)
        )
        residual = start - change + inverse * beside
        ratio_next = 1.0 / (2.0 * scale_ratio - ratio_now)
        update = ratio_next * ratio_now * update + (2.0 * ratio_next / half_width) * residual
        ratio_now = ratio_next
        change = change + update
    return p + change[0:rows, 0:columns]


ROW_SEG = 0
ROW_TRANS = 1
ROW_UP = 2
ROW_P = ROW_UP + ITERS
ROW_S = ROW_P + 1
ROW_ENDS = ROW_S + 1


def first_kernel(members, cell_ref, seg_ref, trans_ref, count_ref, up_ref, state_ref, frac_ref, out_ref):
    _, rows, columns = state_ref.shape
    width = cell_ref.shape[1]
    table = table_of([state_ref[0], state_ref[1]])
    ends = ends_of(frac_ref[0])
    for o in range(members):
        one = slice(o, o + 1)
        row, col = cell_parts(cell_ref[one, :], columns)
        cell_p, cell_s = pick(table, 2, rows, row, one_hot(col, columns))
        live = iota((1, width), 1) < count_ref[0, o]
        out_ref[o, ROW_SEG : ROW_SEG + 1, :] = seg_ref[one, :].astype(F32)
        out_ref[o, ROW_TRANS : ROW_TRANS + 1, :] = jnp.where(live, trans_ref[one, :], 0.0)
        for t in range(ITERS):
            out_ref[o, ROW_UP + t : ROW_UP + t + 1, :] = up_ref[t, one, :].astype(F32)
        out_ref[o, ROW_P : ROW_P + 1, :] = cell_p
        out_ref[o, ROW_S : ROW_S + 1, :] = cell_s
        out_ref[o, ROW_ENDS : ROW_ENDS + 1, :] = ends


def seg_parts(slot_ref, s):
    seg = slot_ref[s, ROW_SEG : ROW_SEG + 1, :].astype(jnp.int32)
    return seg // LANES, seg % LANES


def seg_hots(slot_ref, hot_ref, members, width):
    for s in range(members):
        hot_ref[:, s * width : (s + 1) * width] = one_hot(seg_parts(slot_ref, s)[1], LANES)


def seg_gather(slot_ref, hot_ref, fields, s, width, table):
    return pick(table, 2, fields, seg_parts(slot_ref, s)[0], hot_ref[:, s * width : (s + 1) * width])


def owner_start_kernel(members, slot_ref, frac_ref, aperture_ref, out_ref, new_ref, hot_ref, left_ref):
    width = slot_ref.shape[2]
    rows = frac_ref.shape[1]
    frac, sat = frac_ref[0], frac_ref[1]
    seg_hots(slot_ref, hot_ref, members, width)
    table = table_of([frac, sat])
    for s in range(members):
        seg_p, seg_s = seg_gather(slot_ref, hot_ref, rows, s, width, table)
        out_ref[s, 0:1, :] = seg_p
        out_ref[s, 1:2, :] = seg_s
        slot = slot_ref[s]
        cell_p = slot[ROW_P : ROW_P + 1]
        weight, water = flow(
            slot[ROW_TRANS : ROW_TRANS + 1],
            slot[ROW_UP : ROW_UP + 1],
            cell_p,
            slot[ROW_S : ROW_S + 1],
            seg_p,
            seg_s,
        )
        spread(left_ref, s, width, rows, seg_parts(slot_ref, s)[0], [weight * cell_p, weight, water])
    inflow, total, gained = gathered_sum(left_ref, hot_ref, 3, rows)
    before, after = chain_ends(slot_ref, ROW_ENDS, members)
    new_frac, new_sat = frac_step(frac, sat, aperture_ref[...], before, after, inflow, total, gained)
    new_ref[0] = new_frac
    new_ref[1] = new_sat
    table = table_of([new_frac, new_sat])
    ends = ends_of(new_frac)
    for s in range(members):
        seg_p, seg_s = seg_gather(slot_ref, hot_ref, rows, s, width, table)
        out_ref[s, 2:3, :] = seg_p
        out_ref[s, 3:4, :] = seg_s
        out_ref[s, 4:5, :] = ends


def cell_update(
    members, t, cell_ref, sent_ref, cell_rows, seg_rows, pressure, saturation, perm, hot_ref, left_ref
):
    rows, columns = pressure.shape
    width = cell_ref.shape[1]
    for o in range(members):
        row, col = cell_parts(cell_ref[o : o + 1, :], columns)
        hot_ref[:, o * width : (o + 1) * width] = one_hot(col, columns)
        seg_p, seg_s = seg_rows(o)
        cell_p, cell_s = cell_rows(o)
        weight, water = flow(
            sent_ref[o, ROW_TRANS : ROW_TRANS + 1, :],
            sent_ref[o, ROW_UP + t : ROW_UP + t + 1, :],
            cell_p,
            cell_s,
            seg_p,
            seg_s,
        )
        spread(left_ref, o, width, rows, row, [weight, weight * seg_p, water])
    couple, source, lost = gathered_sum(left_ref, hot_ref, 3, rows)
    inverse = 1.0 / (4.0 + perm + couple)
    new_saturation = saturation - TAU_STEP * lost / (perm + couple)
    return new_saturation, partial_residual(pressure, couple, source, inverse), inverse


def source_start_kernel(
    groups, members, cell_ref, sent_ref, seg_ref, state_ref, perm_ref, out_ref, keep_ref, hot_ref, left_ref
):
    pressure = state_ref[0]
    new_saturation, q, inv = cell_update(
        members,
        0,
        cell_ref,
        sent_ref,
        lambda o: (sent_ref[o, ROW_P : ROW_P + 1, :], sent_ref[o, ROW_S : ROW_S + 1, :]),
        lambda o: (seg_ref[o, 0:1, :], seg_ref[o, 1:2, :]),
        pressure,
        state_ref[1],
        perm_ref[...],
        hot_ref,
        left_ref,
    )
    keep_ref[0] = pressure
    keep_ref[1] = new_saturation
    keep_ref[2] = q
    keep_ref[3] = inv
    send_halo(out_ref, q, inv, pressure, groups, members)


def cell_gather(members, cell_ref, fields, put):
    rows, columns = fields[0].shape
    table = table_of(fields)
    for o in range(members):
        row, col = cell_parts(cell_ref[o : o + 1, :], columns)
        put(o, *pick(table, len(fields), rows, row, one_hot(col, columns)))


def middle_kernel(
    groups, members, halo_ref, cell_ref, sent_ref, seg_ref, kept_ref, perm_ref, out_ref, keep_ref,
    slots_ref, hot_ref, left_ref, q_ext, inv_ext, p_ext,
):
    pressure = chebyshev(
        halo_ref, kept_ref[2], kept_ref[3], kept_ref[0], q_ext, inv_ext, p_ext, groups, members
    )
    saturation = kept_ref[1]
    g = lax.axis_index("grp")

    def put(o, cell_p, cell_s):
        slots_ref[o, 0:1, :] = cell_p
        slots_ref[o, 1:2, :] = cell_s
        for half in range(2):
            at = slice(half * LANES, (half + 1) * LANES)
            out_ref[g * members + o, half : half + 1, LANES : 2 * LANES] = cell_p[:, at]
            out_ref[g * members + o, 2 + half : 3 + half, LANES : 2 * LANES] = cell_s[:, at]

    cell_gather(members, cell_ref, [pressure, saturation], put)
    new_saturation, q, inv = cell_update(
        members,
        1,
        cell_ref,
        sent_ref,
        lambda o: (slots_ref[o, 0:1, :], slots_ref[o, 1:2, :]),
        lambda o: (seg_ref[o, 2:3, :], seg_ref[o, 3:4, :]),
        pressure,
        saturation,
        perm_ref[...],
        hot_ref,
        left_ref,
    )
    keep_ref[0] = pressure
    keep_ref[1] = new_saturation
    keep_ref[2] = q
    keep_ref[3] = inv
    send_halo(out_ref, q, inv, pressure, groups, members)


def owner_update(members, t, slot_ref, cell_rows, seg_rows, frac, sat, aperture, ends, hot_ref, left_ref):
    width = slot_ref.shape[2]
    rows = frac.shape[0]
    seg_hots(slot_ref, hot_ref, members, width)
    for s in range(members):
        cell_p, cell_s = cell_rows(s)
        weight, water = flow(
            slot_ref[s, ROW_TRANS : ROW_TRANS + 1, :],
            slot_ref[s, ROW_UP + t : ROW_UP + t + 1, :],
            cell_p,
            cell_s,
            *seg_rows(s),
        )
        spread(left_ref, s, width, rows, seg_parts(slot_ref, s)[0], [weight * cell_p, weight, water])
    inflow, total, gained = gathered_sum(left_ref, hot_ref, 3, rows)
    return frac_step(frac, sat, aperture, *ends, inflow, total, gained)


def exchange_kernel(
    groups, members, halo_ref, cell_ref, slot_ref, ends_ref, own_ref, frac_ref, aperture_ref, kept_ref,
    out_ref, new_ref, pressure_ref, hot_ref, left_ref, q_ext, inv_ext, p_ext,
):
    width = slot_ref.shape[2]
    rows = frac_ref.shape[1]
    g = lax.axis_index("grp")

    def cell_rows(s):
        block = halo_ref[g * members + s]
        half = block[:, LANES : 2 * LANES]
        return (
            jnp.concatenate([half[0:1], half[1:2]], axis=1),
            jnp.concatenate([half[2:3], half[3:4]], axis=1),
        )

    new_frac, new_sat = owner_update(
        members,
        1,
        slot_ref,
        cell_rows,
        lambda s: (own_ref[s, 2:3, :], own_ref[s, 3:4, :]),
        frac_ref[0],
        frac_ref[1],
        aperture_ref[...],
        chain_ends(ends_ref, 4, members),
        hot_ref,
        left_ref,
    )
    new_ref[0] = new_frac
    new_ref[1] = new_sat
    table = table_of([new_frac, new_sat])
    ends = ends_of(new_frac)
    for s in range(members):
        seg_p, seg_s = seg_gather(slot_ref, hot_ref, rows, s, width, table)
        out_ref[s, 2:3, :] = seg_p
        out_ref[s, 3:4, :] = seg_s
        out_ref[s, 4:5, :] = ends

    pressure = chebyshev(
        halo_ref, kept_ref[2], kept_ref[3], kept_ref[0], q_ext, inv_ext, p_ext, groups, members
    )
    pressure_ref[...] = pressure

    def put(o, cell_p, cell_s):
        out_ref[o, 0:1, :] = cell_p
        out_ref[o, 1:2, :] = cell_s

    cell_gather(members, cell_ref, [pressure, kept_ref[1]], put)


def source_last_kernel(
    groups, members, cell_ref, sent_ref, own_ref, seg_ref, pressure_ref, kept_ref, perm_ref, out_ref, keep_ref,
    hot_ref, left_ref,
):
    pressure = pressure_ref[...]
    new_saturation, q, inv = cell_update(
        members,
        2,
        cell_ref,
        sent_ref,
        lambda o: (own_ref[o, 0:1, :], own_ref[o, 1:2, :]),
        lambda o: (seg_ref[o, 2:3, :], seg_ref[o, 3:4, :]),
        pressure,
        kept_ref[1],
        perm_ref[...],
        hot_ref,
        left_ref,
    )
    keep_ref[0] = new_saturation
    keep_ref[1] = q
    keep_ref[2] = inv
    send_halo(out_ref, q, inv, pressure, groups, members)


def owner_last_kernel(members, slot_ref, own_ref, seg_ref, frac_ref, aperture_ref, out_ref, hot_ref, left_ref):
    new_frac, new_sat = owner_update(
        members,
        2,
        slot_ref,
        lambda s: (seg_ref[s, 0:1, :], seg_ref[s, 1:2, :]),
        lambda s: (own_ref[s, 2:3, :], own_ref[s, 3:4, :]),
        frac_ref[0],
        frac_ref[1],
        aperture_ref[...],
        chain_ends(seg_ref, 4, members),
        hot_ref,
        left_ref,
    )
    out_ref[0] = new_frac
    out_ref[1] = new_sat


def final_kernel(groups, members, halo_ref, pressure_ref, kept_ref, out_ref, q_ext, inv_ext, p_ext):
    out_ref[0] = chebyshev(
        halo_ref, kept_ref[1], kept_ref[2], pressure_ref[...], q_ext, inv_ext, p_ext, groups, members
    )
    out_ref[1] = kept_ref[0]


VMEM = pl.BlockSpec(memory_space=pltpu.VMEM)
SMEM = pl.BlockSpec(memory_space=pltpu.SMEM)


def call(kernel, statics, outs, scratch, *args, smem=()):
    outs = [jax.ShapeDtypeStruct(s, F32) for s in outs]
    return pl.pallas_call(
        functools.partial(kernel, *statics),
        out_shape=outs,
        in_specs=[SMEM if i in smem else VMEM for i in range(len(args))],
        out_specs=[VMEM] * len(outs),
        scratch_shapes=[pltpu.VMEM(s, t) for s, t in scratch],
        compiler_params=pltpu.CompilerParams(vmem_limit_bytes=32 * 1024 * 1024),
        name=kernel.__name__,
    )(*args)


def on_device(
    matrix_state,
    matrix_perm,
    frac_state,
    frac_aperture,
    link_cell,
    link_seg,
    link_trans,
    link_count,
    link_upwind,
):
    groups, members = lax.axis_size("grp"), lax.axis_size("frac")
    both = (groups, members)
    devices = groups * members
    cells = link_cell[0, 0]
    width = cells.shape[1]
    _, rows, columns = matrix_state.shape
    seg_dev = frac_state.shape[2]
    seg_rows = seg_dev // LANES
    frac = frac_state.reshape(2, seg_rows, LANES)
    aperture = frac_aperture.reshape(seg_rows, LANES)

    slots = (members, SUB, width)
    halo = (devices, SUB, columns)
    hot_cell = ((columns, members * width), BF16)
    left_cell = ((9 * rows, members * width), BF16)
    hot_seg = ((LANES, members * width), BF16)
    left_seg = ((9 * seg_rows, members * width), BF16)
    ext = [((rows + SUB, columns + LANES), F32)] * 3

    def to_group(x):
        return lax.all_to_all(x, "frac", split_axis=0, concat_axis=0, tiled=True)

    def to_all(x):
        return lax.all_to_all(x, ("grp", "frac"), split_axis=0, concat_axis=0, tiled=True)

    (sent,) = call(
        first_kernel, (members,), [slots], [],
        cells, link_seg[0, 0], link_trans[0, 0], link_count[0], link_upwind[:, 0, 0], matrix_state, frac,
        smem=(3,),
    )
    slot = to_group(sent)
    own, frac1 = call(
        owner_start_kernel, (members,), [slots, frac.shape], [hot_seg, left_seg], slot, frac, aperture
    )
    segs = to_group(own)
    edge, kept = call(
        source_start_kernel, both, [halo, (4, rows, columns)], [hot_cell, left_cell],
        cells, sent, segs, matrix_state, matrix_perm,
    )
    around = to_all(edge)
    edge, kept = call(
        middle_kernel, both, [halo, (4, rows, columns)], [(slots, F32), hot_cell, left_cell] + ext,
        around, cells, sent, segs, kept, matrix_perm,
    )
    around = to_all(edge)
    own, frac2, pressure = call(
        exchange_kernel, both, [slots, frac.shape, (rows, columns)], [hot_seg, left_seg] + ext,
        around, cells, slot, segs, own, frac1, aperture, kept,
    )
    segs = to_group(own)
    edge, kept = call(
        source_last_kernel, both, [halo, (3, rows, columns)], [hot_cell, left_cell],
        cells, sent, own, segs, pressure, kept, matrix_perm,
    )
    around = to_all(edge)
    (frac3,) = call(
        owner_last_kernel, (members,), [frac.shape], [hot_seg, left_seg], slot, own, segs, frac2, aperture
    )
    (matrix_out,) = call(final_kernel, both, [matrix_state.shape], ext, around, pressure, kept)
    return matrix_out, frac3.reshape(frac_state.shape)


def solution(mesh):
    return jax.shard_map(
        on_device,
        mesh=mesh,
        in_specs=(
            P(None, "grp", "frac"),
            P("grp", "frac"),
            P(None, "grp", "frac"),
            P("grp", "frac"),
            P("grp", "frac", None, None),
            P("grp", "frac", None, None),
            P("grp", "frac", None, None),
            P("grp", "frac", None),
            P(None, "grp", "frac", None, None),
        ),
        out_specs=(P(None, "grp", "frac"), P(None, "grp", "frac")),
        check_vma=False,
    )
```

time: 515 us -> 87.3 us (0.17); the launches traced: 509 us -> 86.7 us
  local copies, waits for them, and re-layouts: 216 us -> 4.62 us
  other arithmetic: 196 us -> 0 us
  starting transfers between devices: 47.9 us -> 2.59 us
  blocking collectives: 31.6 us -> 52.1 us
  Pallas kernels: 0 us -> 17.6 us
  between operations: 6.17 us -> 0.71 us
    gather x24 -> x0, local copies, waits for them, and re-layouts: 141 us -> none  [the longest x6 35.4 us: on_device(): seg_saturation = group_states[1][global_segment]]
    scatter-add x6 -> x0, other arithmetic: 97 us -> none  [the longest x3 55.2 us: on_device(): jnp.zeros((3, row_count * column_count), jnp.float32).at[:, cell_flat]]
    slice x6 -> x0, other arithmetic: 90.9 us -> none  [the longest x3 90.8 us: on_device(): source_term = cell_totals[1].reshape(row_count, column_count)]
    all_to_all x0 -> x5, blocking collectives: none -> 52.1 us  [the longest x2 27.2 us: to_all(): lax.all_to_all(x, ('grp', 'frac'), split_axis=0, concat_axis=0, tiled=True)]
    slice x14 -> x0, local copies, waits for them, and re-layouts: 38.1 us -> none  [the longest x3 34.4 us: on_device(): inflow = segment_totals[0]]
    all_gather x3 -> x0, blocking collectives: 31.6 us -> none  [on_device(): lax.all_gather(jnp.stack([frac_pressure, frac_saturation]), 'frac', axis=...]
    unnamed x39 -> x20, local copies, waits for them, and re-layouts: 29 us -> 4.62 us
    ppermute x12 -> x0, starting transfers between devices: 23.9 us -> none  [the longest x6 16.1 us: extended(): lax.ppermute(tail, axis, [(i, (i + 1) % count) for i in range(ends)])]
  transfers between devices with their start and end apart: 16 -> 1, of which waited for: 5 -> 1; matrix products, arithmetic and copies ran while one was open for 31% -> 0% of each run, Pallas kernels for 0% -> 2%
where the time goes in v1:
time: 87.3 us; the launch traced here: 86.7 us
  blocking collectives  52.1 us (60%)
  Pallas kernels  17.6 us (20%)
  waiting for transfers between devices  9.15 us (10%)
  local copies, waits for them, and re-layouts  4.62 us (5%)
  starting transfers between devices  2.59 us (3%)
    all_to_all x2, blocking collectives, to_all(): lax.all_to_all(x, ('grp', 'frac'), split_axis=0, concat_axis=0, tiled=True)  27.2 us
    all_to_all x3, blocking collectives, to_group(): return lax.all_to_all(x, 'frac', split_axis=0, concat_axis=0, tiled=True)  24.9 us
    pallas_call x8, Pallas kernels, call(): pl.pallas_call(functools.partial(kernel, *statics), out_shape=outs, in_sp...  17.6 us
    all_to_all x1, waiting for transfers between devices, to_all(): lax.all_to_all(x, ('grp', 'frac'), split_axis=0, concat_axis=0, tiled=True)  9.15 us
    unnamed x20, local copies, waits for them, and re-layouts  4.62 us
    all_to_all x1, starting transfers between devices, to_all(): lax.all_to_all(x, ('grp', 'frac'), split_axis=0, concat_axis=0, tiled=True)  2.59 us
  transfers between devices with their start and end apart: 1, of which 1 were waited for; matrix products, arithmetic and copies ran while one was open for 0% of the time, Pallas kernels for 2%

profile of v1, /device:TPU:0, one launch (start us, length us, event | category | flops | bytes accessed | tf_op | source)
XLA Modules:
  0.0 86.7 jit_solution(1148331831821295959)
XLA Ops:
  0.6 0.0 copy-start.5
  0.7 0.7 copy-done.5
  1.3 0.9 %copy-done.1 = f32[2,128,256]{2,1,0:T(8,128)S(1)} copy-done((f32[2,128,256]{2,1,0:T(8,128)S(1)}, f32[2,128,256]{2,1,0:T(8,128)}, u32[]{:S(2)}) %copy-start.1) | copy-done | bytes 262168
  2.3 0.8 copy-done.4
  3.1 0.7 copy-done.6
  3.9 0.7 copy-done.7
  4.6 0.7 copy-done.8
  5.3 1.6 %first_kernel.1.sent_ref = f32[8,8,256]{2,1,0:T(8,128)S(1)} custom-call(s32[8,256]{1,0:T(8,128)S(1)} %bitcast.13, s32[8,256]{1,0:T(8,128)S(1)} %bitcast.19, f32[8,256]{1,0:T(8,128)S(1)} %bitcast.20, s32[1,8]{1,0:T(1,128)S(1)} %bitcast.21, s32[3,8,256]{2,1,0:T(8,128)S(1)} %bitcast.18, f32[2,128,256]{2,1,0:T(8,128)S(1)} %copy-done.1, f32[2,64,128]{2,1,0:T(8,128)S(1)} %bitcast.11), custom_call_target="tpu_custom_call" | custom-call | tf_op jit(solution)/shard_map/first_kernel/pallas_call | solution.py:568
  6.9 0.0 copy-start.2
  6.9 10.1 %all_to_all.30.slot_ref = f32[8,8,256]{2,1,0:T(8,128)S(1)} all-to-all(f32[8,8,256]{2,1,0:T(8,128)S(1)} %first_kernel.1.sent_ref), channel_id=1, replica_groups=mesh['grp'=4,'frac'=8] {'frac'}, dimensions={0} | all-to-all | bytes 131072 | tf_op jit(solution)/shard_map/all_to_all | solution.py:610
  17.0 2.5 %owner_start_kernel.1 = (f32[8,8,256]{2,1,0:T(8,128)S(1)}, f32[2,64,128]{2,1,0:T(8,128)S(1)}) custom-call(f32[8,8,256]{2,1,0:T(8,128)S(1)} %all_to_all.30.slot_ref, f32[2,64,128]{2,1,0:T(8,128)S(1)} %bitcast.12, f32[64,128]{1,0:T(8,128)S(1)} %bitcast.8), custom_call_target="tpu_custom_call" | custom-call | tf_op jit(solution)/shard_map/owner_start_kernel/pallas_call | solution.py:568
  19.6 7.4 %all_to_all.31.seg_ref.ends_ref = f32[8,8,256]{2,1,0:T(8,128)S(1)} all-to-all(f32[8,8,256]{2,1,0:T(8,128)S(1)} %get-tuple-element.13.own_ref), channel_id=1, replica_groups=mesh['grp'=4,'frac'=8] {'frac'}, dimensions={0} | all-to-all | bytes 131072 | tf_op jit(solution)/shard_map/all_to_all | solution.py:610
  27.0 0.0 copy-done.2
  27.0 1.5 %source_start_kernel.1 = (f32[32,8,256]{2,1,0:T(8,128)S(1)}, f32[4,128,256]{2,1,0:T(8,128)S(1)}) custom-call(s32[8,256]{1,0:T(8,128)S(1)} %bitcast.14, f32[8,8,256]{2,1,0:T(8,128)S(1)} %first_kernel.1.sent_ref, f32[8,8,256]{2,1,0:T(8,128)S(1)} %all_to_all.31.seg_ref.ends_ref, f32[2,128,256]{2,1,0:T(8,128)S(1)} %copy-done.2, f32[128,256]{1,0:T(8,128)S(1)} %copy-done), custom_call_target="tpu_custom_call" | custom-call | tf_op jit(solution)/shard_map/source_start_kernel/pallas_call | solution.py:568
  28.5 14.4 %all_to_all.32.halo_ref = f32[32,8,256]{2,1,0:T(8,128)S(1)} all-to-all(f32[32,8,256]{2,1,0:T(8,128)S(1)} %get-tuple-element.14), channel_id=1, replica_groups=mesh['grp'=4,'frac'=8] {'grp','frac'}, dimensions={0} | all-to-all | bytes 524288 | tf_op jit(solution)/shard_map/all_to_all | solution.py:613
  42.9 3.1 %middle_kernel.1 = (f32[32,8,256]{2,1,0:T(8,128)S(1)}, f32[4,128,256]{2,1,0:T(8,128)S(1)}) custom-call(f32[32,8,256]{2,1,0:T(8,128)S(1)} %all_to_all.32.halo_ref, s32[8,256]{1,0:T(8,128)S(1)} %bitcast.15, f32[8,8,256]{2,1,0:T(8,128)S(1)} %first_kernel.1.sent_ref, f32[8,8,256]{2,1,0:T(8,128)S(1)} %all_to_all.31.seg_ref.ends_ref, ...), custom_call_target="tpu_custom_call" | custom-call | tf_op jit(solution)/shard_map/middle_kernel/pallas_call | solution.py:568
  46.0 12.8 %all_to_all.33.halo_ref = f32[32,8,256]{2,1,0:T(8,128)S(1)} all-to-all(f32[32,8,256]{2,1,0:T(8,128)S(1)} %get-tuple-element.16), channel_id=1, replica_groups=mesh['grp'=4,'frac'=8] {'grp','frac'}, dimensions={0} | all-to-all | bytes 524288 | tf_op jit(solution)/shard_map/all_to_all | solution.py:613
  58.8 3.5 %exchange_kernel.1 = (f32[8,8,256]{2,1,0:T(8,128)S(1)}, f32[2,64,128]{2,1,0:T(8,128)S(1)}, f32[128,256]{1,0:T(8,128)S(1)}) custom-call(f32[32,8,256]{2,1,0:T(8,128)S(1)} %all_to_all.33.halo_ref, s32[8,256]{1,0:T(8,128)S(1)} %bitcast.16, f32[8,8,256]{2,1,0:T(8,128)S(1)} %all_to_all.30.slot_ref, f32[8,8,256]{2,1,0:T(8,128)S(1)} %all_to_all.31.seg_ref.ends_ref, ...), custom_call_target="tpu_custom_call" | custom-call | tf_op jit(solution)/shard_map/exchange_kernel/pallas_call | solution.py:568
  62.3 7.4 %all_to_all.34.seg_ref = f32[8,8,256]{2,1,0:T(8,128)S(1)} all-to-all(f32[8,8,256]{2,1,0:T(8,128)S(1)} %get-tuple-element.19.own_ref), channel_id=1, replica_groups=mesh['grp'=4,'frac'=8] {'frac'}, dimensions={0} | all-to-all | bytes 131072 | tf_op jit(solution)/shard_map/all_to_all | solution.py:610
  69.7 2.3 %source_last_kernel.1 = (f32[32,8,256]{2,1,0:T(8,128)}, f32[3,128,256]{2,1,0:T(8,128)S(1)}) custom-call(s32[8,256]{1,0:T(8,128)S(1)} %bitcast.17, f32[8,8,256]{2,1,0:T(8,128)S(1)} %first_kernel.1.sent_ref, f32[8,8,256]{2,1,0:T(8,128)S(1)} %get-tuple-element.19.own_ref, f32[8,8,256]{2,1,0:T(8,128)S(1)} %all_to_all.34.seg_ref, ...), custom_call_target="tpu_custom_call" | custom-call | tf_op jit(solution)/shard_map/source_last_kernel/pallas_call | solution.py:568
  71.9 2.6 %all-to-all-start.5 = ((f32[32,8,256]{2,1,0:T(8,128)}), f32[32,8,256]{2,1,0:T(8,128)S(1)}, u32[]{:S(2)}, u32[]{:S(2)}) async-start(f32[32,8,256]{2,1,0:T(8,128)} %get-tuple-element.21), calls=%async_computation.5 | async-start | bytes 524288 | tf_op jit(solution)/shard_map/all_to_all | solution.py:613
  74.5 1.4 %owner_last_kernel.1 = f32[2,64,128]{2,1,0:T(8,128)} custom-call(f32[8,8,256]{2,1,0:T(8,128)S(1)} %all_to_all.30.slot_ref, f32[8,8,256]{2,1,0:T(8,128)S(1)} %get-tuple-element.19.own_ref, f32[8,8,256]{2,1,0:T(8,128)S(1)} %all_to_all.34.seg_ref, f32[2,64,128]{2,1,0:T(8,128)S(1)} %get-tuple-element.23.frac_ref, f32[64,128]{1,0:T(8,128)S(1)} %bitcast.10), custom_call_target="tpu_custom_call" | custom-call | tf_op jit(solution)/shard_map/owner_last_kernel/pallas_call | solution.py:568
  76.0 9.1 %all-to-all-done.5.halo_ref = f32[32,8,256]{2,1,0:T(8,128)S(1)} async-done(((f32[32,8,256]{2,1,0:T(8,128)}), f32[32,8,256]{2,1,0:T(8,128)S(1)}, u32[]{:S(2)}, u32[]{:S(2)}) %all-to-all-start.5) | async-done | bytes 262176 | tf_op jit(solution)/shard_map/all_to_all | solution.py:613
  85.1 1.6 %final_kernel.1 = f32[2,128,256]{2,1,0:T(8,128)} custom-call(f32[32,8,256]{2,1,0:T(8,128)S(1)} %all-to-all-done.5.halo_ref, f32[128,256]{1,0:T(8,128)S(1)} %get-tuple-element.20.pressure_ref, f32[3,128,256]{2,1,0:T(8,128)S(1)} %get-tuple-element.22.kept_ref), custom_call_target="tpu_custom_call" | custom-call | tf_op jit(solution)/shard_map/final_kernel/pallas_call | solution.py:568
  (11 shorter events, 0.0 us)
Async XLA Ops:
  0.6 0.7 copy-start.5
  0.6 0.7 copy-start.9
  1.3 1.0 %copy-start.1 = (f32[2,128,256]{2,1,0:T(8,128)S(1)}, f32[2,128,256]{2,1,0:T(8,128)}, u32[]{:S(2)}) copy-start(f32[2,128,256]{2,1,0:T(8,128)} %state_ref.3) | copy-start | bytes 786436
  2.3 0.8 copy-start.4
  3.1 0.7 copy-start.6
  3.9 0.7 copy-start.7
  4.6 0.7 copy-start.8
  5.3 11.8 %copy-start.3 = (f32[1,8192]{1,0:T(1,128)S(1)}, f32[1,8192]{1,0:T(1,128)}, u32[]{:S(2)}) copy-start(f32[1,8192]{1,0:T(1,128)} %param.12) | copy-start | bytes 98308
  6.9 20.1 %copy-start.2 = (f32[2,128,256]{2,1,0:T(8,128)S(1)}, f32[2,128,256]{2,1,0:T(8,128)}, u32[]{:S(2)}) copy-start(f32[2,128,256]{2,1,0:T(8,128)} %state_ref.3) | copy-start | bytes 786436
  17.0 10.0 %copy-start = (f32[128,256]{1,0:T(8,128)S(1)}, f32[128,256]{1,0:T(8,128)}, u32[]{:S(2)}) copy-start(f32[128,256]{1,0:T(8,128)} %perm_ref.5) | copy-start | bytes 393220
  71.9 13.2 %all-to-all-start.5 = ((f32[32,8,256]{2,1,0:T(8,128)}), f32[32,8,256]{2,1,0:T(8,128)S(1)}, u32[]{:S(2)}, u32[]{:S(2)}) async-start(f32[32,8,256]{2,1,0:T(8,128)} %get-tuple-element.21), calls=%async_computation.5 | async-start | bytes 524288 | tf_op jit(solution)/shard_map/all_to_all | solution.py:613

commit v2 on v1

--- a/solution.py
+++ b/solution.py
@@ -28,15 +28,15 @@
 
 def parts_of(x):
     high = x.astype(BF16).astype(F32)
-    rest = x - high
-    mid = rest.astype(BF16).astype(F32)
-    low = rest - mid
-    return high, mid, low
+    return high, x - high
+
+
+PARTS = 2
 
 
 def table_of(fields):
     split = [parts_of(f) for f in fields]
-    return jnp.concatenate([s[p] for p in range(3) for s in split], axis=0).astype(BF16)
+    return jnp.concatenate([s[p] for p in range(PARTS) for s in split], axis=0).astype(BF16)
 
 
 def one_hot(index_row, count):
@@ -49,18 +49,20 @@
     hit = iota((rows, row_index.shape[1]), 0) == row_index
     found = []
     for f in range(fields):
-        total = sum(wide[(p * fields + f) * rows : (p * fields + f + 1) * rows] for p in range(3))
+        total = sum(wide[(p * fields + f) * rows : (p * fields + f + 1) * rows] for p in range(PARTS))
         found.append(jnp.sum(jnp.where(hit, total, 0.0), axis=0, keepdims=True))
     return found
 
 
-def spread(left_ref, block, width, rows, row_index, values):
-    hit = iota((rows, row_index.shape[1]), 0) == row_index
+def spread(left_ref, row_hot_ref, block, values):
+    rows = row_hot_ref.shape[0]
+    width = values[0].shape[1]
     at = slice(block * width, (block + 1) * width)
+    hot = row_hot_ref[:, at]
     for f, value in enumerate(values):
         for p, part in enumerate(parts_of(value)):
             row = (p * len(values) + f) * rows
-            left_ref[row : row + rows, at] = jnp.where(hit, part, 0.0).astype(BF16)
+            left_ref[row : row + rows, at] = hot * part.astype(BF16)
 
 
 def gathered_sum(left_ref, hot_ref, fields, rows):
@@ -68,7 +70,7 @@
         left_ref[...], hot_ref[...], (((1,), (1,)), ((), ())), preferred_element_type=F32
     )
     return [
-        sum(wide[(p * fields + f) * rows : (p * fields + f + 1) * rows] for p in range(3))
+        sum(wide[(p * fields + f) * rows : (p * fields + f + 1) * rows] for p in range(PARTS))
         for f in range(fields)
     ]
 
@@ -237,16 +239,23 @@
     p_ext[corner, side] = both(low[:, LANES:], high[:, LANES:], sub, DEPTH, SUB)
 
     shape = (rows + SUB, columns + LANES)
-    row, col = iota(shape, 0), iota(shape, 1)
-    field = p_ext[...]
-    missing = jnp.where((row == 0) | (row == rows), pltpu.roll(field, 1, 0), 0.0)
-    missing += jnp.where((row == rows - 1) | (row == rows + SUB - 1), pltpu.roll(field, shape[0] - 1, 0), 0.0)
-    missing += jnp.where((col == 0) | (col == columns), pltpu.roll(field, 1, 1), 0.0)
-    missing += jnp.where(
-        (col == columns - 1) | (col == columns + LANES - 1), pltpu.roll(field, shape[1] - 1, 1), 0.0
+    for here_row, there_row in ((0, shape[0] - 1), (shape[0] - 1, 0), (rows - 1, rows), (rows, rows - 1)):
+        q_ext[here_row : here_row + 1, :] += (
+            inv_ext[here_row : here_row + 1, :] * p_ext[there_row : there_row + 1, :]
+        )
+    lane = iota((shape[0], LANES), 1)
+    first, final = slice(0, LANES), slice(columns - LANES, columns)
+    p_side = p_ext[:, side]
+    from_left, from_right = pltpu.roll(p_side, 1, 1), pltpu.roll(p_side, LANES - 1, 1)
+    q_ext[:, first] += inv_ext[:, first] * jnp.where(lane == 0, from_left, 0.0)
+    q_ext[:, final] += inv_ext[:, final] * jnp.where(lane == LANES - 1, from_right, 0.0)
+    q_ext[:, side] += inv_ext[:, side] * jnp.where(
+        lane == 0,
+        pltpu.roll(p_ext[:, final], 1, 1),
+        jnp.where(lane == LANES - 1, pltpu.roll(p_ext[:, first], LANES - 1, 1), 0.0),
     )
     inverse = inv_ext[...]
-    start = q_ext[...] + inverse * missing
+    start = q_ext[...]
 
     centre = 0.5 * (HIGH_BOUND + LOW_BOUND)
     half_width = 0.5 * (HIGH_BOUND - LOW_BOUND)
@@ -277,15 +286,45 @@
 ROW_ENDS = ROW_S + 1
 
 
-def first_kernel(members, cell_ref, seg_ref, trans_ref, count_ref, up_ref, state_ref, frac_ref, out_ref):
+def first_kernel(
+    members, cell_any, seg_any, trans_any, count_any, up_any, state_any, frac_any,
+    out_ref, hot_ref, row_hot_ref, cell_ref, seg_ref, trans_ref, count_ref, up_ref, state_ref, ends_ref, sem,
+):
     _, rows, columns = state_ref.shape
     width = cell_ref.shape[1]
+    seg_rows = frac_any.shape[1]
+    copies = [
+        pltpu.make_async_copy(source, target, sem.at[i])
+        for i, (source, target) in enumerate(
+            [
+                (cell_any, cell_ref),
+                (state_any, state_ref),
+                (seg_any, seg_ref),
+                (trans_any, trans_ref),
+                (count_any, count_ref),
+                (up_any, up_ref),
+                (frac_any.at[0, 0:SUB], ends_ref.at[0]),
+                (frac_any.at[0, seg_rows - SUB : seg_rows], ends_ref.at[1]),
+            ]
+        )
+    ]
+    for copy in copies:
+        copy.start()
+    copies[0].wait()
+    for o in range(members):
+        row, col = cell_parts(cell_ref[o : o + 1, :], columns)
+        at = slice(o * width, (o + 1) * width)
+        hot_ref[:, at] = one_hot(col, columns)
+        row_hot_ref[:, at] = one_hot(row, rows)
+    copies[1].wait()
     table = table_of([state_ref[0], state_ref[1]])
-    ends = ends_of(frac_ref[0])
+    for copy in copies[2:]:
+        copy.wait()
+    ends = jnp.concatenate([ends_ref[0, 0:1], ends_ref[1, SUB - 1 : SUB]], axis=1)
     for o in range(members):
         one = slice(o, o + 1)
-        row, col = cell_parts(cell_ref[one, :], columns)
-        cell_p, cell_s = pick(table, 2, rows, row, one_hot(col, columns))
+        row, _ = cell_parts(cell_ref[one, :], columns)
+        cell_p, cell_s = pick(table, 2, rows, row, hot_ref[:, o * width : (o + 1) * width])
         live = iota((1, width), 1) < count_ref[0, o]
         out_ref[o, ROW_SEG : ROW_SEG + 1, :] = seg_ref[one, :].astype(F32)
         out_ref[o, ROW_TRANS : ROW_TRANS + 1, :] = jnp.where(live, trans_ref[one, :], 0.0)
@@ -301,20 +340,25 @@
     return seg // LANES, seg % LANES
 
 
-def seg_hots(slot_ref, hot_ref, members, width):
+def seg_hots(slot_ref, hot_ref, row_hot_ref, members, width):
     for s in range(members):
-        hot_ref[:, s * width : (s + 1) * width] = one_hot(seg_parts(slot_ref, s)[1], LANES)
+        row, lane = seg_parts(slot_ref, s)
+        at = slice(s * width, (s + 1) * width)
+        hot_ref[:, at] = one_hot(lane, LANES)
+        row_hot_ref[:, at] = one_hot(row, row_hot_ref.shape[0])
 
 
 def seg_gather(slot_ref, hot_ref, fields, s, width, table):
     return pick(table, 2, fields, seg_parts(slot_ref, s)[0], hot_ref[:, s * width : (s + 1) * width])
 
 
-def owner_start_kernel(members, slot_ref, frac_ref, aperture_ref, out_ref, new_ref, hot_ref, left_ref):
+def owner_start_kernel(
+    members, slot_ref, frac_ref, aperture_ref, out_ref, new_ref, hot_ref, row_hot_ref, left_ref
+):
     width = slot_ref.shape[2]
     rows = frac_ref.shape[1]
     frac, sat = frac_ref[0], frac_ref[1]
-    seg_hots(slot_ref, hot_ref, members, width)
+    seg_hots(slot_ref, hot_ref, row_hot_ref, members, width)
     table = table_of([frac, sat])
     for s in range(members):
         seg_p, seg_s = seg_gather(slot_ref, hot_ref, rows, s, width, table)
@@ -330,7 +374,7 @@
             seg_p,
             seg_s,
         )
-        spread(left_ref, s, width, rows, seg_parts(slot_ref, s)[0], [weight * cell_p, weight, water])
+        spread(left_ref, row_hot_ref, s, [weight * cell_p, weight, water])
     inflow, total, gained = gathered_sum(left_ref, hot_ref, 3, rows)
     before, after = chain_ends(slot_ref, ROW_ENDS, members)
     new_frac, new_sat = frac_step(frac, sat, aperture_ref[...], before, after, inflow, total, gained)
@@ -346,13 +390,10 @@
 
 
 def cell_update(
-    members, t, cell_ref, sent_ref, cell_rows, seg_rows, pressure, saturation, perm, hot_ref, left_ref
-):
-    rows, columns = pressure.shape
-    width = cell_ref.shape[1]
+    members, t, hot_ref, row_hot_ref, sent_ref, cell_rows, seg_rows, pressure, saturation, perm, left_ref
+):
+    rows = pressure.shape[0]
     for o in range(members):
-        row, col = cell_parts(cell_ref[o : o + 1, :], columns)
-        hot_ref[:, o * width : (o + 1) * width] = one_hot(col, columns)
         seg_p, seg_s = seg_rows(o)
         cell_p, cell_s = cell_rows(o)
         weight, water = flow(
@@ -363,7 +404,7 @@
             seg_p,
             seg_s,
         )
-        spread(left_ref, o, width, rows, row, [weight, weight * seg_p, water])
+        spread(left_ref, row_hot_ref, o, [weight, weight * seg_p, water])
     couple, source, lost = gathered_sum(left_ref, hot_ref, 3, rows)
     inverse = 1.0 / (4.0 + perm + couple)
     new_saturation = saturation - TAU_STEP * lost / (perm + couple)
@@ -371,20 +412,20 @@
 
 
 def source_start_kernel(
-    groups, members, cell_ref, sent_ref, seg_ref, state_ref, perm_ref, out_ref, keep_ref, hot_ref, left_ref
+    groups, members, hot_ref, row_hot_ref, sent_ref, seg_ref, state_ref, perm_ref, out_ref, keep_ref, left_ref
 ):
     pressure = state_ref[0]
     new_saturation, q, inv = cell_update(
         members,
         0,
-        cell_ref,
+        hot_ref,
+        row_hot_ref,
         sent_ref,
         lambda o: (sent_ref[o, ROW_P : ROW_P + 1, :], sent_ref[o, ROW_S : ROW_S + 1, :]),
         lambda o: (seg_ref[o, 0:1, :], seg_ref[o, 1:2, :]),
         pressure,
         state_ref[1],
         perm_ref[...],
-        hot_ref,
         left_ref,
     )
     keep_ref[0] = pressure
@@ -394,17 +435,18 @@
     send_halo(out_ref, q, inv, pressure, groups, members)
 
 
-def cell_gather(members, cell_ref, fields, put):
+def cell_gather(members, cell_ref, hot_ref, fields, put):
     rows, columns = fields[0].shape
+    width = cell_ref.shape[1]
     table = table_of(fields)
     for o in range(members):
-        row, col = cell_parts(cell_ref[o : o + 1, :], columns)
-        put(o, *pick(table, len(fields), rows, row, one_hot(col, columns)))
+        row, _ = cell_parts(cell_ref[o : o + 1, :], columns)
+        put(o, *pick(table, len(fields), rows, row, hot_ref[:, o * width : (o + 1) * width]))
 
 
 def middle_kernel(
-    groups, members, halo_ref, cell_ref, sent_ref, seg_ref, kept_ref, perm_ref, out_ref, keep_ref,
-    slots_ref, hot_ref, left_ref, q_ext, inv_ext, p_ext,
+    groups, members, halo_ref, cell_ref, hot_ref, row_hot_ref, sent_ref, seg_ref, kept_ref, perm_ref,
+    out_ref, keep_ref, slots_ref, left_ref, q_ext, inv_ext, p_ext,
 ):
     pressure = chebyshev(
         halo_ref, kept_ref[2], kept_ref[3], kept_ref[0], q_ext, inv_ext, p_ext, groups, members
@@ -420,18 +462,18 @@
             out_ref[g * members + o, half : half + 1, LANES : 2 * LANES] = cell_p[:, at]
             out_ref[g * members + o, 2 + half : 3 + half, LANES : 2 * LANES] = cell_s[:, at]
 
-    cell_gather(members, cell_ref, [pressure, saturation], put)
+    cell_gather(members, cell_ref, hot_ref, [pressure, saturation], put)
     new_saturation, q, inv = cell_update(
         members,
         1,
-        cell_ref,
+        hot_ref,
+        row_hot_ref,
         sent_ref,
         lambda o: (slots_ref[o, 0:1, :], slots_ref[o, 1:2, :]),
         lambda o: (seg_ref[o, 2:3, :], seg_ref[o, 3:4, :]),
         pressure,
         saturation,
         perm_ref[...],
-        hot_ref,
         left_ref,
     )
     keep_ref[0] = pressure
@@ -441,10 +483,10 @@
     send_halo(out_ref, q, inv, pressure, groups, members)
 
 
-def owner_update(members, t, slot_ref, cell_rows, seg_rows, frac, sat, aperture, ends, hot_ref, left_ref):
-    width = slot_ref.shape[2]
+def owner_update(
+    members, t, slot_ref, cell_rows, seg_rows, frac, sat, aperture, ends, hot_ref, row_hot_ref, left_ref
+):
     rows = frac.shape[0]
-    seg_hots(slot_ref, hot_ref, members, width)
     for s in range(members):
         cell_p, cell_s = cell_rows(s)
         weight, water = flow(
@@ -454,14 +496,14 @@
             cell_s,
             *seg_rows(s),
         )
-        spread(left_ref, s, width, rows, seg_parts(slot_ref, s)[0], [weight * cell_p, weight, water])
+        spread(left_ref, row_hot_ref, s, [weight * cell_p, weight, water])
     inflow, total, gained = gathered_sum(left_ref, hot_ref, 3, rows)
     return frac_step(frac, sat, aperture, *ends, inflow, total, gained)
 
 
 def exchange_kernel(
-    groups, members, halo_ref, cell_ref, slot_ref, ends_ref, own_ref, frac_ref, aperture_ref, kept_ref,
-    out_ref, new_ref, pressure_ref, hot_ref, left_ref, q_ext, inv_ext, p_ext,
+    groups, members, halo_ref, cell_ref, cell_hot_ref, slot_ref, hot_ref, row_hot_ref, ends_ref, own_ref,
+    frac_ref, aperture_ref, kept_ref, out_ref, new_ref, pressure_ref, left_ref, q_ext, inv_ext, p_ext,
 ):
     width = slot_ref.shape[2]
     rows = frac_ref.shape[1]
@@ -486,6 +528,7 @@
         aperture_ref[...],
         chain_ends(ends_ref, 4, members),
         hot_ref,
+        row_hot_ref,
         left_ref,
     )
     new_ref[0] = new_frac
@@ -507,25 +550,25 @@
         out_ref[o, 0:1, :] = cell_p
         out_ref[o, 1:2, :] = cell_s
 
-    cell_gather(members, cell_ref, [pressure, kept_ref[1]], put)
+    cell_gather(members, cell_ref, cell_hot_ref, [pressure, kept_ref[1]], put)
 
 
 def source_last_kernel(
-    groups, members, cell_ref, sent_ref, own_ref, seg_ref, pressure_ref, kept_ref, perm_ref, out_ref, keep_ref,
-    hot_ref, left_ref,
+    groups, members, hot_ref, row_hot_ref, sent_ref, own_ref, seg_ref, pressure_ref, kept_ref, perm_ref,
+    out_ref, keep_ref, left_ref,
 ):
     pressure = pressure_ref[...]
     new_saturation, q, inv = cell_update(
         members,
         2,
-        cell_ref,
+        hot_ref,
+        row_hot_ref,
         sent_ref,
         lambda o: (own_ref[o, 0:1, :], own_ref[o, 1:2, :]),
         lambda o: (seg_ref[o, 2:3, :], seg_ref[o, 3:4, :]),
         pressure,
         kept_ref[1],
         perm_ref[...],
-        hot_ref,
         left_ref,
     )
     keep_ref[0] = new_saturation
@@ -534,7 +577,9 @@
     send_halo(out_ref, q, inv, pressure, groups, members)
 
 
-def owner_last_kernel(members, slot_ref, own_ref, seg_ref, frac_ref, aperture_ref, out_ref, hot_ref, left_ref):
+def owner_last_kernel(
+    members, slot_ref, hot_ref, row_hot_ref, own_ref, seg_ref, frac_ref, aperture_ref, out_ref, left_ref
+):
     new_frac, new_sat = owner_update(
         members,
         2,
@@ -546,6 +591,7 @@
         aperture_ref[...],
         chain_ends(seg_ref, 4, members),
         hot_ref,
+        row_hot_ref,
         left_ref,
     )
     out_ref[0] = new_frac
@@ -560,17 +606,17 @@
 
 
 VMEM = pl.BlockSpec(memory_space=pltpu.VMEM)
-SMEM = pl.BlockSpec(memory_space=pltpu.SMEM)
-
-
-def call(kernel, statics, outs, scratch, *args, smem=()):
-    outs = [jax.ShapeDtypeStruct(s, F32) for s in outs]
+HBM = pl.BlockSpec(memory_space=pltpu.HBM)
+
+
+def call(kernel, statics, outs, scratch, *args, spec=VMEM):
+    outs = [o if hasattr(o, "dtype") else jax.ShapeDtypeStruct(o, F32) for o in outs]
     return pl.pallas_call(
         functools.partial(kernel, *statics),
         out_shape=outs,
-        in_specs=[SMEM if i in smem else VMEM for i in range(len(args))],
+        in_specs=[spec] * len(args),
         out_specs=[VMEM] * len(outs),
-        scratch_shapes=[pltpu.VMEM(s, t) for s, t in scratch],
+        scratch_shapes=scratch,
         compiler_params=pltpu.CompilerParams(vmem_limit_bytes=32 * 1024 * 1024),
         name=kernel.__name__,
     )(*args)
@@ -598,13 +644,12 @@
     frac = frac_state.reshape(2, seg_rows, LANES)
     aperture = frac_aperture.reshape(seg_rows, LANES)
 
+    every = members * width
     slots = (members, SUB, width)
     halo = (devices, SUB, columns)
-    hot_cell = ((columns, members * width), BF16)
-    left_cell = ((9 * rows, members * width), BF16)
-    hot_seg = ((LANES, members * width), BF16)
-    left_seg = ((9 * seg_rows, members * width), BF16)
-    ext = [((rows + SUB, columns + LANES), F32)] * 3
+    left_cell = pltpu.VMEM((3 * PARTS * rows, every), BF16)
+    left_seg = pltpu.VMEM((3 * PARTS * seg_rows, every), BF16)
+    ext = [pltpu.VMEM((rows + SUB, columns + LANES), F32)] * 3
 
     def to_group(x):
         return lax.all_to_all(x, "frac", split_axis=0, concat_axis=0, tiled=True)
@@ -612,38 +657,54 @@
     def to_all(x):
         return lax.all_to_all(x, ("grp", "frac"), split_axis=0, concat_axis=0, tiled=True)
 
-    (sent,) = call(
-        first_kernel, (members,), [slots], [],
+    def hots(*sizes):
+        return [jax.ShapeDtypeStruct((n, every), BF16) for n in sizes]
+
+    sent, cell_hot, cell_row_hot = call(
+        first_kernel,
+        (members,),
+        [slots] + hots(columns, rows),
+        [
+            pltpu.VMEM((members, width), jnp.int32),
+            pltpu.VMEM((members, width), jnp.int32),
+            pltpu.VMEM((members, width), F32),
+            pltpu.SMEM((1, members), jnp.int32),
+            pltpu.VMEM((ITERS, members, width), jnp.int32),
+            pltpu.VMEM(matrix_state.shape, F32),
+            pltpu.VMEM((2, SUB, LANES), F32),
+            pltpu.SemaphoreType.DMA((8,)),
+        ],
         cells, link_seg[0, 0], link_trans[0, 0], link_count[0], link_upwind[:, 0, 0], matrix_state, frac,
-        smem=(3,),
+        spec=HBM,
     )
     slot = to_group(sent)
-    own, frac1 = call(
-        owner_start_kernel, (members,), [slots, frac.shape], [hot_seg, left_seg], slot, frac, aperture
+    own, frac1, hot, row_hot = call(
+        owner_start_kernel, (members,), [slots, frac.shape] + hots(LANES, seg_rows), [left_seg],
+        slot, frac, aperture,
     )
     segs = to_group(own)
     edge, kept = call(
-        source_start_kernel, both, [halo, (4, rows, columns)], [hot_cell, left_cell],
-        cells, sent, segs, matrix_state, matrix_perm,
+        source_start_kernel, both, [halo, (4, rows, columns)], [left_cell],
+        cell_hot, cell_row_hot, sent, segs, matrix_state, matrix_perm,
     )
     around = to_all(edge)
     edge, kept = call(
-        middle_kernel, both, [halo, (4, rows, columns)], [(slots, F32), hot_cell, left_cell] + ext,
-        around, cells, sent, segs, kept, matrix_perm,
+        middle_kernel, both, [halo, (4, rows, columns)], [pltpu.VMEM(slots, F32), left_cell] + ext,
+        around, cells, cell_hot, cell_row_hot, sent, segs, kept, matrix_perm,
     )
     around = to_all(edge)
     own, frac2, pressure = call(
-        exchange_kernel, both, [slots, frac.shape, (rows, columns)], [hot_seg, left_seg] + ext,
-        around, cells, slot, segs, own, frac1, aperture, kept,
+        exchange_kernel, both, [slots, frac.shape, (rows, columns)], [left_seg] + ext,
+        around, cells, cell_hot, slot, hot, row_hot, segs, own, frac1, aperture, kept,
     )
     segs = to_group(own)
     edge, kept = call(
-        source_last_kernel, both, [halo, (3, rows, columns)], [hot_cell, left_cell],
-        cells, sent, own, segs, pressure, kept, matrix_perm,
+        source_last_kernel, both, [halo, (3, rows, columns)], [left_cell],
+        cell_hot, cell_row_hot, sent, own, segs, pressure, kept, matrix_perm,
     )
     around = to_all(edge)
     (frac3,) = call(
-        owner_last_kernel, (members,), [frac.shape], [hot_seg, left_seg], slot, own, segs, frac2, aperture
+        owner_last_kernel, (members,), [frac.shape], [left_seg], slot, hot, row_hot, own, segs, frac2, aperture
     )
     (matrix_out,) = call(final_kernel, both, [matrix_state.shape], ext, around, pressure, kept)
     return matrix_out, frac3.reshape(frac_state.shape)

time: 87.3 us -> 83.7 us (0.959)
  Pallas kernels: 17.6 us -> 13.7 us
    pallas_call x8, Pallas kernels: 17.6 us -> 13.7 us  [call(): pl.pallas_call(functools.partial(kernel, *statics), out_shape=outs, in_sp...]
  transfers between devices with their start and end apart: 1 -> 1, of which waited for: 1 -> 1; matrix products, arithmetic and copies ran while one was open for 0% -> 0% of each run, Pallas kernels for 2% -> 1%
where the time goes in v2:
time: 83.7 us; the launch traced here: 83.1 us
  blocking collectives  52.1 us (62%)
  Pallas kernels  13.7 us (16%)
  waiting for transfers between devices  9.35 us (11%)
  local copies, waits for them, and re-layouts  4.62 us (6%)
  starting transfers between devices  2.59 us (3%)
    all_to_all x2, blocking collectives, to_all(): lax.all_to_all(x, ('grp', 'frac'), split_axis=0, concat_axis=0, tiled=True)  27.1 us
    all_to_all x3, blocking collectives, to_group(): return lax.all_to_all(x, 'frac', split_axis=0, concat_axis=0, tiled=True)  24.9 us
    pallas_call x8, Pallas kernels, call(): pl.pallas_call(functools.partial(kernel, *statics), out_shape=outs, in_sp...  13.7 us
    all_to_all x1, waiting for transfers between devices, to_all(): lax.all_to_all(x, ('grp', 'frac'), split_axis=0, concat_axis=0, tiled=True)  9.35 us
    unnamed x20, local copies, waits for them, and re-layouts  4.62 us
    all_to_all x1, starting transfers between devices, to_all(): lax.all_to_all(x, ('grp', 'frac'), split_axis=0, concat_axis=0, tiled=True)  2.59 us
  transfers between devices with their start and end apart: 1, of which 1 were waited for; matrix products, arithmetic and copies ran while one was open for 0% of the time, Pallas kernels for 1%

profile of v2, /device:TPU:0, one launch (start us, length us, event | category | flops | bytes accessed | tf_op | source)
XLA Modules:
  0.0 83.1 jit_solution(2886613975135305108)
XLA Ops:
  0.6 0.0 copy-start.5
  0.7 0.7 copy-done.5
  1.3 0.9 %copy-done.1 = f32[2,128,256]{2,1,0:T(8,128)S(1)} copy-done((f32[2,128,256]{2,1,0:T(8,128)S(1)}, f32[2,128,256]{2,1,0:T(8,128)}, u32[]{:S(2)}) %copy-start.1) | copy-done | bytes 262168
  2.3 0.8 %copy-done.4 = f32[2,1,8192]{2,1,0:T(1,128)S(1)} copy-done((f32[2,1,8192]{2,1,0:T(1,128)S(1)}, f32[2,1,8192]{2,1,0:T(1,128)}, u32[]{:S(2)}) %copy-start.4) | copy-done | bytes 65560
  3.1 0.7 copy-done.6
  3.9 0.7 copy-done.7
  4.6 0.7 copy-done.8
  5.3 1.4 %first_kernel.1 = (f32[8,8,256]{2,1,0:T(8,128)S(1)}, bf16[256,2048]{1,0:T(8,128)(2,1)S(1)}, bf16[128,2048]{1,0:T(8,128)(2,1)S(1)}) custom-call(s32[8,256]{1,0:T(8,128)S(1)} %bitcast.13, s32[8,256]{1,0:T(8,128)S(1)} %bitcast.17, f32[8,256]{1,0:T(8,128)S(1)} %bitcast.18, s32[1,8]{1,0:T(1,128)S(1)} %bitcast.19, s32[3,8,256]{2,1,0:T(8,128)S(1)} %bitcast.16, ...), custom_call_target="tpu_custom_call" | custom-call | tf_op jit(solution)/shard_map/first_kernel/pallas_call | solution.py:614
  6.7 0.0 copy-start.2
  6.7 10.1 %all_to_all.30.slot_ref = f32[8,8,256]{2,1,0:T(8,128)S(1)} all-to-all(f32[8,8,256]{2,1,0:T(8,128)S(1)} %get-tuple-element.20.sent_ref), channel_id=1, replica_groups=mesh['grp'=4,'frac'=8] {'frac'}, dimensions={0} | all-to-all | bytes 131072 | tf_op jit(solution)/shard_map/all_to_all | solution.py:655
  16.9 0.0 copy-done.3
  16.9 1.9 %owner_start_kernel.1 = (f32[8,8,256]{2,1,0:T(8,128)S(1)}, f32[2,64,128]{2,1,0:T(8,128)S(1)}, bf16[128,2048]{1,0:T(8,128)(2,1)S(1)}, bf16[64,2048]{1,0:T(8,128)(2,1)S(1)}) custom-call(f32[8,8,256]{2,1,0:T(8,128)S(1)} %all_to_all.30.slot_ref, f32[2,64,128]{2,1,0:T(8,128)S(1)} %bitcast.12, f32[64,128]{1,0:T(8,128)S(1)} %bitcast.8), custom_call_target="tpu_custom_call" | custom-call | tf_op jit(solution)/shard_map/owner_start_kernel/pallas_call | solution.py:614
  18.7 7.4 %all_to_all.31.seg_ref.ends_ref = f32[8,8,256]{2,1,0:T(8,128)S(1)} all-to-all(f32[8,8,256]{2,1,0:T(8,128)S(1)} %get-tuple-element.21.own_ref), channel_id=1, replica_groups=mesh['grp'=4,'frac'=8] {'frac'}, dimensions={0} | all-to-all | bytes 131072 | tf_op jit(solution)/shard_map/all_to_all | solution.py:655
  26.1 1.1 %source_start_kernel.1 = (f32[32,8,256]{2,1,0:T(8,128)S(1)}, f32[4,128,256]{2,1,0:T(8,128)S(1)}) custom-call(bf16[256,2048]{1,0:T(8,128)(2,1)S(1)} %get-tuple-element.18.hot_ref.cell_hot_ref, bf16[128,2048]{1,0:T(8,128)(2,1)S(1)} %get-tuple-element.19.row_hot_ref, f32[8,8,256]{2,1,0:T(8,128)S(1)} %get-tuple-element.20.sent_ref, ...), custom_call_target="tpu_custom_call" | custom-call | tf_op jit(solution)/shard_map/source_start_kernel/pallas_call | solution.py:614
  27.2 14.4 %all_to_all.32.halo_ref = f32[32,8,256]{2,1,0:T(8,128)S(1)} all-to-all(f32[32,8,256]{2,1,0:T(8,128)S(1)} %get-tuple-element.22), channel_id=1, replica_groups=mesh['grp'=4,'frac'=8] {'grp','frac'}, dimensions={0} | all-to-all | bytes 524288 | tf_op jit(solution)/shard_map/all_to_all | solution.py:658
  41.6 2.4 %middle_kernel.1 = (f32[32,8,256]{2,1,0:T(8,128)S(1)}, f32[4,128,256]{2,1,0:T(8,128)S(1)}) custom-call(f32[32,8,256]{2,1,0:T(8,128)S(1)} %all_to_all.32.halo_ref, s32[8,256]{1,0:T(8,128)S(1)} %bitcast.14, bf16[256,2048]{1,0:T(8,128)(2,1)S(1)} %get-tuple-element.18.hot_ref.cell_hot_ref, bf16[128,2048]{1,0:T(8,128)(2,1)S(1)} %get-tuple-element.19.row_hot_ref, ...), custom_call_target="tpu_custom_call" | custom-call | tf_op jit(solution)/shard_map/middle_kernel/pallas_call | solution.py:614
  44.0 12.8 %all_to_all.33.halo_ref = f32[32,8,256]{2,1,0:T(8,128)S(1)} all-to-all(f32[32,8,256]{2,1,0:T(8,128)S(1)} %get-tuple-element.24), channel_id=1, replica_groups=mesh['grp'=4,'frac'=8] {'grp','frac'}, dimensions={0} | all-to-all | bytes 524288 | tf_op jit(solution)/shard_map/all_to_all | solution.py:658
  56.8 2.4 %exchange_kernel.1 = (f32[8,8,256]{2,1,0:T(8,128)S(1)}, f32[2,64,128]{2,1,0:T(8,128)S(1)}, f32[128,256]{1,0:T(8,128)S(1)}) custom-call(f32[32,8,256]{2,1,0:T(8,128)S(1)} %all_to_all.33.halo_ref, s32[8,256]{1,0:T(8,128)S(1)} %bitcast.15, bf16[256,2048]{1,0:T(8,128)(2,1)S(1)} %get-tuple-element.18.hot_ref.cell_hot_ref, f32[8,8,256]{2,1,0:T(8,128)S(1)} %all_to_all.30.slot_ref, ...), custom_call_target="tpu_custom_call" | custom-call | tf_op jit(solution)/shard_map/exchange_kernel/pallas_call | solution.py:614
  59.2 7.4 %all_to_all.34.seg_ref = f32[8,8,256]{2,1,0:T(8,128)S(1)} all-to-all(f32[8,8,256]{2,1,0:T(8,128)S(1)} %get-tuple-element.29.own_ref), channel_id=1, replica_groups=mesh['grp'=4,'frac'=8] {'frac'}, dimensions={0} | all-to-all | bytes 131072 | tf_op jit(solution)/shard_map/all_to_all | solution.py:655
  66.6 1.8 %source_last_kernel.1 = (f32[32,8,256]{2,1,0:T(8,128)}, f32[3,128,256]{2,1,0:T(8,128)S(1)}) custom-call(bf16[256,2048]{1,0:T(8,128)(2,1)S(1)} %get-tuple-element.18.hot_ref.cell_hot_ref, bf16[128,2048]{1,0:T(8,128)(2,1)S(1)} %get-tuple-element.19.row_hot_ref, f32[8,8,256]{2,1,0:T(8,128)S(1)} %get-tuple-element.20.sent_ref, ...), custom_call_target="tpu_custom_call" | custom-call | tf_op jit(solution)/shard_map/source_last_kernel/pallas_call | solution.py:614
  68.4 2.6 %all-to-all-start.5 = ((f32[32,8,256]{2,1,0:T(8,128)}), f32[32,8,256]{2,1,0:T(8,128)S(1)}, u32[]{:S(2)}, u32[]{:S(2)}) async-start(f32[32,8,256]{2,1,0:T(8,128)} %get-tuple-element.31), calls=%async_computation.5 | async-start | bytes 524288 | tf_op jit(solution)/shard_map/all_to_all | solution.py:658
  71.0 1.2 %owner_last_kernel.1 = f32[2,64,128]{2,1,0:T(8,128)} custom-call(f32[8,8,256]{2,1,0:T(8,128)S(1)} %all_to_all.30.slot_ref, bf16[128,2048]{1,0:T(8,128)(2,1)S(1)} %get-tuple-element.25.hot_ref, bf16[64,2048]{1,0:T(8,128)(2,1)S(1)} %get-tuple-element.26.row_hot_ref, f32[8,8,256]{2,1,0:T(8,128)S(1)} %get-tuple-element.29.own_ref, ...), custom_call_target="tpu_custom_call" | custom-call | tf_op jit(solution)/shard_map/owner_last_kernel/pallas_call | solution.py:614
  72.2 9.4 %all-to-all-done.5.halo_ref = f32[32,8,256]{2,1,0:T(8,128)S(1)} async-done(((f32[32,8,256]{2,1,0:T(8,128)}), f32[32,8,256]{2,1,0:T(8,128)S(1)}, u32[]{:S(2)}, u32[]{:S(2)}) %all-to-all-start.5) | async-done | bytes 262176 | tf_op jit(solution)/shard_map/all_to_all | solution.py:658
  81.6 1.5 %final_kernel.1 = f32[2,128,256]{2,1,0:T(8,128)} custom-call(f32[32,8,256]{2,1,0:T(8,128)S(1)} %all-to-all-done.5.halo_ref, f32[128,256]{1,0:T(8,128)S(1)} %get-tuple-element.30.pressure_ref, f32[3,128,256]{2,1,0:T(8,128)S(1)} %get-tuple-element.32.kept_ref), custom_call_target="tpu_custom_call" | custom-call | tf_op jit(solution)/shard_map/final_kernel/pallas_call | solution.py:614
  (11 shorter events, 0.0 us)
Async XLA Ops:
  0.6 0.7 copy-start.5
  0.6 0.7 copy-start.9
  1.3 1.0 %copy-start.1 = (f32[2,128,256]{2,1,0:T(8,128)S(1)}, f32[2,128,256]{2,1,0:T(8,128)}, u32[]{:S(2)}) copy-start(f32[2,128,256]{2,1,0:T(8,128)} %state_ref.1) | copy-start | bytes 786436
  2.3 0.8 %copy-start.4 = (f32[2,1,8192]{2,1,0:T(1,128)S(1)}, f32[2,1,8192]{2,1,0:T(1,128)}, u32[]{:S(2)}) copy-start(f32[2,1,8192]{2,1,0:T(1,128)} %param.11) | copy-start | bytes 196612
  3.1 0.7 copy-start.6
  3.9 0.7 copy-start.7
  4.6 0.7 copy-start.8
  5.3 11.6 %copy-start.3 = (f32[1,8192]{1,0:T(1,128)S(1)}, f32[1,8192]{1,0:T(1,128)}, u32[]{:S(2)}) copy-start(f32[1,8192]{1,0:T(1,128)} %param.12) | copy-start | bytes 98308
  6.7 19.4 %copy-start.2 = (f32[2,128,256]{2,1,0:T(8,128)S(1)}, f32[2,128,256]{2,1,0:T(8,128)}, u32[]{:S(2)}) copy-start(f32[2,128,256]{2,1,0:T(8,128)} %state_ref.1) | copy-start | bytes 786436
  16.9 9.3 %copy-start = (f32[128,256]{1,0:T(8,128)S(1)}, f32[128,256]{1,0:T(8,128)}, u32[]{:S(2)}) copy-start(f32[128,256]{1,0:T(8,128)} %perm_ref.5) | copy-start | bytes 393220
  68.4 13.2 %all-to-all-start.5 = ((f32[32,8,256]{2,1,0:T(8,128)}), f32[32,8,256]{2,1,0:T(8,128)S(1)}, u32[]{:S(2)}, u32[]{:S(2)}) async-start(f32[32,8,256]{2,1,0:T(8,128)} %get-tuple-element.31), calls=%async_computation.5 | async-start | bytes 524288 | tf_op jit(solution)/shard_map/all_to_all | solution.py:658

commit v3 on v2

--- a/solution.py
+++ b/solution.py
@@ -674,7 +674,12 @@
             pltpu.VMEM((2, SUB, LANES), F32),
             pltpu.SemaphoreType.DMA((8,)),
         ],
-        cells, link_seg[0, 0], link_trans[0, 0], link_count[0], link_upwind[:, 0, 0], matrix_state, frac,
+        *[
+            pltpu.with_memory_space_constraint(x, pltpu.HBM)
+            for x in (
+                cells, link_seg[0, 0], link_trans[0, 0], link_count[0], link_upwind[:, 0, 0], matrix_state, frac
+            )
+        ],
         spec=HBM,
     )
     slot = to_group(sent)

time: 83.7 us -> 79.4 us (0.949)
  local copies, waits for them, and re-layouts: 4.62 us -> 0.02 us
    unnamed x20 -> x10, local copies, waits for them, and re-layouts: 4.62 us -> 0.02 us
  transfers between devices with their start and end apart: 1 -> 1, of which waited for: 1 -> 1; matrix products, arithmetic and copies ran while one was open for 0% -> 0% of each run, Pallas kernels for 1% -> 2%
where the time goes in v3:
time: 79.4 us; the launch traced here: 79 us
  blocking collectives  52.1 us (66%)
  Pallas kernels  14.2 us (18%)
  waiting for transfers between devices  9.36 us (12%)
  starting transfers between devices  2.59 us (3%)
    all_to_all x2, blocking collectives, to_all(): lax.all_to_all(x, ('grp', 'frac'), split_axis=0, concat_axis=0, tiled=True)  27.2 us
    all_to_all x3, blocking collectives, to_group(): return lax.all_to_all(x, 'frac', split_axis=0, concat_axis=0, tiled=True)  24.9 us
    pallas_call x8, Pallas kernels, call(): pl.pallas_call(functools.partial(kernel, *statics), out_shape=outs, in_sp...  14.2 us
    all_to_all x1, waiting for transfers between devices, to_all(): lax.all_to_all(x, ('grp', 'frac'), split_axis=0, concat_axis=0, tiled=True)  9.36 us
    all_to_all x1, starting transfers between devices, to_all(): lax.all_to_all(x, ('grp', 'frac'), split_axis=0, concat_axis=0, tiled=True)  2.59 us
  transfers between devices with their start and end apart: 1, of which 1 were waited for; matrix products, arithmetic and copies ran while one was open for 0% of the time, Pallas kernels for 2%

profile of v3, /device:TPU:0, one launch (start us, length us, event | category | flops | bytes accessed | tf_op | source)
XLA Modules:
  0.0 79.0 jit_solution(9665349651316471141)
XLA Ops:
  0.6 0.0 copy-start.2
  0.6 0.0 copy-start.3
  0.7 1.9 %first_kernel.1 = (f32[8,8,256]{2,1,0:T(8,128)S(1)}, bf16[256,2048]{1,0:T(8,128)(2,1)S(1)}, bf16[128,2048]{1,0:T(8,128)(2,1)S(1)}) custom-call(s32[8,256]{1,0:T(8,128)} %bitcast.13, s32[8,256]{1,0:T(8,128)} %bitcast.18, f32[8,256]{1,0:T(8,128)} %bitcast.19, s32[1,8]{1,0:T(1,128)} %bitcast.20, s32[3,8,256]{2,1,0:T(8,128)} %bitcast.17, ...), custom_call_target="tpu_custom_call" | custom-call | tf_op jit(solution)/shard_map/first_kernel/pallas_call | solution.py:614
  2.6 0.0 copy-start.1
  2.6 10.1 %all_to_all.30.slot_ref = f32[8,8,256]{2,1,0:T(8,128)S(1)} all-to-all(f32[8,8,256]{2,1,0:T(8,128)S(1)} %get-tuple-element.20.sent_ref), channel_id=1, replica_groups=mesh['grp'=4,'frac'=8] {'frac'}, dimensions={0} | all-to-all | bytes 131072 | tf_op jit(solution)/shard_map/all_to_all | solution.py:655
  12.7 0.0 copy-done.2
  12.7 0.0 copy-done.3
  12.8 1.8 %owner_start_kernel.1 = (f32[8,8,256]{2,1,0:T(8,128)S(1)}, f32[2,64,128]{2,1,0:T(8,128)S(1)}, bf16[128,2048]{1,0:T(8,128)(2,1)S(1)}, bf16[64,2048]{1,0:T(8,128)(2,1)S(1)}) custom-call(f32[8,8,256]{2,1,0:T(8,128)S(1)} %all_to_all.30.slot_ref, f32[2,64,128]{2,1,0:T(8,128)S(1)} %bitcast.12, f32[64,128]{1,0:T(8,128)S(1)} %bitcast.8), custom_call_target="tpu_custom_call" | custom-call | tf_op jit(solution)/shard_map/owner_start_kernel/pallas_call | solution.py:614
  14.6 7.4 %all_to_all.31.seg_ref.ends_ref = f32[8,8,256]{2,1,0:T(8,128)S(1)} all-to-all(f32[8,8,256]{2,1,0:T(8,128)S(1)} %get-tuple-element.21.own_ref), channel_id=1, replica_groups=mesh['grp'=4,'frac'=8] {'frac'}, dimensions={0} | all-to-all | bytes 131072 | tf_op jit(solution)/shard_map/all_to_all | solution.py:655
  22.0 0.0 copy-done.1
  22.0 0.0 copy-done
  22.0 1.1 %source_start_kernel.1 = (f32[32,8,256]{2,1,0:T(8,128)S(1)}, f32[4,128,256]{2,1,0:T(8,128)S(1)}) custom-call(bf16[256,2048]{1,0:T(8,128)(2,1)S(1)} %get-tuple-element.18.hot_ref.cell_hot_ref, bf16[128,2048]{1,0:T(8,128)(2,1)S(1)} %get-tuple-element.19.row_hot_ref, f32[8,8,256]{2,1,0:T(8,128)S(1)} %get-tuple-element.20.sent_ref, ...), custom_call_target="tpu_custom_call" | custom-call | tf_op jit(solution)/shard_map/source_start_kernel/pallas_call | solution.py:614
  23.1 0.0 copy-start.4
  23.1 14.4 %all_to_all.32.halo_ref = f32[32,8,256]{2,1,0:T(8,128)S(1)} all-to-all(f32[32,8,256]{2,1,0:T(8,128)S(1)} %get-tuple-element.22), channel_id=1, replica_groups=mesh['grp'=4,'frac'=8] {'grp','frac'}, dimensions={0} | all-to-all | bytes 524288 | tf_op jit(solution)/shard_map/all_to_all | solution.py:658
  37.5 0.0 copy-done.4
  37.5 2.4 %middle_kernel.1 = (f32[32,8,256]{2,1,0:T(8,128)S(1)}, f32[4,128,256]{2,1,0:T(8,128)S(1)}) custom-call(f32[32,8,256]{2,1,0:T(8,128)S(1)} %all_to_all.32.halo_ref, s32[8,256]{1,0:T(8,128)S(1)} %bitcast.14, bf16[256,2048]{1,0:T(8,128)(2,1)S(1)} %get-tuple-element.18.hot_ref.cell_hot_ref, bf16[128,2048]{1,0:T(8,128)(2,1)S(1)} %get-tuple-element.19.row_hot_ref, ...), custom_call_target="tpu_custom_call" | custom-call | tf_op jit(solution)/shard_map/middle_kernel/pallas_call | solution.py:614
  39.9 12.8 %all_to_all.33.halo_ref = f32[32,8,256]{2,1,0:T(8,128)S(1)} all-to-all(f32[32,8,256]{2,1,0:T(8,128)S(1)} %get-tuple-element.24), channel_id=1, replica_groups=mesh['grp'=4,'frac'=8] {'grp','frac'}, dimensions={0} | all-to-all | bytes 524288 | tf_op jit(solution)/shard_map/all_to_all | solution.py:658
  52.7 2.4 %exchange_kernel.1 = (f32[8,8,256]{2,1,0:T(8,128)S(1)}, f32[2,64,128]{2,1,0:T(8,128)S(1)}, f32[128,256]{1,0:T(8,128)S(1)}) custom-call(f32[32,8,256]{2,1,0:T(8,128)S(1)} %all_to_all.33.halo_ref, s32[8,256]{1,0:T(8,128)S(1)} %bitcast.15, bf16[256,2048]{1,0:T(8,128)(2,1)S(1)} %get-tuple-element.18.hot_ref.cell_hot_ref, f32[8,8,256]{2,1,0:T(8,128)S(1)} %all_to_all.30.slot_ref, ...), custom_call_target="tpu_custom_call" | custom-call | tf_op jit(solution)/shard_map/exchange_kernel/pallas_call | solution.py:614
  55.1 7.4 %all_to_all.34.seg_ref = f32[8,8,256]{2,1,0:T(8,128)S(1)} all-to-all(f32[8,8,256]{2,1,0:T(8,128)S(1)} %get-tuple-element.29.own_ref), channel_id=1, replica_groups=mesh['grp'=4,'frac'=8] {'frac'}, dimensions={0} | all-to-all | bytes 131072 | tf_op jit(solution)/shard_map/all_to_all | solution.py:655
  62.5 1.8 %source_last_kernel.1 = (f32[32,8,256]{2,1,0:T(8,128)}, f32[3,128,256]{2,1,0:T(8,128)S(1)}) custom-call(bf16[256,2048]{1,0:T(8,128)(2,1)S(1)} %get-tuple-element.18.hot_ref.cell_hot_ref, bf16[128,2048]{1,0:T(8,128)(2,1)S(1)} %get-tuple-element.19.row_hot_ref, f32[8,8,256]{2,1,0:T(8,128)S(1)} %get-tuple-element.20.sent_ref, ...), custom_call_target="tpu_custom_call" | custom-call | tf_op jit(solution)/shard_map/source_last_kernel/pallas_call | solution.py:614
  64.3 2.6 %all-to-all-start.5 = ((f32[32,8,256]{2,1,0:T(8,128)}), f32[32,8,256]{2,1,0:T(8,128)S(1)}, u32[]{:S(2)}, u32[]{:S(2)}) async-start(f32[32,8,256]{2,1,0:T(8,128)} %get-tuple-element.31), calls=%async_computation.5 | async-start | bytes 524288 | tf_op jit(solution)/shard_map/all_to_all | solution.py:658
  66.9 1.2 %owner_last_kernel.1 = f32[2,64,128]{2,1,0:T(8,128)} custom-call(f32[8,8,256]{2,1,0:T(8,128)S(1)} %all_to_all.30.slot_ref, bf16[128,2048]{1,0:T(8,128)(2,1)S(1)} %get-tuple-element.25.hot_ref, bf16[64,2048]{1,0:T(8,128)(2,1)S(1)} %get-tuple-element.26.row_hot_ref, f32[8,8,256]{2,1,0:T(8,128)S(1)} %get-tuple-element.29.own_ref, ...), custom_call_target="tpu_custom_call" | custom-call | tf_op jit(solution)/shard_map/owner_last_kernel/pallas_call | solution.py:614
  68.1 9.4 %all-to-all-done.5.halo_ref = f32[32,8,256]{2,1,0:T(8,128)S(1)} async-done(((f32[32,8,256]{2,1,0:T(8,128)}), f32[32,8,256]{2,1,0:T(8,128)S(1)}, u32[]{:S(2)}, u32[]{:S(2)}) %all-to-all-start.5) | async-done | bytes 262176 | tf_op jit(solution)/shard_map/all_to_all | solution.py:658
  77.5 1.5 %final_kernel.1 = f32[2,128,256]{2,1,0:T(8,128)} custom-call(f32[32,8,256]{2,1,0:T(8,128)S(1)} %all-to-all-done.5.halo_ref, f32[128,256]{1,0:T(8,128)S(1)} %get-tuple-element.30.pressure_ref, f32[3,128,256]{2,1,0:T(8,128)S(1)} %get-tuple-element.32.kept_ref), custom_call_target="tpu_custom_call" | custom-call | tf_op jit(solution)/shard_map/final_kernel/pallas_call | solution.py:614
  (1 shorter events, 0.0 us)
Async XLA Ops:
  0.6 12.1 %copy-start.2 = (f32[1,8192]{1,0:T(1,128)S(1)}, f32[1,8192]{1,0:T(1,128)}, u32[]{:S(2)}) copy-start(f32[1,8192]{1,0:T(1,128)} %param.12) | copy-start | bytes 98308
  0.6 12.1 %copy-start.3 = (f32[2,1,8192]{2,1,0:T(1,128)S(1)}, f32[2,1,8192]{2,1,0:T(1,128)}, u32[]{:S(2)}) copy-start(f32[2,1,8192]{2,1,0:T(1,128)} %param.11) | copy-start | bytes 196612
  2.6 19.4 %copy-start.1 = (f32[2,128,256]{2,1,0:T(8,128)S(1)}, f32[2,128,256]{2,1,0:T(8,128)}, u32[]{:S(2)}) copy-start(f32[2,128,256]{2,1,0:T(8,128)} %state_ref.1) | copy-start | bytes 786436
  12.7 9.3 %copy-start = (f32[128,256]{1,0:T(8,128)S(1)}, f32[128,256]{1,0:T(8,128)}, u32[]{:S(2)}) copy-start(f32[128,256]{1,0:T(8,128)} %perm_ref.5) | copy-start | bytes 393220
  23.1 14.4 %copy-start.4 = (s32[1,1,8,256]{3,2,1,0:T(8,128)S(1)}, s32[1,1,8,256]{3,2,1,0:T(8,128)}, u32[]{:S(2)}) copy-start(s32[1,1,8,256]{3,2,1,0:T(8,128)} %param.13) | copy-start | bytes 24580
  64.3 13.2 %all-to-all-start.5 = ((f32[32,8,256]{2,1,0:T(8,128)}), f32[32,8,256]{2,1,0:T(8,128)S(1)}, u32[]{:S(2)}, u32[]{:S(2)}) async-start(f32[32,8,256]{2,1,0:T(8,128)} %get-tuple-element.31), calls=%async_computation.5 | async-start | bytes 524288 | tf_op jit(solution)/shard_map/all_to_all | solution.py:658

commit v4 on v3

--- a/solution.py
+++ b/solution.py
@@ -144,60 +144,109 @@
     )
 
 
-def send_halo(out_ref, q, inv, p, groups, members):
+def block_rows(columns, width):
+    vertical = 2 * DEPTH * (columns // LANES) + 1
+    lateral = SUB + 2 * (width // LANES) + 1
+    return max(vertical, lateral)
+
+
+def put_rows(out_ref, at, values):
+    for k in range(values.shape[0]):
+        out_ref[at + k] = values[k : k + 1]
+
+
+def get_rows(in_ref, at, count):
+    return jnp.concatenate([in_ref[at + k] for k in range(count)], axis=0)
+
+
+def send_slots(out_ref, at, first, second):
+    halves = first.shape[1] // LANES
+    for i, value in enumerate((first, second)):
+        for h in range(halves):
+            out_ref[at + SUB + i * halves + h] = value[:, h * LANES : (h + 1) * LANES]
+
+
+def got_slots(in_ref, at, width):
+    halves = width // LANES
+    return [
+        jnp.concatenate([in_ref[at + SUB + i * halves + h] for h in range(halves)], axis=1) for i in range(2)
+    ]
+
+
+def send_halo(out_ref, q, inv, p, groups, members, size):
     rows, columns = q.shape
+    halves = columns // LANES
     g, f = lax.axis_index("grp"), lax.axis_index("frac")
     here = g * members + f
-    sub = iota((SUB, columns), 0)
-    top = pack_low(q[:SUB], inv[:SUB], p[:SUB], sub, 0)
-    bottom = pack_high(q[rows - SUB :], inv[rows - SUB :], p[rows - SUB :], sub, 0)
     lane = iota((rows, LANES), 1)
     low = pack_low(q[:, :LANES], inv[:, :LANES], p[:, :LANES], lane, 1)
     high = pack_high(q[:, columns - LANES :], inv[:, columns - LANES :], p[:, columns - LANES :], lane, 1)
     turned = jnp.transpose(jnp.where(lane < LANES // 2, low, high))
     left, right = turned[:SUB], turned[LANES - SUB :]
-    p_top, p_bottom = p[:SUB], p[rows - SUB :]
-
-    for step, strip, p_strip in ((-1, top, p_top), (1, bottom, p_bottom)):
+    lane = iota((1, LANES), 1)
+
+    for step in (-1, 1):
+        layer = (lambda k: k) if step < 0 else (lambda k: rows - 1 - k)
+
+        def span(field, count, at):
+            start = 0 if step < 0 else rows - count
+            return field[start : start + count, at]
+
         inside = (g + step >= 0) & (g + step < groups)
         base = here + step * members
+        tiles = [slice(h * LANES, (h + 1) * LANES) for h in range(halves)]
 
         @pl.when(inside)
         def _():
-            out_ref[base] = strip
-
-        @pl.when(inside & (f > 0))
-        def _():
-            out_ref[base - 1, :, 0:LANES] = strip[:, :LANES]
-            out_ref[base - 1, :, LANES : 2 * LANES] = p_strip[:, :LANES]
-
-        @pl.when(inside & (f < members - 1))
-        def _():
-            out_ref[base + 1, :, 0:LANES] = strip[:, columns - LANES :]
-            out_ref[base + 1, :, LANES : 2 * LANES] = p_strip[:, columns - LANES :]
+            at = base * size
+            for h, tile in enumerate(tiles):
+                put_rows(out_ref, at + h * DEPTH, span(q, DEPTH, tile))
+                put_rows(out_ref, at + halves * DEPTH + h * (DEPTH - 1), span(inv, DEPTH - 1, tile))
+                put_rows(out_ref, at + halves * (2 * DEPTH - 1) + h, span(p, 1, tile))
+            deep, next_p = layer(DEPTH - 1), layer(1)
+            extra = jnp.where(
+                lane == 0,
+                inv[deep : deep + 1, tiles[0]],
+                jnp.where(
+                    lane == LANES - 1,
+                    inv[deep : deep + 1, tiles[-1]],
+                    jnp.where(
+                        lane == 1,
+                        pltpu.roll(p[next_p : next_p + 1, tiles[0]], 1, 1),
+                        pltpu.roll(p[next_p : next_p + 1, tiles[-1]], LANES - 1, 1),
+                    ),
+                ),
+            )
+            out_ref[at + halves * 2 * DEPTH] = extra
+
+        for side, tile, there in ((-1, tiles[0], f > 0), (1, tiles[-1], f < members - 1)):
+
+            @pl.when(inside & there)
+            def _(side=side, tile=tile):
+                at = (base + side) * size
+                for i, field in enumerate((q, inv, p)):
+                    put_rows(out_ref, at + i * DEPTH, span(field, DEPTH, tile))
 
     @pl.when(f > 0)
     def _():
-        out_ref[here - 1, :, 0:LANES] = left
+        put_rows(out_ref, (here - 1) * size, left)
 
     @pl.when(f < members - 1)
     def _():
-        out_ref[here + 1, :, 0:LANES] = right
-
-
-def chebyshev(in_ref, q, inv, p, q_ext, inv_ext, p_ext, groups, members):
+        put_rows(out_ref, (here + 1) * size, right)
+
+
+def chebyshev(in_ref, q, inv, p, q_ext, inv_ext, p_ext, groups, members, size):
     rows, columns = q.shape
+    halves = columns // LANES
     g, f = lax.axis_index("grp"), lax.axis_index("frac")
     here = g * members + f
     last = groups * members - 1
 
-    def block(dg, df):
+    def taker(dg, df):
         ok = (g + dg >= 0) & (g + dg < groups) & (f + df >= 0) & (f + df < members)
-        at = jnp.clip(here + dg * members + df, 0, last)
-        return jnp.where(ok, in_ref[at], 0.0)
-
-    sub = iota((SUB, columns), 0)
-    below, above = block(1, 0), block(-1, 0)
+        at = jnp.clip(here + dg * members + df, 0, last) * size
+        return lambda start, count: jnp.where(ok, get_rows(in_ref, at + start, count), 0.0)
 
     def both(low, high, at, count, size):
         return jnp.where(at < count, low, jnp.where(at >= size - count, high, 0.0))
@@ -205,14 +254,48 @@
     q_ext[0:rows, 0:columns] = q
     inv_ext[0:rows, 0:columns] = inv
     p_ext[0:rows, 0:columns] = p
-    q_ext[rows : rows + SUB, 0:columns] = both(below, above, sub, DEPTH, SUB)
-    inv_ext[rows : rows + SUB, 0:columns] = both(
-        pltpu.roll(below, SUB - DEPTH, 0), pltpu.roll(above, DEPTH, 0), sub, DEPTH, SUB
-    )
-    p_ext[rows : rows + SUB, 0:columns] = both(
-        pltpu.roll(below, SUB - 2 * DEPTH, 0), pltpu.roll(above, 2 * DEPTH, 0), sub, 2, SUB
-    )
-    right, left = block(0, 1)[:, :LANES], block(0, -1)[:, :LANES]
+    below, above = taker(1, 0), taker(-1, 0)
+    lane = iota((1, LANES), 1)
+    low_extra, high_extra = below(halves * 2 * DEPTH, 1), above(halves * 2 * DEPTH, 1)
+
+    def filler(count):
+        return jnp.zeros((count, LANES), F32)
+
+    for h in range(halves):
+        tile = slice(h * LANES, (h + 1) * LANES)
+        edge = (lane == 0) & (h == 0) | (lane == LANES - 1) & (h == halves - 1)
+
+        def at_edge(row, turn):
+            return jnp.where(edge, pltpu.roll(row, turn, 1) if turn else row, 0.0)
+
+        turn = LANES - 1 if h == 0 else 1
+        at = h * DEPTH
+        q_ext[rows : rows + SUB, tile] = jnp.concatenate(
+            [below(at, DEPTH), filler(SUB - 2 * DEPTH), above(at, DEPTH)], axis=0
+        )
+        at = halves * DEPTH + h * (DEPTH - 1)
+        inv_ext[rows : rows + SUB, tile] = jnp.concatenate(
+            [
+                below(at, DEPTH - 1),
+                at_edge(low_extra, 0),
+                filler(SUB - 2 * DEPTH),
+                at_edge(high_extra, 0),
+                above(at, DEPTH - 1),
+            ],
+            axis=0,
+        )
+        at = halves * (2 * DEPTH - 1) + h
+        p_ext[rows : rows + SUB, tile] = jnp.concatenate(
+            [
+                below(at, 1),
+                at_edge(low_extra, turn),
+                filler(SUB - 4),
+                at_edge(high_extra, turn),
+                above(at, 1),
+            ],
+            axis=0,
+        )
+    right, left = taker(0, 1)(0, SUB), taker(0, -1)(0, SUB)
     turned = jnp.transpose(
         jnp.concatenate([right, jnp.zeros((LANES - 2 * SUB, rows), F32), left], axis=0)
     )
@@ -225,18 +308,19 @@
     p_ext[0:rows, side] = both(
         pltpu.roll(turned, LANES - 2 * DEPTH, 1), pltpu.roll(turned, 2 * DEPTH, 1), lane, 2, LANES
     )
-    sub = iota((SUB, LANES), 0)
-    lane = iota((SUB, LANES), 1)
-    low_right, low_left = block(1, 1), block(1, -1)
-    high_right, high_left = block(-1, 1), block(-1, -1)
-    low = both(low_right, low_left, iota((SUB, 2 * LANES), 1) % LANES, DEPTH, LANES)
-    high = both(high_right, high_left, iota((SUB, 2 * LANES), 1) % LANES, DEPTH, LANES)
+    lane = iota((DEPTH, LANES), 1)
     corner = slice(rows, rows + SUB)
-    q_ext[corner, side] = both(low[:, :LANES], high[:, :LANES], sub, DEPTH, SUB)
-    inv_ext[corner, side] = both(
-        pltpu.roll(low[:, :LANES], SUB - DEPTH, 0), pltpu.roll(high[:, :LANES], DEPTH, 0), sub, DEPTH, SUB
-    )
-    p_ext[corner, side] = both(low[:, LANES:], high[:, LANES:], sub, DEPTH, SUB)
+    low_right, low_left, high_right, high_left = taker(1, 1), taker(1, -1), taker(-1, 1), taker(-1, -1)
+    for i, ext in enumerate((q_ext, inv_ext, p_ext)):
+        at = i * DEPTH
+        ext[corner, side] = jnp.concatenate(
+            [
+                both(low_right(at, DEPTH), low_left(at, DEPTH), lane, DEPTH, LANES),
+                filler(SUB - 2 * DEPTH),
+                both(high_right(at, DEPTH), high_left(at, DEPTH), lane, DEPTH, LANES),
+            ],
+            axis=0,
+        )
 
     shape = (rows + SUB, columns + LANES)
     for here_row, there_row in ((0, shape[0] - 1), (shape[0] - 1, 0), (rows - 1, rows), (rows, rows - 1)):
@@ -288,11 +372,11 @@
 
 def first_kernel(
     members, cell_any, seg_any, trans_any, count_any, up_any, state_any, frac_any,
-    out_ref, hot_ref, row_hot_ref, cell_ref, seg_ref, trans_ref, count_ref, up_ref, state_ref, ends_ref, sem,
+    out_ref, hot_ref, row_hot_ref, cell_ref, seg_ref, trans_ref, count_ref, up_ref, state_ref, frac_ref, sem,
 ):
     _, rows, columns = state_ref.shape
     width = cell_ref.shape[1]
-    seg_rows = frac_any.shape[1]
+    seg_rows = frac_ref.shape[1]
     copies = [
         pltpu.make_async_copy(source, target, sem.at[i])
         for i, (source, target) in enumerate(
@@ -303,8 +387,7 @@
                 (trans_any, trans_ref),
                 (count_any, count_ref),
                 (up_any, up_ref),
-                (frac_any.at[0, 0:SUB], ends_ref.at[0]),
-                (frac_any.at[0, seg_rows - SUB : seg_rows], ends_ref.at[1]),
+                (frac_any, frac_ref),
             ]
         )
     ]
@@ -320,7 +403,8 @@
     table = table_of([state_ref[0], state_ref[1]])
     for copy in copies[2:]:
         copy.wait()
-    ends = jnp.concatenate([ends_ref[0, 0:1], ends_ref[1, SUB - 1 : SUB]], axis=1)
+    ends = ends_of(frac_ref[0])
+    whole = jnp.concatenate([frac_ref[0], frac_ref[1]], axis=1)
     for o in range(members):
         one = slice(o, o + 1)
         row, _ = cell_parts(cell_ref[one, :], columns)
@@ -333,6 +417,7 @@
         out_ref[o, ROW_P : ROW_P + 1, :] = cell_p
         out_ref[o, ROW_S : ROW_S + 1, :] = cell_s
         out_ref[o, ROW_ENDS : ROW_ENDS + 1, :] = ends
+        out_ref[o, SUB : SUB + seg_rows, :] = whole
 
 
 def seg_parts(slot_ref, s):
@@ -350,43 +435,6 @@
 
 def seg_gather(slot_ref, hot_ref, fields, s, width, table):
     return pick(table, 2, fields, seg_parts(slot_ref, s)[0], hot_ref[:, s * width : (s + 1) * width])
-
-
-def owner_start_kernel(
-    members, slot_ref, frac_ref, aperture_ref, out_ref, new_ref, hot_ref, row_hot_ref, left_ref
-):
-    width = slot_ref.shape[2]
-    rows = frac_ref.shape[1]
-    frac, sat = frac_ref[0], frac_ref[1]
-    seg_hots(slot_ref, hot_ref, row_hot_ref, members, width)
-    table = table_of([frac, sat])
-    for s in range(members):
-        seg_p, seg_s = seg_gather(slot_ref, hot_ref, rows, s, width, table)
-        out_ref[s, 0:1, :] = seg_p
-        out_ref[s, 1:2, :] = seg_s
-        slot = slot_ref[s]
-        cell_p = slot[ROW_P : ROW_P + 1]
-        weight, water = flow(
-            slot[ROW_TRANS : ROW_TRANS + 1],
-            slot[ROW_UP : ROW_UP + 1],
-            cell_p,
-            slot[ROW_S : ROW_S + 1],
-            seg_p,
-            seg_s,
-        )
-        spread(left_ref, row_hot_ref, s, [weight * cell_p, weight, water])
-    inflow, total, gained = gathered_sum(left_ref, hot_ref, 3, rows)
-    before, after = chain_ends(slot_ref, ROW_ENDS, members)
-    new_frac, new_sat = frac_step(frac, sat, aperture_ref[...], before, after, inflow, total, gained)
-    new_ref[0] = new_frac
-    new_ref[1] = new_sat
-    table = table_of([new_frac, new_sat])
-    ends = ends_of(new_frac)
-    for s in range(members):
-        seg_p, seg_s = seg_gather(slot_ref, hot_ref, rows, s, width, table)
-        out_ref[s, 2:3, :] = seg_p
-        out_ref[s, 3:4, :] = seg_s
-        out_ref[s, 4:5, :] = ends
 
 
 def cell_update(
@@ -411,18 +459,59 @@
     return new_saturation, partial_residual(pressure, couple, source, inverse), inverse
 
 
-def source_start_kernel(
-    groups, members, hot_ref, row_hot_ref, sent_ref, seg_ref, state_ref, perm_ref, out_ref, keep_ref, left_ref
+def start_kernel(
+    groups, members, size, slot_ref, sent_ref, cell_hot_ref, cell_row_hot_ref, frac_ref, aperture_ref,
+    state_ref, perm_ref, out_ref, keep_ref, own_ref, new_ref, hot_ref, row_hot_ref,
+    left_seg_ref, left_ref, found_ref,
 ):
+    width = slot_ref.shape[2]
+    rows = frac_ref.shape[1]
+    g = lax.axis_index("grp")
+    frac, sat = frac_ref[0], frac_ref[1]
+    seg_hots(slot_ref, hot_ref, row_hot_ref, members, width)
+    table = table_of([frac, sat])
+    for s in range(members):
+        seg_p, seg_s = seg_gather(slot_ref, hot_ref, rows, s, width, table)
+        cell_p = slot_ref[s, ROW_P : ROW_P + 1, :]
+        weight, water = flow(
+            slot_ref[s, ROW_TRANS : ROW_TRANS + 1, :],
+            slot_ref[s, ROW_UP : ROW_UP + 1, :],
+            cell_p,
+            slot_ref[s, ROW_S : ROW_S + 1, :],
+            seg_p,
+            seg_s,
+        )
+        spread(left_seg_ref, row_hot_ref, s, [weight * cell_p, weight, water])
+    inflow, total, gained = gathered_sum(left_seg_ref, hot_ref, 3, rows)
+    before, after = chain_ends(slot_ref, ROW_ENDS, members)
+    new_frac, new_sat = frac_step(frac, sat, aperture_ref[...], before, after, inflow, total, gained)
+    new_ref[0] = new_frac
+    new_ref[1] = new_sat
+    table = table_of([new_frac, new_sat])
+    lane = iota((1, LANES), 1)
+    ends = jnp.where(lane < LANES // 2, new_frac[0:1], new_frac[rows - 1 : rows])
+    for s in range(members):
+        seg_p, seg_s = seg_gather(slot_ref, hot_ref, rows, s, width, table)
+        own_ref[s, 0:1, :] = seg_p
+        own_ref[s, 1:2, :] = seg_s
+        at = (g * members + s) * size
+        send_slots(out_ref, at, seg_p, seg_s)
+        out_ref[at + size - 1] = ends
+    for o in range(members):
+        row, lane = seg_parts(sent_ref, o)
+        table = table_of([slot_ref[o, SUB : SUB + rows, 0:LANES], slot_ref[o, SUB : SUB + rows, LANES : 2 * LANES]])
+        seg_p, seg_s = pick(table, 2, rows, row, one_hot(lane, LANES))
+        found_ref[o, 0:1, :] = seg_p
+        found_ref[o, 1:2, :] = seg_s
     pressure = state_ref[0]
     new_saturation, q, inv = cell_update(
         members,
         0,
-        hot_ref,
-        row_hot_ref,
+        cell_hot_ref,
+        cell_row_hot_ref,
         sent_ref,
         lambda o: (sent_ref[o, ROW_P : ROW_P + 1, :], sent_ref[o, ROW_S : ROW_S + 1, :]),
-        lambda o: (seg_ref[o, 0:1, :], seg_ref[o, 1:2, :]),
+        lambda o: (found_ref[o, 0:1, :], found_ref[o, 1:2, :]),
         pressure,
         state_ref[1],
         perm_ref[...],
@@ -432,7 +521,7 @@
     keep_ref[1] = new_saturation
     keep_ref[2] = q
     keep_ref[3] = inv
-    send_halo(out_ref, q, inv, pressure, groups, members)
+    send_halo(out_ref, q, inv, pressure, groups, members, size)
 
 
 def cell_gather(members, cell_ref, hot_ref, fields, put):
@@ -445,11 +534,11 @@
 
 
 def middle_kernel(
-    groups, members, halo_ref, cell_ref, hot_ref, row_hot_ref, sent_ref, seg_ref, kept_ref, perm_ref,
+    groups, members, size, halo_ref, cell_ref, hot_ref, row_hot_ref, sent_ref, kept_ref, perm_ref,
     out_ref, keep_ref, slots_ref, left_ref, q_ext, inv_ext, p_ext,
 ):
     pressure = chebyshev(
-        halo_ref, kept_ref[2], kept_ref[3], kept_ref[0], q_ext, inv_ext, p_ext, groups, members
+        halo_ref, kept_ref[2], kept_ref[3], kept_ref[0], q_ext, inv_ext, p_ext, groups, members, size
     )
     saturation = kept_ref[1]
     g = lax.axis_index("grp")
@@ -457,10 +546,7 @@
     def put(o, cell_p, cell_s):
         slots_ref[o, 0:1, :] = cell_p
         slots_ref[o, 1:2, :] = cell_s
-        for half in range(2):
-            at = slice(half * LANES, (half + 1) * LANES)
-            out_ref[g * members + o, half : half + 1, LANES : 2 * LANES] = cell_p[:, at]
-            out_ref[g * members + o, 2 + half : 3 + half, LANES : 2 * LANES] = cell_s[:, at]
+        send_slots(out_ref, (g * members + o) * size, cell_p, cell_s)
 
     cell_gather(members, cell_ref, hot_ref, [pressure, saturation], put)
     new_saturation, q, inv = cell_update(
@@ -470,7 +556,7 @@
         row_hot_ref,
         sent_ref,
         lambda o: (slots_ref[o, 0:1, :], slots_ref[o, 1:2, :]),
-        lambda o: (seg_ref[o, 2:3, :], seg_ref[o, 3:4, :]),
+        lambda o: got_slots(halo_ref, (g * members + o) * size, cell_ref.shape[1]),
         pressure,
         saturation,
         perm_ref[...],
@@ -480,7 +566,7 @@
     keep_ref[1] = new_saturation
     keep_ref[2] = q
     keep_ref[3] = inv
-    send_halo(out_ref, q, inv, pressure, groups, members)
+    send_halo(out_ref, q, inv, pressure, groups, members, size)
 
 
 def owner_update(
@@ -502,7 +588,7 @@
 
 
 def exchange_kernel(
-    groups, members, halo_ref, cell_ref, cell_hot_ref, slot_ref, hot_ref, row_hot_ref, ends_ref, own_ref,
+    groups, members, size, halo_ref, cell_ref, cell_hot_ref, slot_ref, hot_ref, row_hot_ref, ends_ref, own_ref,
     frac_ref, aperture_ref, kept_ref, out_ref, new_ref, pressure_ref, left_ref, q_ext, inv_ext, p_ext,
 ):
     width = slot_ref.shape[2]
@@ -510,23 +596,24 @@
     g = lax.axis_index("grp")
 
     def cell_rows(s):
-        block = halo_ref[g * members + s]
-        half = block[:, LANES : 2 * LANES]
-        return (
-            jnp.concatenate([half[0:1], half[1:2]], axis=1),
-            jnp.concatenate([half[2:3], half[3:4]], axis=1),
-        )
+        return got_slots(halo_ref, (g * members + s) * size, width)
+
+    me = lax.axis_index("frac")
+    prior = ends_ref[(g * members + jnp.maximum(me - 1, 0)) * size + size - 1]
+    later = ends_ref[(g * members + jnp.minimum(me + 1, members - 1)) * size + size - 1]
+    before = jnp.where(me > 0, prior[:, LANES - 1 :], 0.0)
+    after = jnp.where(me < members - 1, later[:, 0:1], 0.0)
 
     new_frac, new_sat = owner_update(
         members,
         1,
         slot_ref,
         cell_rows,
-        lambda s: (own_ref[s, 2:3, :], own_ref[s, 3:4, :]),
+        lambda s: (own_ref[s, 0:1, :], own_ref[s, 1:2, :]),
         frac_ref[0],
         frac_ref[1],
         aperture_ref[...],
-        chain_ends(ends_ref, 4, members),
+        (before, after),
         hot_ref,
         row_hot_ref,
         left_ref,
@@ -542,7 +629,7 @@
         out_ref[s, 4:5, :] = ends
 
     pressure = chebyshev(
-        halo_ref, kept_ref[2], kept_ref[3], kept_ref[0], q_ext, inv_ext, p_ext, groups, members
+        halo_ref, kept_ref[2], kept_ref[3], kept_ref[0], q_ext, inv_ext, p_ext, groups, members, size
     )
     pressure_ref[...] = pressure
 
@@ -554,7 +641,7 @@
 
 
 def source_last_kernel(
-    groups, members, hot_ref, row_hot_ref, sent_ref, own_ref, seg_ref, pressure_ref, kept_ref, perm_ref,
+    groups, members, size, hot_ref, row_hot_ref, sent_ref, own_ref, seg_ref, pressure_ref, kept_ref, perm_ref,
     out_ref, keep_ref, left_ref,
 ):
     pressure = pressure_ref[...]
@@ -574,7 +661,7 @@
     keep_ref[0] = new_saturation
     keep_ref[1] = q
     keep_ref[2] = inv
-    send_halo(out_ref, q, inv, pressure, groups, members)
+    send_halo(out_ref, q, inv, pressure, groups, members, size)
 
 
 def owner_last_kernel(
@@ -598,9 +685,9 @@
     out_ref[1] = new_sat
 
 
-def final_kernel(groups, members, halo_ref, pressure_ref, kept_ref, out_ref, q_ext, inv_ext, p_ext):
+def final_kernel(groups, members, size, halo_ref, pressure_ref, kept_ref, out_ref, q_ext, inv_ext, p_ext):
     out_ref[0] = chebyshev(
-        halo_ref, kept_ref[1], kept_ref[2], pressure_ref[...], q_ext, inv_ext, p_ext, groups, members
+        halo_ref, kept_ref[1], kept_ref[2], pressure_ref[...], q_ext, inv_ext, p_ext, groups, members, size
     )
     out_ref[1] = kept_ref[0]
 
@@ -634,7 +721,6 @@
     link_upwind,
 ):
     groups, members = lax.axis_size("grp"), lax.axis_size("frac")
-    both = (groups, members)
     devices = groups * members
     cells = link_cell[0, 0]
     width = cells.shape[1]
@@ -646,7 +732,9 @@
 
     every = members * width
     slots = (members, SUB, width)
-    halo = (devices, SUB, columns)
+    size = block_rows(columns, width)
+    both = (groups, members, size)
+    halo = (devices * size, 1, LANES)
     left_cell = pltpu.VMEM((3 * PARTS * rows, every), BF16)
     left_seg = pltpu.VMEM((3 * PARTS * seg_rows, every), BF16)
     ext = [pltpu.VMEM((rows + SUB, columns + LANES), F32)] * 3
@@ -663,7 +751,7 @@
     sent, cell_hot, cell_row_hot = call(
         first_kernel,
         (members,),
-        [slots] + hots(columns, rows),
+        [(members, SUB + seg_rows, width)] + hots(columns, rows),
         [
             pltpu.VMEM((members, width), jnp.int32),
             pltpu.VMEM((members, width), jnp.int32),
@@ -671,8 +759,8 @@
             pltpu.SMEM((1, members), jnp.int32),
             pltpu.VMEM((ITERS, members, width), jnp.int32),
             pltpu.VMEM(matrix_state.shape, F32),
-            pltpu.VMEM((2, SUB, LANES), F32),
-            pltpu.SemaphoreType.DMA((8,)),
+            pltpu.VMEM(frac.shape, F32),
+            pltpu.SemaphoreType.DMA((7,)),
         ],
         *[
             pltpu.with_memory_space_constraint(x, pltpu.HBM)
@@ -683,24 +771,22 @@
         spec=HBM,
     )
     slot = to_group(sent)
-    own, frac1, hot, row_hot = call(
-        owner_start_kernel, (members,), [slots, frac.shape] + hots(LANES, seg_rows), [left_seg],
-        slot, frac, aperture,
-    )
-    segs = to_group(own)
+    edge, kept, own, frac1, hot, row_hot = call(
+        start_kernel,
+        both,
+        [halo, (4, rows, columns), (members, 2, width), frac.shape] + hots(LANES, seg_rows),
+        [left_seg, left_cell, pltpu.VMEM((members, 2, width), F32)],
+        slot, sent, cell_hot, cell_row_hot, frac, aperture, matrix_state, matrix_perm,
+    )
+    before = to_all(edge)
     edge, kept = call(
-        source_start_kernel, both, [halo, (4, rows, columns)], [left_cell],
-        cell_hot, cell_row_hot, sent, segs, matrix_state, matrix_perm,
-    )
-    around = to_all(edge)
-    edge, kept = call(
-        middle_kernel, both, [halo, (4, rows, columns)], [pltpu.VMEM(slots, F32), left_cell] + ext,
-        around, cells, cell_hot, cell_row_hot, sent, segs, kept, matrix_perm,
+        middle_kernel, both, [halo, (4, rows, columns)], [pltpu.VMEM((members, 2, width), F32), left_cell] + ext,
+        before, cells, cell_hot, cell_row_hot, sent, kept, matrix_perm,
     )
     around = to_all(edge)
     own, frac2, pressure = call(
         exchange_kernel, both, [slots, frac.shape, (rows, columns)], [left_seg] + ext,
-        around, cells, cell_hot, slot, hot, row_hot, segs, own, frac1, aperture, kept,
+        around, cells, cell_hot, slot, hot, row_hot, before, own, frac1, aperture, kept,
     )
     segs = to_group(own)
     edge, kept = call(

time: 79.4 us -> 74.4 us (0.937)
  blocking collectives: 52.1 us -> 47.8 us
  waiting for transfers between devices: 9.36 us -> 8.2 us
    all_to_all x2, blocking collectives: 27.2 us -> 24.9 us  [to_all(): lax.all_to_all(x, ('grp', 'frac'), split_axis=0, concat_axis=0, tiled=True)]
    all_to_all x3 -> x2, blocking collectives: 24.9 us -> 22.9 us  [to_group(): return lax.all_to_all(x, 'frac', split_axis=0, concat_axis=0, tiled=True)]
    all_to_all x1, waiting for transfers between devices: 9.36 us -> 8.2 us  [to_all(): lax.all_to_all(x, ('grp', 'frac'), split_axis=0, concat_axis=0, tiled=True)]
    pallas_call x8 -> x7, Pallas kernels: 14.2 us -> 14.7 us  [call(): pl.pallas_call(functools.partial(kernel, *statics), out_shape=outs, in_sp...]
where the time goes in v4:
time: 74.4 us; the launch traced here: 74.1 us
  blocking collectives  47.8 us (64%)
  Pallas kernels  14.7 us (20%)
  waiting for transfers between devices  8.2 us (11%)
  starting transfers between devices  2.58 us (3%)
    all_to_all x2, blocking collectives, to_all(): lax.all_to_all(x, ('grp', 'frac'), split_axis=0, concat_axis=0, tiled=True)  24.9 us
    all_to_all x2, blocking collectives, to_group(): return lax.all_to_all(x, 'frac', split_axis=0, concat_axis=0, tiled=True)  22.9 us
    pallas_call x7, Pallas kernels, call(): pl.pallas_call(functools.partial(kernel, *statics), out_shape=outs, in_sp...  14.7 us
    all_to_all x1, waiting for transfers between devices, to_all(): lax.all_to_all(x, ('grp', 'frac'), split_axis=0, concat_axis=0, tiled=True)  8.2 us
    all_to_all x1, starting transfers between devices, to_all(): lax.all_to_all(x, ('grp', 'frac'), split_axis=0, concat_axis=0, tiled=True)  2.58 us
  transfers between devices with their start and end apart: 1, of which 1 were waited for; matrix products, arithmetic and copies ran while one was open for 0% of the time, Pallas kernels for 2%

profile of v4, /device:TPU:0, one launch (start us, length us, event | category | flops | bytes accessed | tf_op | source)
XLA Modules:
  0.0 74.1 jit_solution(6626354939177288128)
XLA Ops:
  0.6 1.9 %first_kernel.1 = (f32[8,72,256]{2,1,0:T(8,128)S(1)}, bf16[256,2048]{1,0:T(8,128)(2,1)S(1)}, bf16[128,2048]{1,0:T(8,128)(2,1)S(1)}) custom-call(s32[8,256]{1,0:T(8,128)} %bitcast.13, s32[8,256]{1,0:T(8,128)} %bitcast.18, f32[8,256]{1,0:T(8,128)} %bitcast.19, s32[1,8]{1,0:T(1,128)} %bitcast.20, s32[3,8,256]{2,1,0:T(8,128)} %bitcast.17, ...), custom_call_target="tpu_custom_call" | custom-call | tf_op jit(solution)/shard_map/first_kernel/pallas_call | solution.py:701
  2.5 0.0 copy-start
  2.5 0.0 copy-start.1
  2.6 0.0 copy-start.2
  2.6 0.0 copy-start.3
  2.6 15.5 %all_to_all.25.slot_ref = f32[8,72,256]{2,1,0:T(8,128)S(1)} all-to-all(f32[8,72,256]{2,1,0:T(8,128)S(1)} %get-tuple-element.20.sent_ref), channel_id=1, replica_groups=mesh['grp'=4,'frac'=8] {'frac'}, dimensions={0} | all-to-all | bytes 1179648 | tf_op jit(solution)/shard_map/all_to_all | solution.py:743
  18.1 0.0 copy-done
  18.1 0.0 copy-done.1
  18.1 0.0 copy-done.2
  18.1 0.0 copy-done.3
  18.1 3.3 %start_kernel.1 = (f32[416,1,128]{2,1,0:T(1,128)S(1)}, f32[4,128,256]{2,1,0:T(8,128)S(1)}, f32[8,2,256]{2,1,0:T(2,128)S(1)}, f32[2,64,128]{2,1,0:T(8,128)S(1)}, ...) custom-call(f32[8,72,256]{2,1,0:T(8,128)S(1)} %all_to_all.25.slot_ref, ...), custom_call_target="tpu_custom_call" | custom-call | tf_op jit(solution)/shard_map/start_kernel/pallas_call | solution.py:701
  21.5 0.0 copy-start.4
  21.5 13.2 %all_to_all.26.halo_ref.ends_ref = f32[416,1,128]{2,1,0:T(1,128)S(1)} all-to-all(f32[416,1,128]{2,1,0:T(1,128)S(1)} %get-tuple-element.21), channel_id=1, replica_groups=mesh['grp'=4,'frac'=8] {'grp','frac'}, dimensions={0} | all-to-all | bytes 425984 | tf_op jit(solution)/shard_map/all_to_all | solution.py:746
  34.7 0.0 copy-done.4
  34.7 2.4 %middle_kernel.1 = (f32[416,1,128]{2,1,0:T(1,128)S(1)}, f32[4,128,256]{2,1,0:T(8,128)S(1)}) custom-call(f32[416,1,128]{2,1,0:T(1,128)S(1)} %all_to_all.26.halo_ref.ends_ref, s32[8,256]{1,0:T(8,128)S(1)} %bitcast.14, bf16[256,2048]{1,0:T(8,128)(2,1)S(1)} %get-tuple-element.18.cell_hot_ref.hot_ref, ...), custom_call_target="tpu_custom_call" | custom-call | tf_op jit(solution)/shard_map/middle_kernel/pallas_call | solution.py:701
  37.1 11.7 %all_to_all.27.halo_ref = f32[416,1,128]{2,1,0:T(1,128)S(1)} all-to-all(f32[416,1,128]{2,1,0:T(1,128)S(1)} %get-tuple-element.23), channel_id=1, replica_groups=mesh['grp'=4,'frac'=8] {'grp','frac'}, dimensions={0} | all-to-all | bytes 425984 | tf_op jit(solution)/shard_map/all_to_all | solution.py:746
  48.8 2.4 %exchange_kernel.1 = (f32[8,8,256]{2,1,0:T(8,128)S(1)}, f32[2,64,128]{2,1,0:T(8,128)S(1)}, f32[128,256]{1,0:T(8,128)S(1)}) custom-call(f32[416,1,128]{2,1,0:T(1,128)S(1)} %all_to_all.27.halo_ref, s32[8,256]{1,0:T(8,128)S(1)} %bitcast.15, bf16[256,2048]{1,0:T(8,128)(2,1)S(1)} %get-tuple-element.18.cell_hot_ref.hot_ref, ...), custom_call_target="tpu_custom_call" | custom-call | tf_op jit(solution)/shard_map/exchange_kernel/pallas_call | solution.py:701
  51.2 7.4 %all_to_all.28.seg_ref = f32[8,8,256]{2,1,0:T(8,128)S(1)} all-to-all(f32[8,8,256]{2,1,0:T(8,128)S(1)} %get-tuple-element.29.own_ref), channel_id=1, replica_groups=mesh['grp'=4,'frac'=8] {'frac'}, dimensions={0} | all-to-all | bytes 131072 | tf_op jit(solution)/shard_map/all_to_all | solution.py:743
  58.6 1.9 %source_last_kernel.1 = (f32[416,1,128]{2,1,0:T(1,128)}, f32[3,128,256]{2,1,0:T(8,128)S(1)}) custom-call(bf16[256,2048]{1,0:T(8,128)(2,1)S(1)} %get-tuple-element.18.cell_hot_ref.hot_ref, bf16[128,2048]{1,0:T(8,128)(2,1)S(1)} %get-tuple-element.19.cell_row_hot_ref.row_hot_ref, f32[8,72,256]{2,1,0:T(8,128)S(1)} %get-tuple-element.20.sent_ref, ...), custom_call_target="tpu_custom_call" | custom-call | tf_op jit(solution)/shard_map/source_last_kernel/pallas_call | solution.py:701
  60.5 2.6 %all-to-all-start.4 = ((f32[416,1,128]{2,1,0:T(1,128)}), f32[416,1,128]{2,1,0:T(1,128)S(1)}, u32[]{:S(2)}, u32[]{:S(2)}) async-start(f32[416,1,128]{2,1,0:T(1,128)} %get-tuple-element.31), calls=%async_computation.4 | async-start | bytes 425984 | tf_op jit(solution)/shard_map/all_to_all | solution.py:746
  63.1 1.2 %owner_last_kernel.1 = f32[2,64,128]{2,1,0:T(8,128)} custom-call(f32[8,72,256]{2,1,0:T(8,128)S(1)} %all_to_all.25.slot_ref, bf16[128,2048]{1,0:T(8,128)(2,1)S(1)} %get-tuple-element.24.hot_ref, bf16[64,2048]{1,0:T(8,128)(2,1)S(1)} %get-tuple-element.25.row_hot_ref, f32[8,8,256]{2,1,0:T(8,128)S(1)} %get-tuple-element.29.own_ref, ...), custom_call_target="tpu_custom_call" | custom-call | tf_op jit(solution)/shard_map/owner_last_kernel/pallas_call | solution.py:701
  64.3 8.2 %all-to-all-done.4.halo_ref = f32[416,1,128]{2,1,0:T(1,128)S(1)} async-done(((f32[416,1,128]{2,1,0:T(1,128)}), f32[416,1,128]{2,1,0:T(1,128)S(1)}, u32[]{:S(2)}, u32[]{:S(2)}) %all-to-all-start.4) | async-done | bytes 213024 | tf_op jit(solution)/shard_map/all_to_all | solution.py:746
  72.5 1.6 %final_kernel.1 = f32[2,128,256]{2,1,0:T(8,128)} custom-call(f32[416,1,128]{2,1,0:T(1,128)S(1)} %all-to-all-done.4.halo_ref, f32[128,256]{1,0:T(8,128)S(1)} %get-tuple-element.30.pressure_ref, f32[3,128,256]{2,1,0:T(8,128)S(1)} %get-tuple-element.32.kept_ref), custom_call_target="tpu_custom_call" | custom-call | tf_op jit(solution)/shard_map/final_kernel/pallas_call | solution.py:701
Async XLA Ops:
  2.5 15.6 %copy-start = (f32[128,256]{1,0:T(8,128)S(1)}, f32[128,256]{1,0:T(8,128)}, u32[]{:S(2)}) copy-start(f32[128,256]{1,0:T(8,128)} %perm_ref.5) | copy-start | bytes 393220
  2.5 15.6 %copy-start.1 = (f32[2,128,256]{2,1,0:T(8,128)S(1)}, f32[2,128,256]{2,1,0:T(8,128)}, u32[]{:S(2)}) copy-start(f32[2,128,256]{2,1,0:T(8,128)} %state_ref.1) | copy-start | bytes 786436
  2.6 15.6 %copy-start.2 = (f32[1,8192]{1,0:T(1,128)S(1)}, f32[1,8192]{1,0:T(1,128)}, u32[]{:S(2)}) copy-start(f32[1,8192]{1,0:T(1,128)} %param.12) | copy-start | bytes 98308
  2.6 15.6 %copy-start.3 = (f32[2,1,8192]{2,1,0:T(1,128)S(1)}, f32[2,1,8192]{2,1,0:T(1,128)}, u32[]{:S(2)}) copy-start(f32[2,1,8192]{2,1,0:T(1,128)} %param.11) | copy-start | bytes 196612
  21.5 13.2 %copy-start.4 = (s32[1,1,8,256]{3,2,1,0:T(8,128)S(1)}, s32[1,1,8,256]{3,2,1,0:T(8,128)}, u32[]{:S(2)}) copy-start(s32[1,1,8,256]{3,2,1,0:T(8,128)} %param.13) | copy-start | bytes 24580
  60.5 12.0 %all-to-all-start.4 = ((f32[416,1,128]{2,1,0:T(1,128)}), f32[416,1,128]{2,1,0:T(1,128)S(1)}, u32[]{:S(2)}, u32[]{:S(2)}) async-start(f32[416,1,128]{2,1,0:T(1,128)} %get-tuple-element.31), calls=%async_computation.4 | async-start | bytes 425984 | tf_op jit(solution)/shard_map/all_to_all | solution.py:746

commit v5 on v4

--- a/solution.py
+++ b/solution.py
@@ -19,6 +19,7 @@
 BF16 = jnp.bfloat16
 LANES = 128
 SUB = 8
+SEG_COLUMNS = 2 * LANES
 DEPTH = SWEEPS - 1
 
 
@@ -40,8 +41,9 @@
 
 
 def one_hot(index_row, count):
-    hit = iota((count, index_row.shape[1]), 0) == index_row
-    return jnp.where(hit, 1.0, 0.0).astype(BF16)
+    shape = (count, index_row.shape[1])
+    hit = iota(shape, 0).astype(F32).astype(BF16) == index_row.astype(F32).astype(BF16)
+    return jnp.where(hit, jnp.ones(shape, BF16), jnp.zeros(shape, BF16))
 
 
 def pick(table, fields, rows, row_index, hot):
@@ -86,9 +88,21 @@
     return cell_row // columns, cell_row % columns
 
 
+def load_segs(ref, *lead):
+    rows = ref.shape[-2] // 2
+    return jnp.concatenate([ref[(*lead, pl.ds(h, rows, 2), slice(None))] for h in range(2)], axis=1)
+
+
+def store_segs(ref, lead, value):
+    rows = value.shape[0]
+    for h in range(2):
+        ref[lead, pl.ds(h, rows, 2), :] = value[:, h * LANES : (h + 1) * LANES]
+
+
 def ends_of(frac):
-    rows = frac.shape[0]
-    return jnp.concatenate([frac[0:1], frac[rows - 1 : rows]], axis=1)
+    rows, columns = frac.shape
+    lane = iota((1, columns), 1)
+    return jnp.where(lane < columns // 2, frac[0:1], frac[rows - 1 : rows])
 
 
 def frac_step(frac, sat, aperture, before, after, inflow, total, gained):
@@ -376,7 +390,6 @@
 ):
     _, rows, columns = state_ref.shape
     width = cell_ref.shape[1]
-    seg_rows = frac_ref.shape[1]
     copies = [
         pltpu.make_async_copy(source, target, sem.at[i])
         for i, (source, target) in enumerate(
@@ -403,8 +416,9 @@
     table = table_of([state_ref[0], state_ref[1]])
     for copy in copies[2:]:
         copy.wait()
-    ends = ends_of(frac_ref[0])
-    whole = jnp.concatenate([frac_ref[0], frac_ref[1]], axis=1)
+    frac = load_segs(frac_ref, 0)
+    ends = ends_of(frac)
+    whole = jnp.concatenate([frac, load_segs(frac_ref, 1)], axis=0)
     for o in range(members):
         one = slice(o, o + 1)
         row, _ = cell_parts(cell_ref[one, :], columns)
@@ -417,19 +431,19 @@
         out_ref[o, ROW_P : ROW_P + 1, :] = cell_p
         out_ref[o, ROW_S : ROW_S + 1, :] = cell_s
         out_ref[o, ROW_ENDS : ROW_ENDS + 1, :] = ends
-        out_ref[o, SUB : SUB + seg_rows, :] = whole
+        out_ref[o, SUB:, :] = whole
 
 
 def seg_parts(slot_ref, s):
     seg = slot_ref[s, ROW_SEG : ROW_SEG + 1, :].astype(jnp.int32)
-    return seg // LANES, seg % LANES
+    return seg // SEG_COLUMNS, seg % SEG_COLUMNS
 
 
 def seg_hots(slot_ref, hot_ref, row_hot_ref, members, width):
     for s in range(members):
         row, lane = seg_parts(slot_ref, s)
         at = slice(s * width, (s + 1) * width)
-        hot_ref[:, at] = one_hot(lane, LANES)
+        hot_ref[:, at] = one_hot(lane, SEG_COLUMNS)
         row_hot_ref[:, at] = one_hot(row, row_hot_ref.shape[0])
 
 
@@ -465,9 +479,9 @@
     left_seg_ref, left_ref, found_ref,
 ):
     width = slot_ref.shape[2]
-    rows = frac_ref.shape[1]
+    rows = new_ref.shape[1]
     g = lax.axis_index("grp")
-    frac, sat = frac_ref[0], frac_ref[1]
+    frac, sat = load_segs(frac_ref, 0), load_segs(frac_ref, 1)
     seg_hots(slot_ref, hot_ref, row_hot_ref, members, width)
     table = table_of([frac, sat])
     for s in range(members):
@@ -484,12 +498,12 @@
         spread(left_seg_ref, row_hot_ref, s, [weight * cell_p, weight, water])
     inflow, total, gained = gathered_sum(left_seg_ref, hot_ref, 3, rows)
     before, after = chain_ends(slot_ref, ROW_ENDS, members)
-    new_frac, new_sat = frac_step(frac, sat, aperture_ref[...], before, after, inflow, total, gained)
+    new_frac, new_sat = frac_step(frac, sat, load_segs(aperture_ref), before, after, inflow, total, gained)
     new_ref[0] = new_frac
     new_ref[1] = new_sat
     table = table_of([new_frac, new_sat])
-    lane = iota((1, LANES), 1)
-    ends = jnp.where(lane < LANES // 2, new_frac[0:1], new_frac[rows - 1 : rows])
+    ends = ends_of(new_frac)
+    ends = jnp.where(iota((1, LANES), 1) < LANES // 2, ends[:, :LANES], ends[:, SEG_COLUMNS - LANES :])
     for s in range(members):
         seg_p, seg_s = seg_gather(slot_ref, hot_ref, rows, s, width, table)
         own_ref[s, 0:1, :] = seg_p
@@ -499,8 +513,8 @@
         out_ref[at + size - 1] = ends
     for o in range(members):
         row, lane = seg_parts(sent_ref, o)
-        table = table_of([slot_ref[o, SUB : SUB + rows, 0:LANES], slot_ref[o, SUB : SUB + rows, LANES : 2 * LANES]])
-        seg_p, seg_s = pick(table, 2, rows, row, one_hot(lane, LANES))
+        table = table_of([slot_ref[o, SUB : SUB + rows, :], slot_ref[o, SUB + rows :, :]])
+        seg_p, seg_s = pick(table, 2, rows, row, one_hot(lane, SEG_COLUMNS))
         found_ref[o, 0:1, :] = seg_p
         found_ref[o, 1:2, :] = seg_s
     pressure = state_ref[0]
@@ -612,7 +626,7 @@
         lambda s: (own_ref[s, 0:1, :], own_ref[s, 1:2, :]),
         frac_ref[0],
         frac_ref[1],
-        aperture_ref[...],
+        load_segs(aperture_ref),
         (before, after),
         hot_ref,
         row_hot_ref,
@@ -675,14 +689,14 @@
         lambda s: (own_ref[s, 2:3, :], own_ref[s, 3:4, :]),
         frac_ref[0],
         frac_ref[1],
-        aperture_ref[...],
+        load_segs(aperture_ref),
         chain_ends(seg_ref, 4, members),
         hot_ref,
         row_hot_ref,
         left_ref,
     )
-    out_ref[0] = new_frac
-    out_ref[1] = new_sat
+    store_segs(out_ref, 0, new_frac)
+    store_segs(out_ref, 1, new_sat)
 
 
 def final_kernel(groups, members, size, halo_ref, pressure_ref, kept_ref, out_ref, q_ext, inv_ext, p_ext):
@@ -736,7 +750,9 @@
     both = (groups, members, size)
     halo = (devices * size, 1, LANES)
     left_cell = pltpu.VMEM((3 * PARTS * rows, every), BF16)
-    left_seg = pltpu.VMEM((3 * PARTS * seg_rows, every), BF16)
+    seg_wide = seg_dev // SEG_COLUMNS
+    segs_wide = (2, seg_wide, SEG_COLUMNS)
+    left_seg = pltpu.VMEM((3 * PARTS * seg_wide, every), BF16)
     ext = [pltpu.VMEM((rows + SUB, columns + LANES), F32)] * 3
 
     def to_group(x):
@@ -751,7 +767,7 @@
     sent, cell_hot, cell_row_hot = call(
         first_kernel,
         (members,),
-        [(members, SUB + seg_rows, width)] + hots(columns, rows),
+        [(members, SUB + 2 * seg_wide, SEG_COLUMNS)] + hots(columns, rows),
         [
             pltpu.VMEM((members, width), jnp.int32),
             pltpu.VMEM((members, width), jnp.int32),
@@ -774,7 +790,7 @@
     edge, kept, own, frac1, hot, row_hot = call(
         start_kernel,
         both,
-        [halo, (4, rows, columns), (members, 2, width), frac.shape] + hots(LANES, seg_rows),
+        [halo, (4, rows, columns), (members, 2, width), segs_wide] + hots(SEG_COLUMNS, seg_wide),
         [left_seg, left_cell, pltpu.VMEM((members, 2, width), F32)],
         slot, sent, cell_hot, cell_row_hot, frac, aperture, matrix_state, matrix_perm,
     )
@@ -785,7 +801,7 @@
     )
     around = to_all(edge)
     own, frac2, pressure = call(
-        exchange_kernel, both, [slots, frac.shape, (rows, columns)], [left_seg] + ext,
+        exchange_kernel, both, [slots, segs_wide, (rows, columns)], [left_seg] + ext,
         around, cells, cell_hot, slot, hot, row_hot, before, own, frac1, aperture, kept,
     )
     segs = to_group(own)

time: 74.4 us -> 73.3 us (0.985)
  Pallas kernels: 14.7 us -> 13.5 us
    pallas_call x7, Pallas kernels: 14.7 us -> 13.5 us  [call(): pl.pallas_call(functools.partial(kernel, *statics), out_shape=outs, in_sp...]
where the time goes in v5:
time: 73.3 us; the launch traced here: 72.9 us
  blocking collectives  47.8 us (65%)
  Pallas kernels  13.5 us (18%)
  waiting for transfers between devices  8.27 us (11%)
  starting transfers between devices  2.58 us (4%)
    all_to_all x2, blocking collectives, to_all(): lax.all_to_all(x, ('grp', 'frac'), split_axis=0, concat_axis=0, tiled=True)  24.9 us
    all_to_all x2, blocking collectives, to_group(): return lax.all_to_all(x, 'frac', split_axis=0, concat_axis=0, tiled=True)  22.9 us
    pallas_call x7, Pallas kernels, call(): pl.pallas_call(functools.partial(kernel, *statics), out_shape=outs, in_sp...  13.5 us
    all_to_all x1, waiting for transfers between devices, to_all(): lax.all_to_all(x, ('grp', 'frac'), split_axis=0, concat_axis=0, tiled=True)  8.27 us
    all_to_all x1, starting transfers between devices, to_all(): lax.all_to_all(x, ('grp', 'frac'), split_axis=0, concat_axis=0, tiled=True)  2.58 us
  transfers between devices with their start and end apart: 1, of which 1 were waited for; matrix products, arithmetic and copies ran while one was open for 0% of the time, Pallas kernels for 2%

profile of v5, /device:TPU:0, one launch (start us, length us, event | category | flops | bytes accessed | tf_op | source)
XLA Modules:
  0.0 72.9 jit_solution(4995848760320553208)
XLA Ops:
  0.6 1.9 %first_kernel.1 = (f32[8,72,256]{2,1,0:T(8,128)S(1)}, bf16[256,2048]{1,0:T(8,128)(2,1)S(1)}, bf16[128,2048]{1,0:T(8,128)(2,1)S(1)}) custom-call(s32[8,256]{1,0:T(8,128)} %bitcast.13, s32[8,256]{1,0:T(8,128)} %bitcast.18, f32[8,256]{1,0:T(8,128)} %bitcast.19, s32[1,8]{1,0:T(1,128)} %bitcast.20, s32[3,8,256]{2,1,0:T(8,128)} %bitcast.17, ...), custom_call_target="tpu_custom_call" | custom-call | tf_op jit(solution)/shard_map/first_kernel/pallas_call | solution.py:715
  2.5 0.0 copy-start
  2.5 0.0 copy-start.1
  2.5 0.0 copy-start.2
  2.5 0.0 copy-start.3
  2.6 15.5 %all_to_all.25.slot_ref = f32[8,72,256]{2,1,0:T(8,128)S(1)} all-to-all(f32[8,72,256]{2,1,0:T(8,128)S(1)} %get-tuple-element.20.sent_ref), channel_id=1, replica_groups=mesh['grp'=4,'frac'=8] {'frac'}, dimensions={0} | all-to-all | bytes 1179648 | tf_op jit(solution)/shard_map/all_to_all | solution.py:759
  18.1 0.0 copy-done
  18.1 0.0 copy-done.1
  18.1 0.0 copy-done.2
  18.1 0.0 copy-done.3
  18.1 2.7 %start_kernel.1 = (f32[416,1,128]{2,1,0:T(1,128)S(1)}, f32[4,128,256]{2,1,0:T(8,128)S(1)}, f32[8,2,256]{2,1,0:T(2,128)S(1)}, f32[2,32,256]{2,1,0:T(8,128)S(1)}, ...) custom-call(f32[8,72,256]{2,1,0:T(8,128)S(1)} %all_to_all.25.slot_ref, ...), custom_call_target="tpu_custom_call" | custom-call | tf_op jit(solution)/shard_map/start_kernel/pallas_call | solution.py:715
  20.8 0.0 copy-start.4
  20.8 13.2 %all_to_all.26.halo_ref.ends_ref = f32[416,1,128]{2,1,0:T(1,128)S(1)} all-to-all(f32[416,1,128]{2,1,0:T(1,128)S(1)} %get-tuple-element.21), channel_id=1, replica_groups=mesh['grp'=4,'frac'=8] {'grp','frac'}, dimensions={0} | all-to-all | bytes 425984 | tf_op jit(solution)/shard_map/all_to_all | solution.py:762
  34.0 0.0 copy-done.4
  34.0 2.4 %middle_kernel.1 = (f32[416,1,128]{2,1,0:T(1,128)S(1)}, f32[4,128,256]{2,1,0:T(8,128)S(1)}) custom-call(f32[416,1,128]{2,1,0:T(1,128)S(1)} %all_to_all.26.halo_ref.ends_ref, s32[8,256]{1,0:T(8,128)S(1)} %bitcast.14, bf16[256,2048]{1,0:T(8,128)(2,1)S(1)} %get-tuple-element.18.cell_hot_ref.hot_ref, ...), custom_call_target="tpu_custom_call" | custom-call | tf_op jit(solution)/shard_map/middle_kernel/pallas_call | solution.py:715
  36.4 11.7 %all_to_all.27.halo_ref = f32[416,1,128]{2,1,0:T(1,128)S(1)} all-to-all(f32[416,1,128]{2,1,0:T(1,128)S(1)} %get-tuple-element.23), channel_id=1, replica_groups=mesh['grp'=4,'frac'=8] {'grp','frac'}, dimensions={0} | all-to-all | bytes 425984 | tf_op jit(solution)/shard_map/all_to_all | solution.py:762
  48.1 1.9 %exchange_kernel.1 = (f32[8,8,256]{2,1,0:T(8,128)S(1)}, f32[2,32,256]{2,1,0:T(8,128)S(1)}, f32[128,256]{1,0:T(8,128)S(1)}) custom-call(f32[416,1,128]{2,1,0:T(1,128)S(1)} %all_to_all.27.halo_ref, s32[8,256]{1,0:T(8,128)S(1)} %bitcast.15, bf16[256,2048]{1,0:T(8,128)(2,1)S(1)} %get-tuple-element.18.cell_hot_ref.hot_ref, ...), custom_call_target="tpu_custom_call" | custom-call | tf_op jit(solution)/shard_map/exchange_kernel/pallas_call | solution.py:715
  50.1 7.4 %all_to_all.28.seg_ref = f32[8,8,256]{2,1,0:T(8,128)S(1)} all-to-all(f32[8,8,256]{2,1,0:T(8,128)S(1)} %get-tuple-element.29.own_ref), channel_id=1, replica_groups=mesh['grp'=4,'frac'=8] {'frac'}, dimensions={0} | all-to-all | bytes 131072 | tf_op jit(solution)/shard_map/all_to_all | solution.py:759
  57.5 1.9 %source_last_kernel.1 = (f32[416,1,128]{2,1,0:T(1,128)}, f32[3,128,256]{2,1,0:T(8,128)S(1)}) custom-call(bf16[256,2048]{1,0:T(8,128)(2,1)S(1)} %get-tuple-element.18.cell_hot_ref.hot_ref, bf16[128,2048]{1,0:T(8,128)(2,1)S(1)} %get-tuple-element.19.cell_row_hot_ref.row_hot_ref, f32[8,72,256]{2,1,0:T(8,128)S(1)} %get-tuple-element.20.sent_ref, ...), custom_call_target="tpu_custom_call" | custom-call | tf_op jit(solution)/shard_map/source_last_kernel/pallas_call | solution.py:715
  59.3 2.6 %all-to-all-start.4 = ((f32[416,1,128]{2,1,0:T(1,128)}), f32[416,1,128]{2,1,0:T(1,128)S(1)}, u32[]{:S(2)}, u32[]{:S(2)}) async-start(f32[416,1,128]{2,1,0:T(1,128)} %get-tuple-element.31), calls=%async_computation.4 | async-start | bytes 425984 | tf_op jit(solution)/shard_map/all_to_all | solution.py:762
  61.9 1.1 %owner_last_kernel.1 = f32[2,64,128]{2,1,0:T(8,128)} custom-call(f32[8,72,256]{2,1,0:T(8,128)S(1)} %all_to_all.25.slot_ref, bf16[256,2048]{1,0:T(8,128)(2,1)S(1)} %get-tuple-element.24.hot_ref, bf16[32,2048]{1,0:T(8,128)(2,1)S(1)} %get-tuple-element.25.row_hot_ref, f32[8,8,256]{2,1,0:T(8,128)S(1)} %get-tuple-element.29.own_ref, ...), custom_call_target="tpu_custom_call" | custom-call | tf_op jit(solution)/shard_map/owner_last_kernel/pallas_call | solution.py:715
  63.1 8.3 %all-to-all-done.4.halo_ref = f32[416,1,128]{2,1,0:T(1,128)S(1)} async-done(((f32[416,1,128]{2,1,0:T(1,128)}), f32[416,1,128]{2,1,0:T(1,128)S(1)}, u32[]{:S(2)}, u32[]{:S(2)}) %all-to-all-start.4) | async-done | bytes 213024 | tf_op jit(solution)/shard_map/all_to_all | solution.py:762
  71.4 1.6 %final_kernel.1 = f32[2,128,256]{2,1,0:T(8,128)} custom-call(f32[416,1,128]{2,1,0:T(1,128)S(1)} %all-to-all-done.4.halo_ref, f32[128,256]{1,0:T(8,128)S(1)} %get-tuple-element.30.pressure_ref, f32[3,128,256]{2,1,0:T(8,128)S(1)} %get-tuple-element.32.kept_ref), custom_call_target="tpu_custom_call" | custom-call | tf_op jit(solution)/shard_map/final_kernel/pallas_call | solution.py:715
Async XLA Ops:
  2.5 15.6 %copy-start = (f32[128,256]{1,0:T(8,128)S(1)}, f32[128,256]{1,0:T(8,128)}, u32[]{:S(2)}) copy-start(f32[128,256]{1,0:T(8,128)} %perm_ref.5) | copy-start | bytes 393220
  2.5 15.6 %copy-start.1 = (f32[2,128,256]{2,1,0:T(8,128)S(1)}, f32[2,128,256]{2,1,0:T(8,128)}, u32[]{:S(2)}) copy-start(f32[2,128,256]{2,1,0:T(8,128)} %state_ref.1) | copy-start | bytes 786436
  2.5 15.6 %copy-start.2 = (f32[1,8192]{1,0:T(1,128)S(1)}, f32[1,8192]{1,0:T(1,128)}, u32[]{:S(2)}) copy-start(f32[1,8192]{1,0:T(1,128)} %param.12) | copy-start | bytes 98308
  2.5 15.6 %copy-start.3 = (f32[2,1,8192]{2,1,0:T(1,128)S(1)}, f32[2,1,8192]{2,1,0:T(1,128)}, u32[]{:S(2)}) copy-start(f32[2,1,8192]{2,1,0:T(1,128)} %param.11) | copy-start | bytes 196612
  20.8 13.2 %copy-start.4 = (s32[1,1,8,256]{3,2,1,0:T(8,128)S(1)}, s32[1,1,8,256]{3,2,1,0:T(8,128)}, u32[]{:S(2)}) copy-start(s32[1,1,8,256]{3,2,1,0:T(8,128)} %param.13) | copy-start | bytes 24580
  59.3 12.0 %all-to-all-start.4 = ((f32[416,1,128]{2,1,0:T(1,128)}), f32[416,1,128]{2,1,0:T(1,128)S(1)}, u32[]{:S(2)}, u32[]{:S(2)}) async-start(f32[416,1,128]{2,1,0:T(1,128)} %get-tuple-element.31), calls=%async_computation.4 | async-start | bytes 425984 | tf_op jit(solution)/shard_map/all_to_all | solution.py:762

commit v6 on v5

--- a/solution.py
+++ b/solution.py
@@ -250,9 +250,11 @@
         put_rows(out_ref, (here + 1) * size, right)
 
 
-def chebyshev(in_ref, q, inv, p, q_ext, inv_ext, p_ext, groups, members, size):
-    rows, columns = q.shape
+def chebyshev(in_ref, q_ref, inv_ref, p_ref, target, scratch, groups, members, size):
+    q_ext, inv_ext, p_ext, update_ref, even_ref, odd_ref = scratch
+    rows, columns = target.shape
     halves = columns // LANES
+    side = halves
     g, f = lax.axis_index("grp"), lax.axis_index("frac")
     here = g * members + f
     last = groups * members - 1
@@ -265,18 +267,17 @@
     def both(low, high, at, count, size):
         return jnp.where(at < count, low, jnp.where(at >= size - count, high, 0.0))
 
-    q_ext[0:rows, 0:columns] = q
-    inv_ext[0:rows, 0:columns] = inv
-    p_ext[0:rows, 0:columns] = p
+    def filler(count):
+        return jnp.zeros((count, LANES), F32)
+
+    for h in range(halves):
+        for ext, ref in ((q_ext, q_ref), (inv_ext, inv_ref), (p_ext, p_ref)):
+            ext[h, 0:rows, :] = ref[:, h * LANES : (h + 1) * LANES]
+    outer = slice(rows, rows + SUB)
     below, above = taker(1, 0), taker(-1, 0)
     lane = iota((1, LANES), 1)
     low_extra, high_extra = below(halves * 2 * DEPTH, 1), above(halves * 2 * DEPTH, 1)
-
-    def filler(count):
-        return jnp.zeros((count, LANES), F32)
-
     for h in range(halves):
-        tile = slice(h * LANES, (h + 1) * LANES)
         edge = (lane == 0) & (h == 0) | (lane == LANES - 1) & (h == halves - 1)
 
         def at_edge(row, turn):
@@ -284,11 +285,11 @@
 
         turn = LANES - 1 if h == 0 else 1
         at = h * DEPTH
-        q_ext[rows : rows + SUB, tile] = jnp.concatenate(
+        q_ext[h, outer, :] = jnp.concatenate(
             [below(at, DEPTH), filler(SUB - 2 * DEPTH), above(at, DEPTH)], axis=0
         )
         at = halves * DEPTH + h * (DEPTH - 1)
-        inv_ext[rows : rows + SUB, tile] = jnp.concatenate(
+        inv_ext[h, outer, :] = jnp.concatenate(
             [
                 below(at, DEPTH - 1),
                 at_edge(low_extra, 0),
@@ -299,7 +300,7 @@
             axis=0,
         )
         at = halves * (2 * DEPTH - 1) + h
-        p_ext[rows : rows + SUB, tile] = jnp.concatenate(
+        p_ext[h, outer, :] = jnp.concatenate(
             [
                 below(at, 1),
                 at_edge(low_extra, turn),
@@ -314,20 +315,18 @@
         jnp.concatenate([right, jnp.zeros((LANES - 2 * SUB, rows), F32), left], axis=0)
     )
     lane = iota((rows, LANES), 1)
-    side = slice(columns, columns + LANES)
-    q_ext[0:rows, side] = both(turned, turned, lane, DEPTH, LANES)
-    inv_ext[0:rows, side] = both(
+    q_ext[side, 0:rows, :] = both(turned, turned, lane, DEPTH, LANES)
+    inv_ext[side, 0:rows, :] = both(
         pltpu.roll(turned, LANES - DEPTH, 1), pltpu.roll(turned, DEPTH, 1), lane, DEPTH, LANES
     )
-    p_ext[0:rows, side] = both(
+    p_ext[side, 0:rows, :] = both(
         pltpu.roll(turned, LANES - 2 * DEPTH, 1), pltpu.roll(turned, 2 * DEPTH, 1), lane, 2, LANES
     )
     lane = iota((DEPTH, LANES), 1)
-    corner = slice(rows, rows + SUB)
     low_right, low_left, high_right, high_left = taker(1, 1), taker(1, -1), taker(-1, 1), taker(-1, -1)
     for i, ext in enumerate((q_ext, inv_ext, p_ext)):
         at = i * DEPTH
-        ext[corner, side] = jnp.concatenate(
+        ext[side, outer, :] = jnp.concatenate(
             [
                 both(low_right(at, DEPTH), low_left(at, DEPTH), lane, DEPTH, LANES),
                 filler(SUB - 2 * DEPTH),
@@ -336,44 +335,66 @@
             axis=0,
         )
 
-    shape = (rows + SUB, columns + LANES)
-    for here_row, there_row in ((0, shape[0] - 1), (shape[0] - 1, 0), (rows - 1, rows), (rows, rows - 1)):
-        q_ext[here_row : here_row + 1, :] += (
-            inv_ext[here_row : here_row + 1, :] * p_ext[there_row : there_row + 1, :]
-        )
-    lane = iota((shape[0], LANES), 1)
-    first, final = slice(0, LANES), slice(columns - LANES, columns)
-    p_side = p_ext[:, side]
-    from_left, from_right = pltpu.roll(p_side, 1, 1), pltpu.roll(p_side, LANES - 1, 1)
-    q_ext[:, first] += inv_ext[:, first] * jnp.where(lane == 0, from_left, 0.0)
-    q_ext[:, final] += inv_ext[:, final] * jnp.where(lane == LANES - 1, from_right, 0.0)
-    q_ext[:, side] += inv_ext[:, side] * jnp.where(
-        lane == 0,
-        pltpu.roll(p_ext[:, final], 1, 1),
-        jnp.where(lane == LANES - 1, pltpu.roll(p_ext[:, first], LANES - 1, 1), 0.0),
-    )
-    inverse = inv_ext[...]
-    start = q_ext[...]
-
+    end = rows + SUB - 1
+    for own, other in ((0, end), (end, 0), (rows - 1, rows), (rows, rows - 1)):
+        for c in range(halves + 1):
+            q_ext[c, own : own + 1, :] += inv_ext[c, own : own + 1, :] * p_ext[c, other : other + 1, :]
     centre = 0.5 * (HIGH_BOUND + LOW_BOUND)
     half_width = 0.5 * (HIGH_BOUND - LOW_BOUND)
     scale_ratio = centre / half_width
     ratio_now = 1.0 / scale_ratio
-    update = start / centre if centre != 1.0 else start
-    change = update
-    for _ in range(SWEEPS - 1):
-        beside = (
-            pltpu.roll(change, 1, 0)
-            + pltpu.roll(change, shape[0] - 1, 0)
-            + pltpu.roll(change, 1, 1)
-            + pltpu.roll(change, shape[1] - 1, 1)
+    lane = iota((SUB, LANES), 1)
+    count = rows // SUB + 1
+
+    def keep(ref, c, r, value):
+        at = (r + 1) * SUB
+        ref[c, at : at + SUB, :] = value
+        if r == count - 1:
+            ref[c, 0:SUB, :] = value
+        if r == 0:
+            at = (count + 1) * SUB
+            ref[c, at : at + SUB, :] = value
+
+    for r in range(count):
+        at = slice(r * SUB, (r + 1) * SUB)
+        p_side, p_first, p_final = p_ext[side, at, :], p_ext[0, at, :], p_ext[halves - 1, at, :]
+        missing = [0.0] * (halves + 1)
+        missing[0] += jnp.where(lane == 0, pltpu.roll(p_side, 1, 1), 0.0)
+        missing[halves - 1] += jnp.where(lane == LANES - 1, pltpu.roll(p_side, LANES - 1, 1), 0.0)
+        missing[side] = jnp.where(
+            lane == 0,
+            pltpu.roll(p_final, 1, 1),
+            jnp.where(lane == LANES - 1, pltpu.roll(p_first, LANES - 1, 1), 0.0),
         )
-        residual = start - change + inverse * beside
+        for c in range(halves + 1):
+            start = q_ext[c, at, :] + inv_ext[c, at, :] * missing[c]
+            q_ext[c, at, :] = start
+            keep(even_ref, c, r, start / centre if centre != 1.0 else start)
+    now_ref, next_ref = even_ref, odd_ref
+    for sweep in range(1, SWEEPS):
         ratio_next = 1.0 / (2.0 * scale_ratio - ratio_now)
-        update = ratio_next * ratio_now * update + (2.0 * ratio_next / half_width) * residual
+        final = sweep == SWEEPS - 1
+        for r in range(count - 1 if final else count):
+            at = slice(r * SUB, (r + 1) * SUB)
+            mids = [now_ref[c, (r + 1) * SUB : (r + 2) * SUB, :] for c in range(halves + 1)]
+            after = [pltpu.roll(m, 1, 1) for m in mids]
+            ahead = [pltpu.roll(m, LANES - 1, 1) for m in mids]
+            for c in range(halves if final else halves + 1):
+                beside = now_ref[c, (r + 1) * SUB - 1 : (r + 2) * SUB - 1, :]
+                beside += now_ref[c, (r + 1) * SUB + 1 : (r + 2) * SUB + 1, :]
+                beside += jnp.where(lane == 0, after[(c - 1) % (halves + 1)], after[c])
+                beside += jnp.where(lane == LANES - 1, ahead[(c + 1) % (halves + 1)], ahead[c])
+                residual = q_ext[c, at, :] - mids[c] + inv_ext[c, at, :] * beside
+                old = mids[c] if sweep == 1 else update_ref[c, at, :]
+                update = ratio_next * ratio_now * old + (2.0 * ratio_next / half_width) * residual
+                if final:
+                    tile = slice(c * LANES, (c + 1) * LANES)
+                    target[at, tile] = p_ref[at, tile] + mids[c] + update
+                else:
+                    update_ref[c, at, :] = update
+                    keep(next_ref, c, r, mids[c] + update)
         ratio_now = ratio_next
-        change = change + update
-    return p + change[0:rows, 0:columns]
+        now_ref, next_ref = next_ref, now_ref
 
 
 ROW_SEG = 0
@@ -549,11 +570,12 @@
 
 def middle_kernel(
     groups, members, size, halo_ref, cell_ref, hot_ref, row_hot_ref, sent_ref, kept_ref, perm_ref,
-    out_ref, keep_ref, slots_ref, left_ref, q_ext, inv_ext, p_ext,
+    out_ref, keep_ref, slots_ref, left_ref, *scratch,
 ):
-    pressure = chebyshev(
-        halo_ref, kept_ref[2], kept_ref[3], kept_ref[0], q_ext, inv_ext, p_ext, groups, members, size
-    )
+    chebyshev(
+        halo_ref, kept_ref.at[2], kept_ref.at[3], kept_ref.at[0], keep_ref.at[0], scratch, groups, members, size
+    )
+    pressure = keep_ref[0]
     saturation = kept_ref[1]
     g = lax.axis_index("grp")
 
@@ -576,7 +598,6 @@
         perm_ref[...],
         left_ref,
     )
-    keep_ref[0] = pressure
     keep_ref[1] = new_saturation
     keep_ref[2] = q
     keep_ref[3] = inv
@@ -603,7 +624,7 @@
 
 def exchange_kernel(
     groups, members, size, halo_ref, cell_ref, cell_hot_ref, slot_ref, hot_ref, row_hot_ref, ends_ref, own_ref,
-    frac_ref, aperture_ref, kept_ref, out_ref, new_ref, pressure_ref, left_ref, q_ext, inv_ext, p_ext,
+    frac_ref, aperture_ref, kept_ref, out_ref, new_ref, pressure_ref, left_ref, *scratch,
 ):
     width = slot_ref.shape[2]
     rows = frac_ref.shape[1]
@@ -642,10 +663,10 @@
         out_ref[s, 3:4, :] = seg_s
         out_ref[s, 4:5, :] = ends
 
-    pressure = chebyshev(
-        halo_ref, kept_ref[2], kept_ref[3], kept_ref[0], q_ext, inv_ext, p_ext, groups, members, size
-    )
-    pressure_ref[...] = pressure
+    chebyshev(
+        halo_ref, kept_ref.at[2], kept_ref.at[3], kept_ref.at[0], pressure_ref, scratch, groups, members, size
+    )
+    pressure = pressure_ref[...]
 
     def put(o, cell_p, cell_s):
         out_ref[o, 0:1, :] = cell_p
@@ -699,9 +720,9 @@
     store_segs(out_ref, 1, new_sat)
 
 
-def final_kernel(groups, members, size, halo_ref, pressure_ref, kept_ref, out_ref, q_ext, inv_ext, p_ext):
-    out_ref[0] = chebyshev(
-        halo_ref, kept_ref[1], kept_ref[2], pressure_ref[...], q_ext, inv_ext, p_ext, groups, members, size
+def final_kernel(groups, members, size, halo_ref, pressure_ref, kept_ref, out_ref, *scratch):
+    chebyshev(
+        halo_ref, kept_ref.at[1], kept_ref.at[2], pressure_ref, out_ref.at[0], scratch, groups, members, size
     )
     out_ref[1] = kept_ref[0]
 
@@ -753,7 +774,8 @@
     seg_wide = seg_dev // SEG_COLUMNS
     segs_wide = (2, seg_wide, SEG_COLUMNS)
     left_seg = pltpu.VMEM((3 * PARTS * seg_wide, every), BF16)
-    ext = [pltpu.VMEM((rows + SUB, columns + LANES), F32)] * 3
+    tiles = columns // LANES + 1
+    ext = [pltpu.VMEM((tiles, rows + SUB, LANES), F32)] * 4 + [pltpu.VMEM((tiles, rows + 3 * SUB, LANES), F32)] * 2
 
     def to_group(x):
         return lax.all_to_all(x, "frac", split_axis=0, concat_axis=0, tiled=True)

time: 73.3 us -> 73 us (level)
  no operation moved by 1% of the time
where the time goes in v6:
time: 73 us; the launch traced here: 72.6 us
  blocking collectives  47.8 us (65%)
  Pallas kernels  13.2 us (18%)
  waiting for transfers between devices  8.28 us (11%)
  starting transfers between devices  2.58 us (4%)
    all_to_all x2, blocking collectives, to_all(): lax.all_to_all(x, ('grp', 'frac'), split_axis=0, concat_axis=0, tiled=True)  24.9 us
    all_to_all x2, blocking collectives, to_group(): return lax.all_to_all(x, 'frac', split_axis=0, concat_axis=0, tiled=True)  22.9 us
    pallas_call x7, Pallas kernels, call(): pl.pallas_call(functools.partial(kernel, *statics), out_shape=outs, in_sp...  13.2 us
    all_to_all x1, waiting for transfers between devices, to_all(): lax.all_to_all(x, ('grp', 'frac'), split_axis=0, concat_axis=0, tiled=True)  8.28 us
    all_to_all x1, starting transfers between devices, to_all(): lax.all_to_all(x, ('grp', 'frac'), split_axis=0, concat_axis=0, tiled=True)  2.58 us
  transfers between devices with their start and end apart: 1, of which 1 were waited for; matrix products, arithmetic and copies ran while one was open for 0% of the time, Pallas kernels for 2%

profile of v6, /device:TPU:0, one launch (start us, length us, event | category | flops | bytes accessed | tf_op | source)
XLA Modules:
  0.0 72.6 jit_solution(2011985217181618454)
XLA Ops:
  0.6 1.9 %first_kernel.1 = (f32[8,72,256]{2,1,0:T(8,128)S(1)}, bf16[256,2048]{1,0:T(8,128)(2,1)S(1)}, bf16[128,2048]{1,0:T(8,128)(2,1)S(1)}) custom-call(s32[8,256]{1,0:T(8,128)} %bitcast.13, s32[8,256]{1,0:T(8,128)} %bitcast.18, f32[8,256]{1,0:T(8,128)} %bitcast.19, s32[1,8]{1,0:T(1,128)} %bitcast.20, s32[3,8,256]{2,1,0:T(8,128)} %bitcast.17, ...), custom_call_target="tpu_custom_call" | custom-call | tf_op jit(solution)/shard_map/first_kernel/pallas_call | solution.py:736
  2.5 0.0 copy-start
  2.5 0.0 copy-start.1
  2.5 0.0 copy-start.2
  2.5 0.0 copy-start.3
  2.6 15.5 %all_to_all.25.slot_ref = f32[8,72,256]{2,1,0:T(8,128)S(1)} all-to-all(f32[8,72,256]{2,1,0:T(8,128)S(1)} %get-tuple-element.20.sent_ref), channel_id=1, replica_groups=mesh['grp'=4,'frac'=8] {'frac'}, dimensions={0} | all-to-all | bytes 1179648 | tf_op jit(solution)/shard_map/all_to_all | solution.py:781
  18.1 0.0 copy-done
  18.1 0.0 copy-done.1
  18.1 0.0 copy-done.2
  18.1 0.0 copy-done.3
  18.1 2.7 %start_kernel.1 = (f32[416,1,128]{2,1,0:T(1,128)S(1)}, f32[4,128,256]{2,1,0:T(8,128)S(1)}, f32[8,2,256]{2,1,0:T(2,128)S(1)}, f32[2,32,256]{2,1,0:T(8,128)S(1)}, ...) custom-call(f32[8,72,256]{2,1,0:T(8,128)S(1)} %all_to_all.25.slot_ref, ...), custom_call_target="tpu_custom_call" | custom-call | tf_op jit(solution)/shard_map/start_kernel/pallas_call | solution.py:736
  20.8 0.0 copy-start.4
  20.8 13.2 %all_to_all.26.halo_ref.ends_ref = f32[416,1,128]{2,1,0:T(1,128)S(1)} all-to-all(f32[416,1,128]{2,1,0:T(1,128)S(1)} %get-tuple-element.21), channel_id=1, replica_groups=mesh['grp'=4,'frac'=8] {'grp','frac'}, dimensions={0} | all-to-all | bytes 425984 | tf_op jit(solution)/shard_map/all_to_all | solution.py:784
  34.0 0.0 copy-done.4
  34.0 2.4 %middle_kernel.1 = (f32[416,1,128]{2,1,0:T(1,128)S(1)}, f32[4,128,256]{2,1,0:T(8,128)S(1)}) custom-call(f32[416,1,128]{2,1,0:T(1,128)S(1)} %all_to_all.26.halo_ref.ends_ref, s32[8,256]{1,0:T(8,128)S(1)} %bitcast.14, bf16[256,2048]{1,0:T(8,128)(2,1)S(1)} %get-tuple-element.18.cell_hot_ref.hot_ref, ...), custom_call_target="tpu_custom_call" | custom-call | tf_op jit(solution)/shard_map/middle_kernel/pallas_call | solution.py:736
  36.4 11.7 %all_to_all.27.halo_ref = f32[416,1,128]{2,1,0:T(1,128)S(1)} all-to-all(f32[416,1,128]{2,1,0:T(1,128)S(1)} %get-tuple-element.23), channel_id=1, replica_groups=mesh['grp'=4,'frac'=8] {'grp','frac'}, dimensions={0} | all-to-all | bytes 425984 | tf_op jit(solution)/shard_map/all_to_all | solution.py:784
  48.1 1.9 %exchange_kernel.1 = (f32[8,8,256]{2,1,0:T(8,128)S(1)}, f32[2,32,256]{2,1,0:T(8,128)S(1)}, f32[128,256]{1,0:T(8,128)S(1)}) custom-call(f32[416,1,128]{2,1,0:T(1,128)S(1)} %all_to_all.27.halo_ref, s32[8,256]{1,0:T(8,128)S(1)} %bitcast.15, bf16[256,2048]{1,0:T(8,128)(2,1)S(1)} %get-tuple-element.18.cell_hot_ref.hot_ref, ...), custom_call_target="tpu_custom_call" | custom-call | tf_op jit(solution)/shard_map/exchange_kernel/pallas_call | solution.py:736
  50.0 7.4 %all_to_all.28.seg_ref = f32[8,8,256]{2,1,0:T(8,128)S(1)} all-to-all(f32[8,8,256]{2,1,0:T(8,128)S(1)} %get-tuple-element.29.own_ref), channel_id=1, replica_groups=mesh['grp'=4,'frac'=8] {'frac'}, dimensions={0} | all-to-all | bytes 131072 | tf_op jit(solution)/shard_map/all_to_all | solution.py:781
  57.4 1.9 %source_last_kernel.1 = (f32[416,1,128]{2,1,0:T(1,128)}, f32[3,128,256]{2,1,0:T(8,128)S(1)}) custom-call(bf16[256,2048]{1,0:T(8,128)(2,1)S(1)} %get-tuple-element.18.cell_hot_ref.hot_ref, bf16[128,2048]{1,0:T(8,128)(2,1)S(1)} %get-tuple-element.19.cell_row_hot_ref.row_hot_ref, f32[8,72,256]{2,1,0:T(8,128)S(1)} %get-tuple-element.20.sent_ref, ...), custom_call_target="tpu_custom_call" | custom-call | tf_op jit(solution)/shard_map/source_last_kernel/pallas_call | solution.py:736
  59.3 2.6 %all-to-all-start.4 = ((f32[416,1,128]{2,1,0:T(1,128)}), f32[416,1,128]{2,1,0:T(1,128)S(1)}, u32[]{:S(2)}, u32[]{:S(2)}) async-start(f32[416,1,128]{2,1,0:T(1,128)} %get-tuple-element.31), calls=%async_computation.4 | async-start | bytes 425984 | tf_op jit(solution)/shard_map/all_to_all | solution.py:784
  61.9 1.1 %owner_last_kernel.1 = f32[2,64,128]{2,1,0:T(8,128)} custom-call(f32[8,72,256]{2,1,0:T(8,128)S(1)} %all_to_all.25.slot_ref, bf16[256,2048]{1,0:T(8,128)(2,1)S(1)} %get-tuple-element.24.hot_ref, bf16[32,2048]{1,0:T(8,128)(2,1)S(1)} %get-tuple-element.25.row_hot_ref, f32[8,8,256]{2,1,0:T(8,128)S(1)} %get-tuple-element.29.own_ref, ...), custom_call_target="tpu_custom_call" | custom-call | tf_op jit(solution)/shard_map/owner_last_kernel/pallas_call | solution.py:736
  63.0 8.3 %all-to-all-done.4.halo_ref = f32[416,1,128]{2,1,0:T(1,128)S(1)} async-done(((f32[416,1,128]{2,1,0:T(1,128)}), f32[416,1,128]{2,1,0:T(1,128)S(1)}, u32[]{:S(2)}, u32[]{:S(2)}) %all-to-all-start.4) | async-done | bytes 213024 | tf_op jit(solution)/shard_map/all_to_all | solution.py:784
  71.3 1.4 %final_kernel.1 = f32[2,128,256]{2,1,0:T(8,128)} custom-call(f32[416,1,128]{2,1,0:T(1,128)S(1)} %all-to-all-done.4.halo_ref, f32[128,256]{1,0:T(8,128)S(1)} %get-tuple-element.30.pressure_ref, f32[3,128,256]{2,1,0:T(8,128)S(1)} %get-tuple-element.32.kept_ref), custom_call_target="tpu_custom_call" | custom-call | tf_op jit(solution)/shard_map/final_kernel/pallas_call | solution.py:736
Async XLA Ops:
  2.5 15.6 %copy-start = (f32[128,256]{1,0:T(8,128)S(1)}, f32[128,256]{1,0:T(8,128)}, u32[]{:S(2)}) copy-start(f32[128,256]{1,0:T(8,128)} %perm_ref.5) | copy-start | bytes 393220
  2.5 15.6 %copy-start.1 = (f32[2,128,256]{2,1,0:T(8,128)S(1)}, f32[2,128,256]{2,1,0:T(8,128)}, u32[]{:S(2)}) copy-start(f32[2,128,256]{2,1,0:T(8,128)} %state_ref.1) | copy-start | bytes 786436
  2.5 15.6 %copy-start.2 = (f32[1,8192]{1,0:T(1,128)S(1)}, f32[1,8192]{1,0:T(1,128)}, u32[]{:S(2)}) copy-start(f32[1,8192]{1,0:T(1,128)} %param.12) | copy-start | bytes 98308
  2.5 15.6 %copy-start.3 = (f32[2,1,8192]{2,1,0:T(1,128)S(1)}, f32[2,1,8192]{2,1,0:T(1,128)}, u32[]{:S(2)}) copy-start(f32[2,1,8192]{2,1,0:T(1,128)} %param.11) | copy-start | bytes 196612
  20.8 13.2 %copy-start.4 = (s32[1,1,8,256]{3,2,1,0:T(8,128)S(1)}, s32[1,1,8,256]{3,2,1,0:T(8,128)}, u32[]{:S(2)}) copy-start(s32[1,1,8,256]{3,2,1,0:T(8,128)} %param.13) | copy-start | bytes 24580
  59.3 12.0 %all-to-all-start.4 = ((f32[416,1,128]{2,1,0:T(1,128)}), f32[416,1,128]{2,1,0:T(1,128)S(1)}, u32[]{:S(2)}, u32[]{:S(2)}) async-start(f32[416,1,128]{2,1,0:T(1,128)} %get-tuple-element.31), calls=%async_computation.4 | async-start | bytes 425984 | tf_op jit(solution)/shard_map/all_to_all | solution.py:784

commit v7 on v6

--- a/solution.py
+++ b/solution.py
@@ -250,7 +250,7 @@
         put_rows(out_ref, (here + 1) * size, right)
 
 
-def chebyshev(in_ref, q_ref, inv_ref, p_ref, target, scratch, groups, members, size):
+def chebyshev(in_ref, q_ref, inv_ref, p_ref, target, scratch, groups, members, size, ready=None):
     q_ext, inv_ext, p_ext, update_ref, even_ref, odd_ref = scratch
     rows, columns = target.shape
     halves = columns // LANES
@@ -393,6 +393,8 @@
                 else:
                     update_ref[c, at, :] = update
                     keep(next_ref, c, r, mids[c] + update)
+            if final and ready is not None:
+                ready(r + 1)
         ratio_now = ratio_next
         now_ref, next_ref = next_ref, now_ref
 
@@ -428,11 +430,6 @@
     for copy in copies:
         copy.start()
     copies[0].wait()
-    for o in range(members):
-        row, col = cell_parts(cell_ref[o : o + 1, :], columns)
-        at = slice(o * width, (o + 1) * width)
-        hot_ref[:, at] = one_hot(col, columns)
-        row_hot_ref[:, at] = one_hot(row, rows)
     copies[1].wait()
     table = table_of([state_ref[0], state_ref[1]])
     for copy in copies[2:]:
@@ -442,8 +439,12 @@
     whole = jnp.concatenate([frac, load_segs(frac_ref, 1)], axis=0)
     for o in range(members):
         one = slice(o, o + 1)
-        row, _ = cell_parts(cell_ref[one, :], columns)
-        cell_p, cell_s = pick(table, 2, rows, row, hot_ref[:, o * width : (o + 1) * width])
+        at = slice(o * width, (o + 1) * width)
+        row, col = cell_parts(cell_ref[one, :], columns)
+        hot = one_hot(col, columns)
+        hot_ref[:, at] = hot
+        row_hot_ref[:, at] = one_hot(row, rows)
+        cell_p, cell_s = pick(table, 2, rows, row, hot)
         live = iota((1, width), 1) < count_ref[0, o]
         out_ref[o, ROW_SEG : ROW_SEG + 1, :] = seg_ref[one, :].astype(F32)
         out_ref[o, ROW_TRANS : ROW_TRANS + 1, :] = jnp.where(live, trans_ref[one, :], 0.0)
@@ -572,19 +573,23 @@
     groups, members, size, halo_ref, cell_ref, hot_ref, row_hot_ref, sent_ref, kept_ref, perm_ref,
     out_ref, keep_ref, slots_ref, left_ref, *scratch,
 ):
+    saturation = kept_ref[1]
+    g = lax.axis_index("grp")
+
+    def put_s(o, cell_s):
+        slots_ref[o, 1:2, :] = cell_s
+
+    cell_gather(members, cell_ref, hot_ref, [saturation], put_s)
     chebyshev(
         halo_ref, kept_ref.at[2], kept_ref.at[3], kept_ref.at[0], keep_ref.at[0], scratch, groups, members, size
     )
     pressure = keep_ref[0]
-    saturation = kept_ref[1]
-    g = lax.axis_index("grp")
-
-    def put(o, cell_p, cell_s):
+
+    def put_p(o, cell_p):
         slots_ref[o, 0:1, :] = cell_p
-        slots_ref[o, 1:2, :] = cell_s
-        send_slots(out_ref, (g * members + o) * size, cell_p, cell_s)
-
-    cell_gather(members, cell_ref, hot_ref, [pressure, saturation], put)
+        send_slots(out_ref, (g * members + o) * size, cell_p, slots_ref[o, 1:2, :])
+
+    cell_gather(members, cell_ref, hot_ref, [pressure], put_p)
     new_saturation, q, inv = cell_update(
         members,
         1,
@@ -677,7 +682,7 @@
 
 def source_last_kernel(
     groups, members, size, hot_ref, row_hot_ref, sent_ref, own_ref, seg_ref, pressure_ref, kept_ref, perm_ref,
-    out_ref, keep_ref, left_ref,
+    out_any, keep_ref, left_ref, out_ref, sem,
 ):
     pressure = pressure_ref[...]
     new_saturation, q, inv = cell_update(
@@ -697,6 +702,16 @@
     keep_ref[1] = q
     keep_ref[2] = inv
     send_halo(out_ref, q, inv, pressure, groups, members, size)
+    g, f = lax.axis_index("grp"), lax.axis_index("frac")
+    runs = []
+    for i, step in enumerate((-1, 0, 1)):
+        at = jnp.clip((g + step) * members + f - 1, 0, groups * members - 3) * size
+        run = pltpu.make_async_copy(out_ref.at[pl.ds(at, 3 * size)], out_any.at[pl.ds(at, 3 * size)], sem.at[i])
+        runs.append(((g + step >= 0) & (g + step < groups), run))
+    for inside, run in runs:
+        pl.when(inside)(run.start)
+    for inside, run in runs:
+        pl.when(inside)(run.wait)
 
 
 def owner_last_kernel(
@@ -720,24 +735,36 @@
     store_segs(out_ref, 1, new_sat)
 
 
-def final_kernel(groups, members, size, halo_ref, pressure_ref, kept_ref, out_ref, *scratch):
+def final_kernel(groups, members, size, halo_ref, pressure_ref, kept_ref, out_any, new_ref, sem, *scratch):
+    rows = pressure_ref.shape[0]
+    chunk = rows // 2
+    copies = [pltpu.make_async_copy(kept_ref.at[0], out_any.at[1], sem.at[0])]
+    copies[0].start()
+
+    def ready(tiles):
+        if tiles * SUB % chunk == 0:
+            at = pl.ds(tiles * SUB - chunk, chunk)
+            copies.append(pltpu.make_async_copy(new_ref.at[at], out_any.at[0, at], sem.at[len(copies)]))
+            copies[-1].start()
+
     chebyshev(
-        halo_ref, kept_ref.at[1], kept_ref.at[2], pressure_ref, out_ref.at[0], scratch, groups, members, size
-    )
-    out_ref[1] = kept_ref[0]
+        halo_ref, kept_ref.at[1], kept_ref.at[2], pressure_ref, new_ref, scratch, groups, members, size, ready
+    )
+    for copy in copies:
+        copy.wait()
 
 
 VMEM = pl.BlockSpec(memory_space=pltpu.VMEM)
 HBM = pl.BlockSpec(memory_space=pltpu.HBM)
 
 
-def call(kernel, statics, outs, scratch, *args, spec=VMEM):
+def call(kernel, statics, outs, scratch, *args, spec=VMEM, away=()):
     outs = [o if hasattr(o, "dtype") else jax.ShapeDtypeStruct(o, F32) for o in outs]
     return pl.pallas_call(
         functools.partial(kernel, *statics),
         out_shape=outs,
         in_specs=[spec] * len(args),
-        out_specs=[VMEM] * len(outs),
+        out_specs=[HBM if i in away else VMEM for i in range(len(outs))],
         scratch_shapes=scratch,
         compiler_params=pltpu.CompilerParams(vmem_limit_bytes=32 * 1024 * 1024),
         name=kernel.__name__,
@@ -828,14 +855,25 @@
     )
     segs = to_group(own)
     edge, kept = call(
-        source_last_kernel, both, [halo, (3, rows, columns)], [left_cell],
+        source_last_kernel,
+        both,
+        [halo, (3, rows, columns)],
+        [left_cell, pltpu.VMEM(halo, F32), pltpu.SemaphoreType.DMA((3,))],
         cell_hot, cell_row_hot, sent, own, segs, pressure, kept, matrix_perm,
+        away=(0,),
     )
     around = to_all(edge)
     (frac3,) = call(
         owner_last_kernel, (members,), [frac.shape], [left_seg], slot, hot, row_hot, own, segs, frac2, aperture
     )
-    (matrix_out,) = call(final_kernel, both, [matrix_state.shape], ext, around, pressure, kept)
+    (matrix_out,) = call(
+        final_kernel,
+        both,
+        [matrix_state.shape],
+        [pltpu.VMEM((rows, columns), F32), pltpu.SemaphoreType.DMA((3,))] + ext,
+        around, pressure, kept,
+        away=(0,),
+    )
     return matrix_out, frac3.reshape(frac_state.shape)
 
 

time: 73 us -> 73 us (level)
  no operation moved by 1% of the time
where the time goes in v7:
time: 73 us; the launch traced here: 72.6 us
  blocking collectives  47.8 us (65%)
  Pallas kernels  13.1 us (18%)
  waiting for transfers between devices  8.27 us (11%)
  starting transfers between devices  2.6 us (4%)
    all_to_all x2, blocking collectives, to_all(): lax.all_to_all(x, ('grp', 'frac'), split_axis=0, concat_axis=0, tiled=True)  24.9 us
    all_to_all x2, blocking collectives, to_group(): return lax.all_to_all(x, 'frac', split_axis=0, concat_axis=0, tiled=True)  22.9 us
    pallas_call x7, Pallas kernels, call(): pl.pallas_call(functools.partial(kernel, *statics), out_shape=outs, in_sp...  13.1 us
    all_to_all x1, waiting for transfers between devices, to_all(): lax.all_to_all(x, ('grp', 'frac'), split_axis=0, concat_axis=0, tiled=True)  8.27 us
    all_to_all x1, starting transfers between devices, to_all(): lax.all_to_all(x, ('grp', 'frac'), split_axis=0, concat_axis=0, tiled=True)  2.6 us
  transfers between devices with their start and end apart: 1, of which 1 were waited for; matrix products, arithmetic and copies ran while one was open for 0% of the time, Pallas kernels for 2%

profile of v7, /device:TPU:0, one launch (start us, length us, event | category | flops | bytes accessed | tf_op | source)
XLA Modules:
  0.0 72.6 jit_solution(17184977145542999124)
XLA Ops:
  0.6 2.0 %first_kernel.1 = (f32[8,72,256]{2,1,0:T(8,128)S(1)}, bf16[256,2048]{1,0:T(8,128)(2,1)S(1)}, bf16[128,2048]{1,0:T(8,128)(2,1)S(1)}) custom-call(s32[8,256]{1,0:T(8,128)} %bitcast.13, s32[8,256]{1,0:T(8,128)} %bitcast.18, f32[8,256]{1,0:T(8,128)} %bitcast.19, s32[1,8]{1,0:T(1,128)} %bitcast.20, s32[3,8,256]{2,1,0:T(8,128)} %bitcast.17, ...), custom_call_target="tpu_custom_call" | custom-call | tf_op jit(solution)/shard_map/first_kernel/pallas_call | solution.py:763
  2.6 0.0 copy-start
  2.6 0.0 copy-start.1
  2.6 0.0 copy-start.2
  2.6 0.0 copy-start.3
  2.7 15.5 %all_to_all.25.slot_ref = f32[8,72,256]{2,1,0:T(8,128)S(1)} all-to-all(f32[8,72,256]{2,1,0:T(8,128)S(1)} %get-tuple-element.20.sent_ref), channel_id=1, replica_groups=mesh['grp'=4,'frac'=8] {'frac'}, dimensions={0} | all-to-all | bytes 1179648 | tf_op jit(solution)/shard_map/all_to_all | solution.py:808
  18.2 0.0 copy-done
  18.2 0.0 copy-done.1
  18.2 0.0 copy-done.2
  18.2 0.0 copy-done.3
  18.2 2.7 %start_kernel.1 = (f32[416,1,128]{2,1,0:T(1,128)S(1)}, f32[4,128,256]{2,1,0:T(8,128)S(1)}, f32[8,2,256]{2,1,0:T(2,128)S(1)}, f32[2,32,256]{2,1,0:T(8,128)S(1)}, ...) custom-call(f32[8,72,256]{2,1,0:T(8,128)S(1)} %all_to_all.25.slot_ref, ...), custom_call_target="tpu_custom_call" | custom-call | tf_op jit(solution)/shard_map/start_kernel/pallas_call | solution.py:763
  20.9 0.0 copy-start.4
  20.9 13.2 %all_to_all.26.halo_ref.ends_ref = f32[416,1,128]{2,1,0:T(1,128)S(1)} all-to-all(f32[416,1,128]{2,1,0:T(1,128)S(1)} %get-tuple-element.21), channel_id=1, replica_groups=mesh['grp'=4,'frac'=8] {'grp','frac'}, dimensions={0} | all-to-all | bytes 425984 | tf_op jit(solution)/shard_map/all_to_all | solution.py:811
  34.1 0.0 copy-done.4
  34.1 2.3 %middle_kernel.1 = (f32[416,1,128]{2,1,0:T(1,128)S(1)}, f32[4,128,256]{2,1,0:T(8,128)S(1)}) custom-call(f32[416,1,128]{2,1,0:T(1,128)S(1)} %all_to_all.26.halo_ref.ends_ref, s32[8,256]{1,0:T(8,128)S(1)} %bitcast.14, bf16[256,2048]{1,0:T(8,128)(2,1)S(1)} %get-tuple-element.18.cell_hot_ref.hot_ref, ...), custom_call_target="tpu_custom_call" | custom-call | tf_op jit(solution)/shard_map/middle_kernel/pallas_call | solution.py:763
  36.4 11.7 %all_to_all.27.halo_ref = f32[416,1,128]{2,1,0:T(1,128)S(1)} all-to-all(f32[416,1,128]{2,1,0:T(1,128)S(1)} %get-tuple-element.23), channel_id=1, replica_groups=mesh['grp'=4,'frac'=8] {'grp','frac'}, dimensions={0} | all-to-all | bytes 425984 | tf_op jit(solution)/shard_map/all_to_all | solution.py:811
  48.1 1.9 %exchange_kernel.1 = (f32[8,8,256]{2,1,0:T(8,128)S(1)}, f32[2,32,256]{2,1,0:T(8,128)S(1)}, f32[128,256]{1,0:T(8,128)S(1)}) custom-call(f32[416,1,128]{2,1,0:T(1,128)S(1)} %all_to_all.27.halo_ref, s32[8,256]{1,0:T(8,128)S(1)} %bitcast.15, bf16[256,2048]{1,0:T(8,128)(2,1)S(1)} %get-tuple-element.18.cell_hot_ref.hot_ref, ...), custom_call_target="tpu_custom_call" | custom-call | tf_op jit(solution)/shard_map/exchange_kernel/pallas_call | solution.py:763
  50.0 7.4 %all_to_all.28.seg_ref = f32[8,8,256]{2,1,0:T(8,128)S(1)} all-to-all(f32[8,8,256]{2,1,0:T(8,128)S(1)} %get-tuple-element.29.own_ref), channel_id=1, replica_groups=mesh['grp'=4,'frac'=8] {'frac'}, dimensions={0} | all-to-all | bytes 131072 | tf_op jit(solution)/shard_map/all_to_all | solution.py:808
  57.4 1.8 %source_last_kernel.1 = (f32[416,1,128]{2,1,0:T(1,128)}, f32[3,128,256]{2,1,0:T(8,128)S(1)}) custom-call(bf16[256,2048]{1,0:T(8,128)(2,1)S(1)} %get-tuple-element.18.cell_hot_ref.hot_ref, bf16[128,2048]{1,0:T(8,128)(2,1)S(1)} %get-tuple-element.19.cell_row_hot_ref.row_hot_ref, f32[8,72,256]{2,1,0:T(8,128)S(1)} %get-tuple-element.20.sent_ref, ...), custom_call_target="tpu_custom_call" | custom-call | tf_op jit(solution)/shard_map/source_last_kernel/pallas_call | solution.py:763
  59.2 2.6 %all-to-all-start.4 = ((f32[416,1,128]{2,1,0:T(1,128)}), f32[416,1,128]{2,1,0:T(1,128)S(1)}, u32[]{:S(2)}, u32[]{:S(2)}) async-start(f32[416,1,128]{2,1,0:T(1,128)} %get-tuple-element.31), calls=%async_computation.4 | async-start | bytes 425984 | tf_op jit(solution)/shard_map/all_to_all | solution.py:811
  61.8 1.1 %owner_last_kernel.1 = f32[2,64,128]{2,1,0:T(8,128)} custom-call(f32[8,72,256]{2,1,0:T(8,128)S(1)} %all_to_all.25.slot_ref, bf16[256,2048]{1,0:T(8,128)(2,1)S(1)} %get-tuple-element.24.hot_ref, bf16[32,2048]{1,0:T(8,128)(2,1)S(1)} %get-tuple-element.25.row_hot_ref, f32[8,8,256]{2,1,0:T(8,128)S(1)} %get-tuple-element.29.own_ref, ...), custom_call_target="tpu_custom_call" | custom-call | tf_op jit(solution)/shard_map/owner_last_kernel/pallas_call | solution.py:763
  63.0 8.3 %all-to-all-done.4.halo_ref = f32[416,1,128]{2,1,0:T(1,128)S(1)} async-done(((f32[416,1,128]{2,1,0:T(1,128)}), f32[416,1,128]{2,1,0:T(1,128)S(1)}, u32[]{:S(2)}, u32[]{:S(2)}) %all-to-all-start.4) | async-done | bytes 213024 | tf_op jit(solution)/shard_map/all_to_all | solution.py:811
  71.3 1.3 %final_kernel.1 = f32[2,128,256]{2,1,0:T(8,128)} custom-call(f32[416,1,128]{2,1,0:T(1,128)S(1)} %all-to-all-done.4.halo_ref, f32[128,256]{1,0:T(8,128)S(1)} %get-tuple-element.30.pressure_ref, f32[3,128,256]{2,1,0:T(8,128)S(1)} %get-tuple-element.32.kept_ref), custom_call_target="tpu_custom_call" | custom-call | tf_op jit(solution)/shard_map/final_kernel/pallas_call | solution.py:763
Async XLA Ops:
  2.6 15.6 %copy-start = (f32[128,256]{1,0:T(8,128)S(1)}, f32[128,256]{1,0:T(8,128)}, u32[]{:S(2)}) copy-start(f32[128,256]{1,0:T(8,128)} %perm_ref.5) | copy-start | bytes 393220
  2.6 15.6 %copy-start.1 = (f32[2,128,256]{2,1,0:T(8,128)S(1)}, f32[2,128,256]{2,1,0:T(8,128)}, u32[]{:S(2)}) copy-start(f32[2,128,256]{2,1,0:T(8,128)} %state_ref.1) | copy-start | bytes 786436
  2.6 15.6 %copy-start.2 = (f32[1,8192]{1,0:T(1,128)S(1)}, f32[1,8192]{1,0:T(1,128)}, u32[]{:S(2)}) copy-start(f32[1,8192]{1,0:T(1,128)} %param.12) | copy-start | bytes 98308
  2.6 15.6 %copy-start.3 = (f32[2,1,8192]{2,1,0:T(1,128)S(1)}, f32[2,1,8192]{2,1,0:T(1,128)}, u32[]{:S(2)}) copy-start(f32[2,1,8192]{2,1,0:T(1,128)} %param.11) | copy-start | bytes 196612
  20.9 13.2 %copy-start.4 = (s32[1,1,8,256]{3,2,1,0:T(8,128)S(1)}, s32[1,1,8,256]{3,2,1,0:T(8,128)}, u32[]{:S(2)}) copy-start(s32[1,1,8,256]{3,2,1,0:T(8,128)} %param.13) | copy-start | bytes 24580
  59.2 12.0 %all-to-all-start.4 = ((f32[416,1,128]{2,1,0:T(1,128)}), f32[416,1,128]{2,1,0:T(1,128)S(1)}, u32[]{:S(2)}, u32[]{:S(2)}) async-start(f32[416,1,128]{2,1,0:T(1,128)} %get-tuple-element.31), calls=%async_computation.4 | async-start | bytes 425984 | tf_op jit(solution)/shard_map/all_to_all | solution.py:811

commit v8 on v6

--- a/solution.py
+++ b/solution.py
@@ -198,6 +198,7 @@
     turned = jnp.transpose(jnp.where(lane < LANES // 2, low, high))
     left, right = turned[:SUB], turned[LANES - SUB :]
     lane = iota((1, LANES), 1)
+    spare = jnp.where(g + 2 < groups, here + 2 * members, here - 2 * members)
 
     for step in (-1, 1):
         layer = (lambda k: k) if step < 0 else (lambda k: rows - 1 - k)
@@ -210,44 +211,34 @@
         base = here + step * members
         tiles = [slice(h * LANES, (h + 1) * LANES) for h in range(halves)]
 
-        @pl.when(inside)
-        def _():
-            at = base * size
-            for h, tile in enumerate(tiles):
-                put_rows(out_ref, at + h * DEPTH, span(q, DEPTH, tile))
-                put_rows(out_ref, at + halves * DEPTH + h * (DEPTH - 1), span(inv, DEPTH - 1, tile))
-                put_rows(out_ref, at + halves * (2 * DEPTH - 1) + h, span(p, 1, tile))
-            deep, next_p = layer(DEPTH - 1), layer(1)
-            extra = jnp.where(
-                lane == 0,
-                inv[deep : deep + 1, tiles[0]],
+        at = jnp.where(inside, base, spare) * size
+        for h, tile in enumerate(tiles):
+            put_rows(out_ref, at + h * DEPTH, span(q, DEPTH, tile))
+            put_rows(out_ref, at + halves * DEPTH + h * (DEPTH - 1), span(inv, DEPTH - 1, tile))
+            put_rows(out_ref, at + halves * (2 * DEPTH - 1) + h, span(p, 1, tile))
+        deep, next_p = layer(DEPTH - 1), layer(1)
+        extra = jnp.where(
+            lane == 0,
+            inv[deep : deep + 1, tiles[0]],
+            jnp.where(
+                lane == LANES - 1,
+                inv[deep : deep + 1, tiles[-1]],
                 jnp.where(
-                    lane == LANES - 1,
-                    inv[deep : deep + 1, tiles[-1]],
-                    jnp.where(
-                        lane == 1,
-                        pltpu.roll(p[next_p : next_p + 1, tiles[0]], 1, 1),
-                        pltpu.roll(p[next_p : next_p + 1, tiles[-1]], LANES - 1, 1),
-                    ),
+                    lane == 1,
+                    pltpu.roll(p[next_p : next_p + 1, tiles[0]], 1, 1),
+                    pltpu.roll(p[next_p : next_p + 1, tiles[-1]], LANES - 1, 1),
                 ),
-            )
-            out_ref[at + halves * 2 * DEPTH] = extra
+            ),
+        )
+        out_ref[at + halves * 2 * DEPTH] = extra
 
         for side, tile, there in ((-1, tiles[0], f > 0), (1, tiles[-1], f < members - 1)):
-
-            @pl.when(inside & there)
-            def _(side=side, tile=tile):
-                at = (base + side) * size
-                for i, field in enumerate((q, inv, p)):
-                    put_rows(out_ref, at + i * DEPTH, span(field, DEPTH, tile))
-
-    @pl.when(f > 0)
-    def _():
-        put_rows(out_ref, (here - 1) * size, left)
-
-    @pl.when(f < members - 1)
-    def _():
-        put_rows(out_ref, (here + 1) * size, right)
+            at = jnp.where(inside & there, base + side, spare) * size
+            for i, field in enumerate((q, inv, p)):
+                put_rows(out_ref, at + i * DEPTH, span(field, DEPTH, tile))
+
+    put_rows(out_ref, jnp.where(f > 0, here - 1, spare) * size, left)
+    put_rows(out_ref, jnp.where(f < members - 1, here + 1, spare) * size, right)
 
 
 def chebyshev(in_ref, q_ref, inv_ref, p_ref, target, scratch, groups, members, size):
@@ -572,19 +563,23 @@
     groups, members, size, halo_ref, cell_ref, hot_ref, row_hot_ref, sent_ref, kept_ref, perm_ref,
     out_ref, keep_ref, slots_ref, left_ref, *scratch,
 ):
+    saturation = kept_ref[1]
+    g = lax.axis_index("grp")
+
+    def put_s(o, cell_s):
+        slots_ref[o, 1:2, :] = cell_s
+
+    cell_gather(members, cell_ref, hot_ref, [saturation], put_s)
     chebyshev(
         halo_ref, kept_ref.at[2], kept_ref.at[3], kept_ref.at[0], keep_ref.at[0], scratch, groups, members, size
     )
     pressure = keep_ref[0]
-    saturation = kept_ref[1]
-    g = lax.axis_index("grp")
-
-    def put(o, cell_p, cell_s):
+
+    def put_p(o, cell_p):
         slots_ref[o, 0:1, :] = cell_p
-        slots_ref[o, 1:2, :] = cell_s
-        send_slots(out_ref, (g * members + o) * size, cell_p, cell_s)
-
-    cell_gather(members, cell_ref, hot_ref, [pressure, saturation], put)
+        send_slots(out_ref, (g * members + o) * size, cell_p, slots_ref[o, 1:2, :])
+
+    cell_gather(members, cell_ref, hot_ref, [pressure], put_p)
     new_saturation, q, inv = cell_update(
         members,
         1,

time: 73 us -> 72.7 us (level)
  no operation moved by 1% of the time
where the time goes in v8:
time: 72.7 us; the launch traced here: 72.3 us
  blocking collectives  47.9 us (66%)
  Pallas kernels  12.8 us (18%)
  waiting for transfers between devices  8.28 us (11%)
  starting transfers between devices  2.58 us (4%)
    all_to_all x2, blocking collectives, to_all(): lax.all_to_all(x, ('grp', 'frac'), split_axis=0, concat_axis=0, tiled=True)  24.9 us
    all_to_all x2, blocking collectives, to_group(): return lax.all_to_all(x, 'frac', split_axis=0, concat_axis=0, tiled=True)  22.9 us
    pallas_call x7, Pallas kernels, call(): pl.pallas_call(functools.partial(kernel, *statics), out_shape=outs, in_sp...  12.8 us
    all_to_all x1, waiting for transfers between devices, to_all(): lax.all_to_all(x, ('grp', 'frac'), split_axis=0, concat_axis=0, tiled=True)  8.28 us
    all_to_all x1, starting transfers between devices, to_all(): lax.all_to_all(x, ('grp', 'frac'), split_axis=0, concat_axis=0, tiled=True)  2.58 us
  transfers between devices with their start and end apart: 1, of which 1 were waited for; matrix products, arithmetic and copies ran while one was open for 0% of the time, Pallas kernels for 2%

profile of v8, /device:TPU:0, one launch (start us, length us, event | category | flops | bytes accessed | tf_op | source)
XLA Modules:
  0.0 72.3 jit_solution(7144915727415674785)
XLA Ops:
  0.6 1.9 %first_kernel.1 = (f32[8,72,256]{2,1,0:T(8,128)S(1)}, bf16[256,2048]{1,0:T(8,128)(2,1)S(1)}, bf16[128,2048]{1,0:T(8,128)(2,1)S(1)}) custom-call(s32[8,256]{1,0:T(8,128)} %bitcast.13, s32[8,256]{1,0:T(8,128)} %bitcast.18, f32[8,256]{1,0:T(8,128)} %bitcast.19, s32[1,8]{1,0:T(1,128)} %bitcast.20, s32[3,8,256]{2,1,0:T(8,128)} %bitcast.17, ...), custom_call_target="tpu_custom_call" | custom-call | tf_op jit(solution)/shard_map/first_kernel/pallas_call | solution.py:731
  2.5 0.0 copy-start
  2.5 0.0 copy-start.1
  2.5 0.0 copy-start.2
  2.5 0.0 copy-start.3
  2.6 15.5 %all_to_all.25.slot_ref = f32[8,72,256]{2,1,0:T(8,128)S(1)} all-to-all(f32[8,72,256]{2,1,0:T(8,128)S(1)} %get-tuple-element.20.sent_ref), channel_id=1, replica_groups=mesh['grp'=4,'frac'=8] {'frac'}, dimensions={0} | all-to-all | bytes 1179648 | tf_op jit(solution)/shard_map/all_to_all | solution.py:776
  18.1 0.0 copy-done
  18.1 0.0 copy-done.1
  18.1 0.0 copy-done.2
  18.1 0.0 copy-done.3
  18.1 2.6 %start_kernel.1 = (f32[416,1,128]{2,1,0:T(1,128)S(1)}, f32[4,128,256]{2,1,0:T(8,128)S(1)}, f32[8,2,256]{2,1,0:T(2,128)S(1)}, f32[2,32,256]{2,1,0:T(8,128)S(1)}, ...) custom-call(f32[8,72,256]{2,1,0:T(8,128)S(1)} %all_to_all.25.slot_ref, ...), custom_call_target="tpu_custom_call" | custom-call | tf_op jit(solution)/shard_map/start_kernel/pallas_call | solution.py:731
  20.7 0.0 copy-start.4
  20.7 13.2 %all_to_all.26.halo_ref.ends_ref = f32[416,1,128]{2,1,0:T(1,128)S(1)} all-to-all(f32[416,1,128]{2,1,0:T(1,128)S(1)} %get-tuple-element.21), channel_id=1, replica_groups=mesh['grp'=4,'frac'=8] {'grp','frac'}, dimensions={0} | all-to-all | bytes 425984 | tf_op jit(solution)/shard_map/all_to_all | solution.py:779
  33.9 0.0 copy-done.4
  33.9 2.2 %middle_kernel.1 = (f32[416,1,128]{2,1,0:T(1,128)S(1)}, f32[4,128,256]{2,1,0:T(8,128)S(1)}) custom-call(f32[416,1,128]{2,1,0:T(1,128)S(1)} %all_to_all.26.halo_ref.ends_ref, s32[8,256]{1,0:T(8,128)S(1)} %bitcast.14, bf16[256,2048]{1,0:T(8,128)(2,1)S(1)} %get-tuple-element.18.cell_hot_ref.hot_ref, ...), custom_call_target="tpu_custom_call" | custom-call | tf_op jit(solution)/shard_map/middle_kernel/pallas_call | solution.py:731
  36.1 11.7 %all_to_all.27.halo_ref = f32[416,1,128]{2,1,0:T(1,128)S(1)} all-to-all(f32[416,1,128]{2,1,0:T(1,128)S(1)} %get-tuple-element.23), channel_id=1, replica_groups=mesh['grp'=4,'frac'=8] {'grp','frac'}, dimensions={0} | all-to-all | bytes 425984 | tf_op jit(solution)/shard_map/all_to_all | solution.py:779
  47.9 1.9 %exchange_kernel.1 = (f32[8,8,256]{2,1,0:T(8,128)S(1)}, f32[2,32,256]{2,1,0:T(8,128)S(1)}, f32[128,256]{1,0:T(8,128)S(1)}) custom-call(f32[416,1,128]{2,1,0:T(1,128)S(1)} %all_to_all.27.halo_ref, s32[8,256]{1,0:T(8,128)S(1)} %bitcast.15, bf16[256,2048]{1,0:T(8,128)(2,1)S(1)} %get-tuple-element.18.cell_hot_ref.hot_ref, ...), custom_call_target="tpu_custom_call" | custom-call | tf_op jit(solution)/shard_map/exchange_kernel/pallas_call | solution.py:731
  49.8 7.4 %all_to_all.28.seg_ref = f32[8,8,256]{2,1,0:T(8,128)S(1)} all-to-all(f32[8,8,256]{2,1,0:T(8,128)S(1)} %get-tuple-element.29.own_ref), channel_id=1, replica_groups=mesh['grp'=4,'frac'=8] {'frac'}, dimensions={0} | all-to-all | bytes 131072 | tf_op jit(solution)/shard_map/all_to_all | solution.py:776
  57.2 1.8 %source_last_kernel.1 = (f32[416,1,128]{2,1,0:T(1,128)}, f32[3,128,256]{2,1,0:T(8,128)S(1)}) custom-call(bf16[256,2048]{1,0:T(8,128)(2,1)S(1)} %get-tuple-element.18.cell_hot_ref.hot_ref, bf16[128,2048]{1,0:T(8,128)(2,1)S(1)} %get-tuple-element.19.cell_row_hot_ref.row_hot_ref, f32[8,72,256]{2,1,0:T(8,128)S(1)} %get-tuple-element.20.sent_ref, ...), custom_call_target="tpu_custom_call" | custom-call | tf_op jit(solution)/shard_map/source_last_kernel/pallas_call | solution.py:731
  59.0 2.6 %all-to-all-start.4 = ((f32[416,1,128]{2,1,0:T(1,128)}), f32[416,1,128]{2,1,0:T(1,128)S(1)}, u32[]{:S(2)}, u32[]{:S(2)}) async-start(f32[416,1,128]{2,1,0:T(1,128)} %get-tuple-element.31), calls=%async_computation.4 | async-start | bytes 425984 | tf_op jit(solution)/shard_map/all_to_all | solution.py:779
  61.5 1.1 %owner_last_kernel.1 = f32[2,64,128]{2,1,0:T(8,128)} custom-call(f32[8,72,256]{2,1,0:T(8,128)S(1)} %all_to_all.25.slot_ref, bf16[256,2048]{1,0:T(8,128)(2,1)S(1)} %get-tuple-element.24.hot_ref, bf16[32,2048]{1,0:T(8,128)(2,1)S(1)} %get-tuple-element.25.row_hot_ref, f32[8,8,256]{2,1,0:T(8,128)S(1)} %get-tuple-element.29.own_ref, ...), custom_call_target="tpu_custom_call" | custom-call | tf_op jit(solution)/shard_map/owner_last_kernel/pallas_call | solution.py:731
  62.7 8.3 %all-to-all-done.4.halo_ref = f32[416,1,128]{2,1,0:T(1,128)S(1)} async-done(((f32[416,1,128]{2,1,0:T(1,128)}), f32[416,1,128]{2,1,0:T(1,128)S(1)}, u32[]{:S(2)}, u32[]{:S(2)}) %all-to-all-start.4) | async-done | bytes 213024 | tf_op jit(solution)/shard_map/all_to_all | solution.py:779
  71.0 1.4 %final_kernel.1 = f32[2,128,256]{2,1,0:T(8,128)} custom-call(f32[416,1,128]{2,1,0:T(1,128)S(1)} %all-to-all-done.4.halo_ref, f32[128,256]{1,0:T(8,128)S(1)} %get-tuple-element.30.pressure_ref, f32[3,128,256]{2,1,0:T(8,128)S(1)} %get-tuple-element.32.kept_ref), custom_call_target="tpu_custom_call" | custom-call | tf_op jit(solution)/shard_map/final_kernel/pallas_call | solution.py:731
Async XLA Ops:
  2.5 15.6 %copy-start = (f32[128,256]{1,0:T(8,128)S(1)}, f32[128,256]{1,0:T(8,128)}, u32[]{:S(2)}) copy-start(f32[128,256]{1,0:T(8,128)} %perm_ref.5) | copy-start | bytes 393220
  2.5 15.6 %copy-start.1 = (f32[2,128,256]{2,1,0:T(8,128)S(1)}, f32[2,128,256]{2,1,0:T(8,128)}, u32[]{:S(2)}) copy-start(f32[2,128,256]{2,1,0:T(8,128)} %state_ref.1) | copy-start | bytes 786436
  2.5 15.6 %copy-start.2 = (f32[1,8192]{1,0:T(1,128)S(1)}, f32[1,8192]{1,0:T(1,128)}, u32[]{:S(2)}) copy-start(f32[1,8192]{1,0:T(1,128)} %param.12) | copy-start | bytes 98308
  2.5 15.6 %copy-start.3 = (f32[2,1,8192]{2,1,0:T(1,128)S(1)}, f32[2,1,8192]{2,1,0:T(1,128)}, u32[]{:S(2)}) copy-start(f32[2,1,8192]{2,1,0:T(1,128)} %param.11) | copy-start | bytes 196612
  20.7 13.2 %copy-start.4 = (s32[1,1,8,256]{3,2,1,0:T(8,128)S(1)}, s32[1,1,8,256]{3,2,1,0:T(8,128)}, u32[]{:S(2)}) copy-start(s32[1,1,8,256]{3,2,1,0:T(8,128)} %param.13) | copy-start | bytes 24580
  59.0 12.0 %all-to-all-start.4 = ((f32[416,1,128]{2,1,0:T(1,128)}), f32[416,1,128]{2,1,0:T(1,128)S(1)}, u32[]{:S(2)}, u32[]{:S(2)}) async-start(f32[416,1,128]{2,1,0:T(1,128)} %get-tuple-element.31), calls=%async_computation.4 | async-start | bytes 425984 | tf_op jit(solution)/shard_map/all_to_all | solution.py:779

commit v9 on v8

--- a/solution.py
+++ b/solution.py
@@ -599,10 +599,7 @@
     send_halo(out_ref, q, inv, pressure, groups, members, size)
 
 
-def owner_update(
-    members, t, slot_ref, cell_rows, seg_rows, frac, sat, aperture, ends, hot_ref, row_hot_ref, left_ref
-):
-    rows = frac.shape[0]
+def owner_spread(members, t, slot_ref, cell_rows, seg_rows, row_hot_ref, left_ref):
     for s in range(members):
         cell_p, cell_s = cell_rows(s)
         weight, water = flow(
@@ -613,7 +610,13 @@
             *seg_rows(s),
         )
         spread(left_ref, row_hot_ref, s, [weight * cell_p, weight, water])
-    inflow, total, gained = gathered_sum(left_ref, hot_ref, 3, rows)
+
+
+def owner_update(
+    members, t, slot_ref, cell_rows, seg_rows, frac, sat, aperture, ends, hot_ref, row_hot_ref, left_ref
+):
+    owner_spread(members, t, slot_ref, cell_rows, seg_rows, row_hot_ref, left_ref)
+    inflow, total, gained = gathered_sum(left_ref, hot_ref, 3, frac.shape[0])
     return frac_step(frac, sat, aperture, *ends, inflow, total, gained)
 
 
@@ -622,7 +625,6 @@
     frac_ref, aperture_ref, kept_ref, out_ref, new_ref, pressure_ref, left_ref, *scratch,
 ):
     width = slot_ref.shape[2]
-    rows = frac_ref.shape[1]
     g = lax.axis_index("grp")
 
     def cell_rows(s):
@@ -634,40 +636,39 @@
     before = jnp.where(me > 0, prior[:, LANES - 1 :], 0.0)
     after = jnp.where(me < members - 1, later[:, 0:1], 0.0)
 
-    new_frac, new_sat = owner_update(
+    rows, columns = pressure_ref.shape
+    seg_wide = frac_ref.shape[1]
+    owner_spread(
         members,
         1,
         slot_ref,
         cell_rows,
         lambda s: (own_ref[s, 0:1, :], own_ref[s, 1:2, :]),
-        frac_ref[0],
-        frac_ref[1],
-        load_segs(aperture_ref),
-        (before, after),
-        hot_ref,
         row_hot_ref,
         left_ref,
     )
+    chebyshev(
+        halo_ref, kept_ref.at[2], kept_ref.at[3], kept_ref.at[0], pressure_ref, scratch, groups, members, size
+    )
+    inflow, total, gained = gathered_sum(left_ref, hot_ref, 3, seg_wide)
+    new_frac, new_sat = frac_step(
+        frac_ref[0], frac_ref[1], load_segs(aperture_ref), before, after, inflow, total, gained
+    )
     new_ref[0] = new_frac
     new_ref[1] = new_sat
-    table = table_of([new_frac, new_sat])
+    seg_table = table_of([new_frac, new_sat])
     ends = ends_of(new_frac)
-    for s in range(members):
-        seg_p, seg_s = seg_gather(slot_ref, hot_ref, rows, s, width, table)
-        out_ref[s, 2:3, :] = seg_p
-        out_ref[s, 3:4, :] = seg_s
-        out_ref[s, 4:5, :] = ends
-
-    chebyshev(
-        halo_ref, kept_ref.at[2], kept_ref.at[3], kept_ref.at[0], pressure_ref, scratch, groups, members, size
-    )
-    pressure = pressure_ref[...]
-
-    def put(o, cell_p, cell_s):
+    table = table_of([pressure_ref[...], kept_ref[1]])
+    for o in range(members):
+        at = slice(o * width, (o + 1) * width)
+        row, _ = cell_parts(cell_ref[o : o + 1, :], columns)
+        cell_p, cell_s = pick(table, 2, rows, row, cell_hot_ref[:, at])
         out_ref[o, 0:1, :] = cell_p
         out_ref[o, 1:2, :] = cell_s
-
-    cell_gather(members, cell_ref, cell_hot_ref, [pressure, kept_ref[1]], put)
+        seg_p, seg_s = pick(seg_table, 2, seg_wide, seg_parts(slot_ref, o)[0], hot_ref[:, at])
+        out_ref[o, 2:3, :] = seg_p
+        out_ref[o, 3:4, :] = seg_s
+        out_ref[o, 4:5, :] = ends
 
 
 def source_last_kernel(
@@ -694,8 +695,9 @@
     send_halo(out_ref, q, inv, pressure, groups, members, size)
 
 
-def owner_last_kernel(
-    members, slot_ref, hot_ref, row_hot_ref, own_ref, seg_ref, frac_ref, aperture_ref, out_ref, left_ref
+def final_kernel(
+    groups, members, size, halo_ref, pressure_ref, kept_ref, slot_ref, hot_ref, row_hot_ref, own_ref, seg_ref,
+    frac_ref, aperture_ref, out_ref, new_ref, left_ref, *scratch,
 ):
     new_frac, new_sat = owner_update(
         members,
@@ -711,11 +713,8 @@
         row_hot_ref,
         left_ref,
     )
-    store_segs(out_ref, 0, new_frac)
-    store_segs(out_ref, 1, new_sat)
-
-
-def final_kernel(groups, members, size, halo_ref, pressure_ref, kept_ref, out_ref, *scratch):
+    store_segs(new_ref, 0, new_frac)
+    store_segs(new_ref, 1, new_sat)
     chebyshev(
         halo_ref, kept_ref.at[1], kept_ref.at[2], pressure_ref, out_ref.at[0], scratch, groups, members, size
     )
@@ -827,10 +826,13 @@
         cell_hot, cell_row_hot, sent, own, segs, pressure, kept, matrix_perm,
     )
     around = to_all(edge)
-    (frac3,) = call(
-        owner_last_kernel, (members,), [frac.shape], [left_seg], slot, hot, row_hot, own, segs, frac2, aperture
-    )
-    (matrix_out,) = call(final_kernel, both, [matrix_state.shape], ext, around, pressure, kept)
+    matrix_out, frac3 = call(
+        final_kernel,
+        both,
+        [matrix_state.shape, frac.shape],
+        [left_seg] + ext,
+        around, pressure, kept, slot, hot, row_hot, own, segs, frac2, aperture,
+    )
     return matrix_out, frac3.reshape(frac_state.shape)
 
 

time: 72.7 us -> 71.1 us (0.978)
  blocking collectives: 47.9 us -> 59 us
  waiting for transfers between devices: 8.28 us -> 0 us
  starting transfers between devices: 2.58 us -> 0 us
  Pallas kernels: 12.8 us -> 11.1 us
    all_to_all x2 -> x3, blocking collectives: 24.9 us -> 36.1 us  [to_all(): lax.all_to_all(x, ('grp', 'frac'), split_axis=0, concat_axis=0, tiled=True)]
    all_to_all x1 -> x0, waiting for transfers between devices: 8.28 us -> none  [to_all(): lax.all_to_all(x, ('grp', 'frac'), split_axis=0, concat_axis=0, tiled=True)]
    all_to_all x1 -> x0, starting transfers between devices: 2.58 us -> none  [to_all(): lax.all_to_all(x, ('grp', 'frac'), split_axis=0, concat_axis=0, tiled=True)]
    pallas_call x7 -> x6, Pallas kernels: 12.8 us -> 11.1 us  [call(): pl.pallas_call(functools.partial(kernel, *statics), out_shape=outs, in_sp...]
  transfers between devices with their start and end apart: 1 -> 0, of which waited for: 1 -> 0; matrix products, arithmetic and copies ran while one was open for 0% -> 0% of each run, Pallas kernels for 2% -> 0%
where the time goes in v9:
time: 71.1 us; the launch traced here: 70.8 us
  blocking collectives  59 us (83%)
  Pallas kernels  11.1 us (16%)
  between operations  0.72 us (1%)
    all_to_all x3, blocking collectives, to_all(): lax.all_to_all(x, ('grp', 'frac'), split_axis=0, concat_axis=0, tiled=True)  36.1 us
    all_to_all x2, blocking collectives, to_group(): return lax.all_to_all(x, 'frac', split_axis=0, concat_axis=0, tiled=True)  22.9 us
    pallas_call x6, Pallas kernels, call(): pl.pallas_call(functools.partial(kernel, *statics), out_shape=outs, in_sp...  11.1 us

profile of v9, /device:TPU:0, one launch (start us, length us, event | category | flops | bytes accessed | tf_op | source)
XLA Modules:
  0.0 70.8 jit_solution(6716750444263917549)
XLA Ops:
  0.6 1.9 %first_kernel.1 = (f32[8,72,256]{2,1,0:T(8,128)S(1)}, bf16[256,2048]{1,0:T(8,128)(2,1)S(1)}, bf16[128,2048]{1,0:T(8,128)(2,1)S(1)}) custom-call(s32[8,256]{1,0:T(8,128)} %bitcast.13, s32[8,256]{1,0:T(8,128)} %bitcast.17, f32[8,256]{1,0:T(8,128)} %bitcast.18, s32[1,8]{1,0:T(1,128)} %bitcast.19, s32[3,8,256]{2,1,0:T(8,128)} %bitcast.16, ...), custom_call_target="tpu_custom_call" | custom-call | tf_op jit(solution)/shard_map/first_kernel/pallas_call | solution.py:730
  2.5 0.0 copy-start
  2.5 0.0 copy-start.1
  2.5 0.0 copy-start.2
  2.5 0.0 copy-start.3
  2.6 15.5 %all_to_all.25.slot_ref = f32[8,72,256]{2,1,0:T(8,128)S(1)} all-to-all(f32[8,72,256]{2,1,0:T(8,128)S(1)} %get-tuple-element.22.sent_ref), channel_id=1, replica_groups=mesh['grp'=4,'frac'=8] {'frac'}, dimensions={0} | all-to-all | bytes 1179648 | tf_op jit(solution)/shard_map/all_to_all | solution.py:775
  18.1 0.0 copy-done
  18.1 0.0 copy-done.1
  18.1 0.0 copy-done.2
  18.1 0.0 copy-done.3
  18.1 2.6 %start_kernel.1 = (f32[416,1,128]{2,1,0:T(1,128)S(1)}, f32[4,128,256]{2,1,0:T(8,128)S(1)}, f32[8,2,256]{2,1,0:T(2,128)S(1)}, f32[2,32,256]{2,1,0:T(8,128)S(1)}, ...) custom-call(f32[8,72,256]{2,1,0:T(8,128)S(1)} %all_to_all.25.slot_ref, ...), custom_call_target="tpu_custom_call" | custom-call | tf_op jit(solution)/shard_map/start_kernel/pallas_call | solution.py:730
  20.7 0.0 copy-start.4
  20.7 13.2 %all_to_all.26.halo_ref.ends_ref = f32[416,1,128]{2,1,0:T(1,128)S(1)} all-to-all(f32[416,1,128]{2,1,0:T(1,128)S(1)} %get-tuple-element.23), channel_id=1, replica_groups=mesh['grp'=4,'frac'=8] {'grp','frac'}, dimensions={0} | all-to-all | bytes 425984 | tf_op jit(solution)/shard_map/all_to_all | solution.py:778
  33.9 0.0 copy-done.4
  33.9 2.2 %middle_kernel.1 = (f32[416,1,128]{2,1,0:T(1,128)S(1)}, f32[4,128,256]{2,1,0:T(8,128)S(1)}) custom-call(f32[416,1,128]{2,1,0:T(1,128)S(1)} %all_to_all.26.halo_ref.ends_ref, s32[8,256]{1,0:T(8,128)S(1)} %bitcast.14, bf16[256,2048]{1,0:T(8,128)(2,1)S(1)} %get-tuple-element.20.cell_hot_ref.hot_ref, ...), custom_call_target="tpu_custom_call" | custom-call | tf_op jit(solution)/shard_map/middle_kernel/pallas_call | solution.py:730
  36.1 11.7 %all_to_all.27.halo_ref = f32[416,1,128]{2,1,0:T(1,128)S(1)} all-to-all(f32[416,1,128]{2,1,0:T(1,128)S(1)} %get-tuple-element.25), channel_id=1, replica_groups=mesh['grp'=4,'frac'=8] {'grp','frac'}, dimensions={0} | all-to-all | bytes 425984 | tf_op jit(solution)/shard_map/all_to_all | solution.py:778
  47.9 1.8 %exchange_kernel.1 = (f32[8,8,256]{2,1,0:T(8,128)S(1)}, f32[2,32,256]{2,1,0:T(8,128)S(1)}, f32[128,256]{1,0:T(8,128)S(1)}) custom-call(f32[416,1,128]{2,1,0:T(1,128)S(1)} %all_to_all.27.halo_ref, s32[8,256]{1,0:T(8,128)S(1)} %bitcast.15, bf16[256,2048]{1,0:T(8,128)(2,1)S(1)} %get-tuple-element.20.cell_hot_ref.hot_ref, ...), custom_call_target="tpu_custom_call" | custom-call | tf_op jit(solution)/shard_map/exchange_kernel/pallas_call | solution.py:730
  49.7 7.4 %all_to_all.28.seg_ref = f32[8,8,256]{2,1,0:T(8,128)S(1)} all-to-all(f32[8,8,256]{2,1,0:T(8,128)S(1)} %get-tuple-element.31.own_ref), channel_id=1, replica_groups=mesh['grp'=4,'frac'=8] {'frac'}, dimensions={0} | all-to-all | bytes 131072 | tf_op jit(solution)/shard_map/all_to_all | solution.py:775
  57.1 1.1 %source_last_kernel.1 = (f32[416,1,128]{2,1,0:T(1,128)S(1)}, f32[3,128,256]{2,1,0:T(8,128)S(1)}) custom-call(bf16[256,2048]{1,0:T(8,128)(2,1)S(1)} %get-tuple-element.20.cell_hot_ref.hot_ref, bf16[128,2048]{1,0:T(8,128)(2,1)S(1)} %get-tuple-element.21.cell_row_hot_ref.row_hot_ref, f32[8,72,256]{2,1,0:T(8,128)S(1)} %get-tuple-element.22.sent_ref, ...), custom_call_target="tpu_custom_call" | custom-call | tf_op jit(solution)/shard_map/source_last_kernel/pallas_call | solution.py:730
  58.2 11.2 %all_to_all.29.halo_ref = f32[416,1,128]{2,1,0:T(1,128)S(1)} all-to-all(f32[416,1,128]{2,1,0:T(1,128)S(1)} %get-tuple-element.33), channel_id=1, replica_groups=mesh['grp'=4,'frac'=8] {'grp','frac'}, dimensions={0} | all-to-all | bytes 425984 | tf_op jit(solution)/shard_map/all_to_all | solution.py:778
  69.3 1.5 %final_kernel.1 = (f32[2,128,256]{2,1,0:T(8,128)}, f32[2,64,128]{2,1,0:T(8,128)}) custom-call(f32[416,1,128]{2,1,0:T(1,128)S(1)} %all_to_all.29.halo_ref, f32[128,256]{1,0:T(8,128)S(1)} %get-tuple-element.32.pressure_ref, f32[3,128,256]{2,1,0:T(8,128)S(1)} %get-tuple-element.34.kept_ref, f32[8,72,256]{2,1,0:T(8,128)S(1)} %all_to_all.25.slot_ref, ...), custom_call_target="tpu_custom_call" | custom-call | tf_op jit(solution)/shard_map/final_kernel/pallas_call | solution.py:730
Async XLA Ops:
  2.5 15.6 %copy-start = (f32[128,256]{1,0:T(8,128)S(1)}, f32[128,256]{1,0:T(8,128)}, u32[]{:S(2)}) copy-start(f32[128,256]{1,0:T(8,128)} %perm_ref.5) | copy-start | bytes 393220
  2.5 15.6 %copy-start.1 = (f32[2,128,256]{2,1,0:T(8,128)S(1)}, f32[2,128,256]{2,1,0:T(8,128)}, u32[]{:S(2)}) copy-start(f32[2,128,256]{2,1,0:T(8,128)} %state_ref.1) | copy-start | bytes 786436
  2.5 15.6 %copy-start.2 = (f32[1,8192]{1,0:T(1,128)S(1)}, f32[1,8192]{1,0:T(1,128)}, u32[]{:S(2)}) copy-start(f32[1,8192]{1,0:T(1,128)} %param.12) | copy-start | bytes 98308
  2.5 15.6 %copy-start.3 = (f32[2,1,8192]{2,1,0:T(1,128)S(1)}, f32[2,1,8192]{2,1,0:T(1,128)}, u32[]{:S(2)}) copy-start(f32[2,1,8192]{2,1,0:T(1,128)} %param.11) | copy-start | bytes 196612
  20.7 13.2 %copy-start.4 = (s32[1,1,8,256]{3,2,1,0:T(8,128)S(1)}, s32[1,1,8,256]{3,2,1,0:T(8,128)}, u32[]{:S(2)}) copy-start(s32[1,1,8,256]{3,2,1,0:T(8,128)} %param.13) | copy-start | bytes 24580

commit v10 on v9

--- a/solution.py
+++ b/solution.py
@@ -129,14 +129,37 @@
     return before, after
 
 
-def partial_residual(pressure, couple, source, inverse):
+def partial_residual(pressure, couple, source, inverse, ring):
     rows, columns = pressure.shape
     row, col = iota((rows, columns), 0), iota((rows, columns), 1)
     beside = jnp.where(row == 0, 0.0, pltpu.roll(pressure, 1, 0))
     beside += jnp.where(row == rows - 1, 0.0, pltpu.roll(pressure, rows - 1, 0))
     beside += jnp.where(col == 0, 0.0, pltpu.roll(pressure, 1, 1))
     beside += jnp.where(col == columns - 1, 0.0, pltpu.roll(pressure, columns - 1, 1))
+    if ring is not None:
+        beside += ring
     return inverse * (source - (4.0 + couple) * pressure + beside)
+
+
+def edge_columns(p):
+    rows, columns = p.shape
+    lane = iota((rows, LANES), 1)
+    turned = jnp.transpose(jnp.where(lane < LANES // 2, p[:, :LANES], p[:, columns - LANES :]))
+    return turned[0:1], turned[LANES - 1 : LANES]
+
+
+def ring_of(left, right, columns, members):
+    f = lax.axis_index("frac")
+    rows = left.shape[1]
+    left = jnp.where(f > 0, left, 0.0)
+    right = jnp.where(f < members - 1, right, 0.0)
+    turned = jnp.transpose(jnp.concatenate([left, jnp.zeros((LANES - 2, rows), F32), right], axis=0))
+    lane = iota((rows, LANES), 1)
+    low = jnp.where(lane == 0, turned, 0.0)
+    high = jnp.where(lane == LANES - 1, turned, 0.0)
+    if columns == LANES:
+        return low + high
+    return jnp.concatenate([low] + [jnp.zeros((rows, LANES), F32)] * (columns // LANES - 2) + [high], axis=1)
 
 
 def pack_low(q, inv, p, at, axis):
@@ -158,10 +181,10 @@
     )
 
 
-def block_rows(columns, width):
-    vertical = 2 * DEPTH * (columns // LANES) + 1
-    lateral = SUB + 2 * (width // LANES) + 1
-    return max(vertical, lateral)
+def block_rows(columns, width, closed):
+    vertical = 2 * DEPTH * (columns // LANES)
+    lateral = SUB + 2 * (width // LANES)
+    return max(vertical, lateral) + (0 if closed else 1)
 
 
 def put_rows(out_ref, at, values):
@@ -187,7 +210,7 @@
     ]
 
 
-def send_halo(out_ref, q, inv, p, groups, members, size):
+def send_halo(out_ref, q, inv, p, groups, members, size, closed, ends=None):
     rows, columns = q.shape
     halves = columns // LANES
     g, f = lax.axis_index("grp"), lax.axis_index("frac")
@@ -197,6 +220,10 @@
     high = pack_high(q[:, columns - LANES :], inv[:, columns - LANES :], p[:, columns - LANES :], lane, 1)
     turned = jnp.transpose(jnp.where(lane < LANES // 2, low, high))
     left, right = turned[:SUB], turned[LANES - SUB :]
+    if ends is not None:
+        sub, lane = iota((SUB, LANES), 0), iota((SUB, LANES), 1)
+        left = jnp.where((sub == SUB - 1) & (lane == 1), ends[0], left)
+        right = jnp.where((sub == 0) & (lane == LANES - 2), ends[1], right)
     lane = iota((1, LANES), 1)
     spare = jnp.where(g + 2 < groups, here + 2 * members, here - 2 * members)
 
@@ -216,21 +243,22 @@
             put_rows(out_ref, at + h * DEPTH, span(q, DEPTH, tile))
             put_rows(out_ref, at + halves * DEPTH + h * (DEPTH - 1), span(inv, DEPTH - 1, tile))
             put_rows(out_ref, at + halves * (2 * DEPTH - 1) + h, span(p, 1, tile))
-        deep, next_p = layer(DEPTH - 1), layer(1)
-        extra = jnp.where(
-            lane == 0,
-            inv[deep : deep + 1, tiles[0]],
-            jnp.where(
-                lane == LANES - 1,
-                inv[deep : deep + 1, tiles[-1]],
+        if not closed:
+            deep, next_p = layer(DEPTH - 1), layer(1)
+            extra = jnp.where(
+                lane == 0,
+                inv[deep : deep + 1, tiles[0]],
                 jnp.where(
-                    lane == 1,
-                    pltpu.roll(p[next_p : next_p + 1, tiles[0]], 1, 1),
-                    pltpu.roll(p[next_p : next_p + 1, tiles[-1]], LANES - 1, 1),
+                    lane == LANES - 1,
+                    inv[deep : deep + 1, tiles[-1]],
+                    jnp.where(
+                        lane == 1,
+                        pltpu.roll(p[next_p : next_p + 1, tiles[0]], 1, 1),
+                        pltpu.roll(p[next_p : next_p + 1, tiles[-1]], LANES - 1, 1),
+                    ),
                 ),
-            ),
-        )
-        out_ref[at + halves * 2 * DEPTH] = extra
+            )
+            out_ref[at + halves * 2 * DEPTH] = extra
 
         for side, tile, there in ((-1, tiles[0], f > 0), (1, tiles[-1], f < members - 1)):
             at = jnp.where(inside & there, base + side, spare) * size
@@ -241,7 +269,7 @@
     put_rows(out_ref, jnp.where(f < members - 1, here + 1, spare) * size, right)
 
 
-def chebyshev(in_ref, q_ref, inv_ref, p_ref, target, scratch, groups, members, size):
+def chebyshev(in_ref, q_ref, inv_ref, p_ref, target, scratch, groups, members, size, closed):
     q_ext, inv_ext, p_ext, update_ref, even_ref, odd_ref = scratch
     rows, columns = target.shape
     halves = columns // LANES
@@ -267,11 +295,15 @@
     outer = slice(rows, rows + SUB)
     below, above = taker(1, 0), taker(-1, 0)
     lane = iota((1, LANES), 1)
-    low_extra, high_extra = below(halves * 2 * DEPTH, 1), above(halves * 2 * DEPTH, 1)
+    if not closed:
+        low_extra, high_extra = below(halves * 2 * DEPTH, 1), above(halves * 2 * DEPTH, 1)
     for h in range(halves):
         edge = (lane == 0) & (h == 0) | (lane == LANES - 1) & (h == halves - 1)
 
-        def at_edge(row, turn):
+        def at_edge(high, turn):
+            if closed:
+                return filler(1)
+            row = high_extra if high else low_extra
             return jnp.where(edge, pltpu.roll(row, turn, 1) if turn else row, 0.0)
 
         turn = LANES - 1 if h == 0 else 1
@@ -283,9 +315,9 @@
         inv_ext[h, outer, :] = jnp.concatenate(
             [
                 below(at, DEPTH - 1),
-                at_edge(low_extra, 0),
+                at_edge(False, 0),
                 filler(SUB - 2 * DEPTH),
-                at_edge(high_extra, 0),
+                at_edge(True, 0),
                 above(at, DEPTH - 1),
             ],
             axis=0,
@@ -294,9 +326,9 @@
         p_ext[h, outer, :] = jnp.concatenate(
             [
                 below(at, 1),
-                at_edge(low_extra, turn),
+                at_edge(False, turn),
                 filler(SUB - 4),
-                at_edge(high_extra, turn),
+                at_edge(True, turn),
                 above(at, 1),
             ],
             axis=0,
@@ -348,6 +380,11 @@
 
     for r in range(count):
         at = slice(r * SUB, (r + 1) * SUB)
+        if closed:
+            for c in range(halves + 1):
+                start = q_ext[c, at, :]
+                keep(even_ref, c, r, start / centre if centre != 1.0 else start)
+            continue
         p_side, p_first, p_final = p_ext[side, at, :], p_ext[0, at, :], p_ext[halves - 1, at, :]
         missing = [0.0] * (halves + 1)
         missing[0] += jnp.where(lane == 0, pltpu.roll(p_side, 1, 1), 0.0)
@@ -402,12 +439,13 @@
 ):
     _, rows, columns = state_ref.shape
     width = cell_ref.shape[1]
+    state_rows = [pl.ds(h * rows // 2, rows // 2) for h in range(2)]
     copies = [
         pltpu.make_async_copy(source, target, sem.at[i])
         for i, (source, target) in enumerate(
             [
                 (cell_any, cell_ref),
-                (state_any, state_ref),
+                *[(state_any.at[k, at], state_ref.at[k, at]) for at in state_rows for k in range(2)],
                 (seg_any, seg_ref),
                 (trans_any, trans_ref),
                 (count_any, count_ref),
@@ -419,21 +457,33 @@
     for copy in copies:
         copy.start()
     copies[0].wait()
-    for o in range(members):
+
+    def make_hots(o):
         row, col = cell_parts(cell_ref[o : o + 1, :], columns)
         at = slice(o * width, (o + 1) * width)
         hot_ref[:, at] = one_hot(col, columns)
         row_hot_ref[:, at] = one_hot(row, rows)
-    copies[1].wait()
+
+    early = members // 2
+    for o in range(early):
+        make_hots(o)
+    for copy in copies[1:5]:
+        copy.wait()
     table = table_of([state_ref[0], state_ref[1]])
-    for copy in copies[2:]:
+    for copy in copies[5:]:
         copy.wait()
     frac = load_segs(frac_ref, 0)
     ends = ends_of(frac)
+    left, right = edge_columns(state_ref[0])
+    me = lax.axis_index("frac")
+    to_left = jnp.concatenate([ends[:, :LANES], left], axis=1)
+    to_right = jnp.concatenate([right, ends[:, LANES:]], axis=1)
     whole = jnp.concatenate([frac, load_segs(frac_ref, 1)], axis=0)
     for o in range(members):
         one = slice(o, o + 1)
         row, _ = cell_parts(cell_ref[one, :], columns)
+        if o >= early:
+            make_hots(o)
         cell_p, cell_s = pick(table, 2, rows, row, hot_ref[:, o * width : (o + 1) * width])
         live = iota((1, width), 1) < count_ref[0, o]
         out_ref[o, ROW_SEG : ROW_SEG + 1, :] = seg_ref[one, :].astype(F32)
@@ -442,7 +492,7 @@
             out_ref[o, ROW_UP + t : ROW_UP + t + 1, :] = up_ref[t, one, :].astype(F32)
         out_ref[o, ROW_P : ROW_P + 1, :] = cell_p
         out_ref[o, ROW_S : ROW_S + 1, :] = cell_s
-        out_ref[o, ROW_ENDS : ROW_ENDS + 1, :] = ends
+        out_ref[o, ROW_ENDS : ROW_ENDS + 1, :] = jnp.where(me + 1 == o, to_right, to_left)
         out_ref[o, SUB:, :] = whole
 
 
@@ -464,7 +514,7 @@
 
 
 def cell_update(
-    members, t, hot_ref, row_hot_ref, sent_ref, cell_rows, seg_rows, pressure, saturation, perm, left_ref
+    members, t, hot_ref, row_hot_ref, sent_ref, cell_rows, seg_rows, pressure, saturation, perm, left_ref, ring
 ):
     rows = pressure.shape[0]
     for o in range(members):
@@ -482,7 +532,7 @@
     couple, source, lost = gathered_sum(left_ref, hot_ref, 3, rows)
     inverse = 1.0 / (4.0 + perm + couple)
     new_saturation = saturation - TAU_STEP * lost / (perm + couple)
-    return new_saturation, partial_residual(pressure, couple, source, inverse), inverse
+    return new_saturation, partial_residual(pressure, couple, source, inverse, ring), inverse
 
 
 def start_kernel(
@@ -514,21 +564,19 @@
     new_ref[0] = new_frac
     new_ref[1] = new_sat
     table = table_of([new_frac, new_sat])
-    ends = ends_of(new_frac)
-    ends = jnp.where(iota((1, LANES), 1) < LANES // 2, ends[:, :LANES], ends[:, SEG_COLUMNS - LANES :])
     for s in range(members):
         seg_p, seg_s = seg_gather(slot_ref, hot_ref, rows, s, width, table)
         own_ref[s, 0:1, :] = seg_p
         own_ref[s, 1:2, :] = seg_s
         at = (g * members + s) * size
         send_slots(out_ref, at, seg_p, seg_s)
-        out_ref[at + size - 1] = ends
     for o in range(members):
         row, lane = seg_parts(sent_ref, o)
         table = table_of([slot_ref[o, SUB : SUB + rows, :], slot_ref[o, SUB + rows :, :]])
         seg_p, seg_s = pick(table, 2, rows, row, one_hot(lane, SEG_COLUMNS))
         found_ref[o, 0:1, :] = seg_p
         found_ref[o, 1:2, :] = seg_s
+    me = lax.axis_index("frac")
     pressure = state_ref[0]
     new_saturation, q, inv = cell_update(
         members,
@@ -542,12 +590,19 @@
         state_ref[1],
         perm_ref[...],
         left_ref,
+        ring_of(
+            slot_ref[jnp.maximum(me - 1, 0), ROW_ENDS : ROW_ENDS + 1, :][:, :LANES],
+            slot_ref[jnp.minimum(me + 1, members - 1), ROW_ENDS : ROW_ENDS + 1, :][:, LANES:],
+            state_ref.shape[2],
+            members,
+        ),
     )
     keep_ref[0] = pressure
     keep_ref[1] = new_saturation
     keep_ref[2] = q
     keep_ref[3] = inv
-    send_halo(out_ref, q, inv, pressure, groups, members, size)
+    ends = (new_frac[0:1, 0:1], new_frac[rows - 1 : rows, SEG_COLUMNS - 1 : SEG_COLUMNS])
+    send_halo(out_ref, q, inv, pressure, groups, members, size, True, ends)
 
 
 def cell_gather(members, cell_ref, hot_ref, fields, put):
@@ -560,7 +615,7 @@
 
 
 def middle_kernel(
-    groups, members, size, halo_ref, cell_ref, hot_ref, row_hot_ref, sent_ref, kept_ref, perm_ref,
+    groups, members, size, open_size, halo_ref, cell_ref, hot_ref, row_hot_ref, sent_ref, kept_ref, perm_ref,
     out_ref, keep_ref, slots_ref, left_ref, *scratch,
 ):
     saturation = kept_ref[1]
@@ -571,13 +626,13 @@
 
     cell_gather(members, cell_ref, hot_ref, [saturation], put_s)
     chebyshev(
-        halo_ref, kept_ref.at[2], kept_ref.at[3], kept_ref.at[0], keep_ref.at[0], scratch, groups, members, size
+        halo_ref, kept_ref.at[2], kept_ref.at[3], kept_ref.at[0], keep_ref.at[0], scratch, groups, members, size, True
     )
     pressure = keep_ref[0]
 
     def put_p(o, cell_p):
         slots_ref[o, 0:1, :] = cell_p
-        send_slots(out_ref, (g * members + o) * size, cell_p, slots_ref[o, 1:2, :])
+        send_slots(out_ref, (g * members + o) * open_size, cell_p, slots_ref[o, 1:2, :])
 
     cell_gather(members, cell_ref, hot_ref, [pressure], put_p)
     new_saturation, q, inv = cell_update(
@@ -592,11 +647,12 @@
         saturation,
         perm_ref[...],
         left_ref,
+        None,
     )
     keep_ref[1] = new_saturation
     keep_ref[2] = q
     keep_ref[3] = inv
-    send_halo(out_ref, q, inv, pressure, groups, members, size)
+    send_halo(out_ref, q, inv, pressure, groups, members, open_size, False)
 
 
 def owner_spread(members, t, slot_ref, cell_rows, seg_rows, row_hot_ref, left_ref):
@@ -621,7 +677,7 @@
 
 
 def exchange_kernel(
-    groups, members, size, halo_ref, cell_ref, cell_hot_ref, slot_ref, hot_ref, row_hot_ref, ends_ref, own_ref,
+    groups, members, closed_size, size, halo_ref, cell_ref, cell_hot_ref, slot_ref, hot_ref, row_hot_ref, ends_ref, own_ref,
     frac_ref, aperture_ref, kept_ref, out_ref, new_ref, pressure_ref, left_ref, *scratch,
 ):
     width = slot_ref.shape[2]
@@ -631,10 +687,10 @@
         return got_slots(halo_ref, (g * members + s) * size, width)
 
     me = lax.axis_index("frac")
-    prior = ends_ref[(g * members + jnp.maximum(me - 1, 0)) * size + size - 1]
-    later = ends_ref[(g * members + jnp.minimum(me + 1, members - 1)) * size + size - 1]
-    before = jnp.where(me > 0, prior[:, LANES - 1 :], 0.0)
-    after = jnp.where(me < members - 1, later[:, 0:1], 0.0)
+    prior = ends_ref[(g * members + jnp.maximum(me - 1, 0)) * closed_size]
+    later = ends_ref[(g * members + jnp.minimum(me + 1, members - 1)) * closed_size + SUB - 1]
+    before = jnp.where(me > 0, prior[:, LANES - 2 : LANES - 1], 0.0)
+    after = jnp.where(me < members - 1, later[:, 1:2], 0.0)
 
     rows, columns = pressure_ref.shape
     seg_wide = frac_ref.shape[1]
@@ -648,7 +704,7 @@
         left_ref,
     )
     chebyshev(
-        halo_ref, kept_ref.at[2], kept_ref.at[3], kept_ref.at[0], pressure_ref, scratch, groups, members, size
+        halo_ref, kept_ref.at[2], kept_ref.at[3], kept_ref.at[0], pressure_ref, scratch, groups, members, size, False
     )
     inflow, total, gained = gathered_sum(left_ref, hot_ref, 3, seg_wide)
     new_frac, new_sat = frac_step(
@@ -659,6 +715,7 @@
     seg_table = table_of([new_frac, new_sat])
     ends = ends_of(new_frac)
     table = table_of([pressure_ref[...], kept_ref[1]])
+    columns_row = jnp.concatenate(edge_columns(pressure_ref[...]), axis=1)
     for o in range(members):
         at = slice(o * width, (o + 1) * width)
         row, _ = cell_parts(cell_ref[o : o + 1, :], columns)
@@ -669,12 +726,14 @@
         out_ref[o, 2:3, :] = seg_p
         out_ref[o, 3:4, :] = seg_s
         out_ref[o, 4:5, :] = ends
+        out_ref[o, 5:6, :] = columns_row
 
 
 def source_last_kernel(
     groups, members, size, hot_ref, row_hot_ref, sent_ref, own_ref, seg_ref, pressure_ref, kept_ref, perm_ref,
     out_ref, keep_ref, left_ref,
 ):
+    me = lax.axis_index("frac")
     pressure = pressure_ref[...]
     new_saturation, q, inv = cell_update(
         members,
@@ -688,11 +747,17 @@
         kept_ref[1],
         perm_ref[...],
         left_ref,
+        ring_of(
+            seg_ref[jnp.maximum(me - 1, 0), 5:6, :][:, LANES:],
+            seg_ref[jnp.minimum(me + 1, members - 1), 5:6, :][:, :LANES],
+            pressure_ref.shape[1],
+            members,
+        ),
     )
     keep_ref[0] = new_saturation
     keep_ref[1] = q
     keep_ref[2] = inv
-    send_halo(out_ref, q, inv, pressure, groups, members, size)
+    send_halo(out_ref, q, inv, pressure, groups, members, size, True)
 
 
 def final_kernel(
@@ -716,7 +781,7 @@
     store_segs(new_ref, 0, new_frac)
     store_segs(new_ref, 1, new_sat)
     chebyshev(
-        halo_ref, kept_ref.at[1], kept_ref.at[2], pressure_ref, out_ref.at[0], scratch, groups, members, size
+        halo_ref, kept_ref.at[1], kept_ref.at[2], pressure_ref, out_ref.at[0], scratch, groups, members, size, True
     )
     out_ref[1] = kept_ref[0]
 
@@ -761,9 +826,10 @@
 
     every = members * width
     slots = (members, SUB, width)
-    size = block_rows(columns, width)
-    both = (groups, members, size)
-    halo = (devices * size, 1, LANES)
+    closed_size, open_size = block_rows(columns, width, True), block_rows(columns, width, False)
+    both = (groups, members, closed_size)
+    halves = (groups, members, closed_size, open_size)
+    halo, open_halo = (devices * closed_size, 1, LANES), (devices * open_size, 1, LANES)
     left_cell = pltpu.VMEM((3 * PARTS * rows, every), BF16)
     seg_wide = seg_dev // SEG_COLUMNS
     segs_wide = (2, seg_wide, SEG_COLUMNS)
@@ -792,7 +858,7 @@
             pltpu.VMEM((ITERS, members, width), jnp.int32),
             pltpu.VMEM(matrix_state.shape, F32),
             pltpu.VMEM(frac.shape, F32),
-            pltpu.SemaphoreType.DMA((7,)),
+            pltpu.SemaphoreType.DMA((10,)),
         ],
         *[
             pltpu.with_memory_space_constraint(x, pltpu.HBM)
@@ -812,12 +878,12 @@
     )
     before = to_all(edge)
     edge, kept = call(
-        middle_kernel, both, [halo, (4, rows, columns)], [pltpu.VMEM((members, 2, width), F32), left_cell] + ext,
+        middle_kernel, halves, [open_halo, (4, rows, columns)], [pltpu.VMEM((members, 2, width), F32), left_cell] + ext,
         before, cells, cell_hot, cell_row_hot, sent, kept, matrix_perm,
     )
     around = to_all(edge)
     own, frac2, pressure = call(
-        exchange_kernel, both, [slots, segs_wide, (rows, columns)], [left_seg] + ext,
+        exchange_kernel, halves, [slots, segs_wide, (rows, columns)], [left_seg] + ext,
         around, cells, cell_hot, slot, hot, row_hot, before, own, frac1, aperture, kept,
     )
     segs = to_group(own)

time: 71.1 us -> 70.3 us (0.989)
  blocking collectives: 59 us -> 58.2 us
    all_to_all x3, blocking collectives: 36.1 us -> 35.3 us  [to_all(): lax.all_to_all(x, ('grp', 'frac'), split_axis=0, concat_axis=0, tiled=True)]
where the time goes in v10:
time: 70.3 us; the launch traced here: 70 us
  blocking collectives  58.2 us (83%)
  Pallas kernels  11 us (16%)
  between operations  0.72 us (1%)
    all_to_all x3, blocking collectives, to_all(): lax.all_to_all(x, ('grp', 'frac'), split_axis=0, concat_axis=0, tiled=True)  35.3 us
    all_to_all x2, blocking collectives, to_group(): return lax.all_to_all(x, 'frac', split_axis=0, concat_axis=0, tiled=True)  22.9 us
    pallas_call x6, Pallas kernels, call(): pl.pallas_call(functools.partial(kernel, *statics), out_shape=outs, in_sp...  11 us

profile of v10, /device:TPU:0, one launch (start us, length us, event | category | flops | bytes accessed | tf_op | source)
XLA Modules:
  0.0 70.0 jit_solution(8618720467990991543)
XLA Ops:
  0.6 2.0 %first_kernel.1 = (f32[8,72,256]{2,1,0:T(8,128)S(1)}, bf16[256,2048]{1,0:T(8,128)(2,1)S(1)}, bf16[128,2048]{1,0:T(8,128)(2,1)S(1)}) custom-call(s32[8,256]{1,0:T(8,128)} %bitcast.13, s32[8,256]{1,0:T(8,128)} %bitcast.17, f32[8,256]{1,0:T(8,128)} %bitcast.18, s32[1,8]{1,0:T(1,128)} %bitcast.19, s32[3,8,256]{2,1,0:T(8,128)} %bitcast.16, ...), custom_call_target="tpu_custom_call" | custom-call | tf_op jit(solution)/shard_map/first_kernel/pallas_call | solution.py:795
  2.6 0.0 copy-start
  2.6 0.0 copy-start.1
  2.7 0.0 copy-start.2
  2.7 0.0 copy-start.3
  2.7 15.5 %all_to_all.25.slot_ref = f32[8,72,256]{2,1,0:T(8,128)S(1)} all-to-all(f32[8,72,256]{2,1,0:T(8,128)S(1)} %get-tuple-element.22.sent_ref), channel_id=1, replica_groups=mesh['grp'=4,'frac'=8] {'frac'}, dimensions={0} | all-to-all | bytes 1179648 | tf_op jit(solution)/shard_map/all_to_all | solution.py:841
  18.2 0.0 copy-done
  18.2 0.0 copy-done.1
  18.2 0.0 copy-done.2
  18.2 0.0 copy-done.3
  18.2 2.6 %start_kernel.1 = (f32[384,1,128]{2,1,0:T(1,128)S(1)}, f32[4,128,256]{2,1,0:T(8,128)S(1)}, f32[8,2,256]{2,1,0:T(2,128)S(1)}, f32[2,32,256]{2,1,0:T(8,128)S(1)}, ...) custom-call(f32[8,72,256]{2,1,0:T(8,128)S(1)} %all_to_all.25.slot_ref, ...), custom_call_target="tpu_custom_call" | custom-call | tf_op jit(solution)/shard_map/start_kernel/pallas_call | solution.py:795
  20.9 0.0 copy-start.4
  20.9 12.7 %all_to_all.26.halo_ref.ends_ref = f32[384,1,128]{2,1,0:T(1,128)S(1)} all-to-all(f32[384,1,128]{2,1,0:T(1,128)S(1)} %get-tuple-element.23), channel_id=1, replica_groups=mesh['grp'=4,'frac'=8] {'grp','frac'}, dimensions={0} | all-to-all | bytes 393216 | tf_op jit(solution)/shard_map/all_to_all | solution.py:844
  33.6 0.0 copy-done.4
  33.6 2.1 %middle_kernel.1 = (f32[416,1,128]{2,1,0:T(1,128)S(1)}, f32[4,128,256]{2,1,0:T(8,128)S(1)}) custom-call(f32[384,1,128]{2,1,0:T(1,128)S(1)} %all_to_all.26.halo_ref.ends_ref, s32[8,256]{1,0:T(8,128)S(1)} %bitcast.14, bf16[256,2048]{1,0:T(8,128)(2,1)S(1)} %get-tuple-element.20.cell_hot_ref.hot_ref, ...), custom_call_target="tpu_custom_call" | custom-call | tf_op jit(solution)/shard_map/middle_kernel/pallas_call | solution.py:795
  35.7 11.9 %all_to_all.27.halo_ref = f32[416,1,128]{2,1,0:T(1,128)S(1)} all-to-all(f32[416,1,128]{2,1,0:T(1,128)S(1)} %get-tuple-element.25), channel_id=1, replica_groups=mesh['grp'=4,'frac'=8] {'grp','frac'}, dimensions={0} | all-to-all | bytes 425984 | tf_op jit(solution)/shard_map/all_to_all | solution.py:844
  47.5 1.8 %exchange_kernel.1 = (f32[8,8,256]{2,1,0:T(8,128)S(1)}, f32[2,32,256]{2,1,0:T(8,128)S(1)}, f32[128,256]{1,0:T(8,128)S(1)}) custom-call(f32[416,1,128]{2,1,0:T(1,128)S(1)} %all_to_all.27.halo_ref, s32[8,256]{1,0:T(8,128)S(1)} %bitcast.15, bf16[256,2048]{1,0:T(8,128)(2,1)S(1)} %get-tuple-element.20.cell_hot_ref.hot_ref, ...), custom_call_target="tpu_custom_call" | custom-call | tf_op jit(solution)/shard_map/exchange_kernel/pallas_call | solution.py:795
  49.3 7.4 %all_to_all.28.seg_ref = f32[8,8,256]{2,1,0:T(8,128)S(1)} all-to-all(f32[8,8,256]{2,1,0:T(8,128)S(1)} %get-tuple-element.31.own_ref), channel_id=1, replica_groups=mesh['grp'=4,'frac'=8] {'frac'}, dimensions={0} | all-to-all | bytes 131072 | tf_op jit(solution)/shard_map/all_to_all | solution.py:841
  56.7 1.1 %source_last_kernel.1 = (f32[384,1,128]{2,1,0:T(1,128)S(1)}, f32[3,128,256]{2,1,0:T(8,128)S(1)}) custom-call(bf16[256,2048]{1,0:T(8,128)(2,1)S(1)} %get-tuple-element.20.cell_hot_ref.hot_ref, bf16[128,2048]{1,0:T(8,128)(2,1)S(1)} %get-tuple-element.21.cell_row_hot_ref.row_hot_ref, f32[8,72,256]{2,1,0:T(8,128)S(1)} %get-tuple-element.22.sent_ref, ...), custom_call_target="tpu_custom_call" | custom-call | tf_op jit(solution)/shard_map/source_last_kernel/pallas_call | solution.py:795
  57.8 10.7 %all_to_all.29.halo_ref = f32[384,1,128]{2,1,0:T(1,128)S(1)} all-to-all(f32[384,1,128]{2,1,0:T(1,128)S(1)} %get-tuple-element.33), channel_id=1, replica_groups=mesh['grp'=4,'frac'=8] {'grp','frac'}, dimensions={0} | all-to-all | bytes 393216 | tf_op jit(solution)/shard_map/all_to_all | solution.py:844
  68.5 1.4 %final_kernel.1 = (f32[2,128,256]{2,1,0:T(8,128)}, f32[2,64,128]{2,1,0:T(8,128)}) custom-call(f32[384,1,128]{2,1,0:T(1,128)S(1)} %all_to_all.29.halo_ref, f32[128,256]{1,0:T(8,128)S(1)} %get-tuple-element.32.pressure_ref, f32[3,128,256]{2,1,0:T(8,128)S(1)} %get-tuple-element.34.kept_ref, f32[8,72,256]{2,1,0:T(8,128)S(1)} %all_to_all.25.slot_ref, ...), custom_call_target="tpu_custom_call" | custom-call | tf_op jit(solution)/shard_map/final_kernel/pallas_call | solution.py:795
Async XLA Ops:
  2.6 15.6 %copy-start = (f32[128,256]{1,0:T(8,128)S(1)}, f32[128,256]{1,0:T(8,128)}, u32[]{:S(2)}) copy-start(f32[128,256]{1,0:T(8,128)} %perm_ref.5) | copy-start | bytes 393220
  2.6 15.6 %copy-start.1 = (f32[2,128,256]{2,1,0:T(8,128)S(1)}, f32[2,128,256]{2,1,0:T(8,128)}, u32[]{:S(2)}) copy-start(f32[2,128,256]{2,1,0:T(8,128)} %state_ref.1) | copy-start | bytes 786436
  2.7 15.6 %copy-start.2 = (f32[1,8192]{1,0:T(1,128)S(1)}, f32[1,8192]{1,0:T(1,128)}, u32[]{:S(2)}) copy-start(f32[1,8192]{1,0:T(1,128)} %param.12) | copy-start | bytes 98308
  2.7 15.6 %copy-start.3 = (f32[2,1,8192]{2,1,0:T(1,128)S(1)}, f32[2,1,8192]{2,1,0:T(1,128)}, u32[]{:S(2)}) copy-start(f32[2,1,8192]{2,1,0:T(1,128)} %param.11) | copy-start | bytes 196612
  20.9 12.7 %copy-start.4 = (s32[1,1,8,256]{3,2,1,0:T(8,128)S(1)}, s32[1,1,8,256]{3,2,1,0:T(8,128)}, u32[]{:S(2)}) copy-start(s32[1,1,8,256]{3,2,1,0:T(8,128)} %param.13) | copy-start | bytes 24580

commit v11 on v10

--- a/solution.py
+++ b/solution.py
@@ -439,13 +439,12 @@
 ):
     _, rows, columns = state_ref.shape
     width = cell_ref.shape[1]
-    state_rows = [pl.ds(h * rows // 2, rows // 2) for h in range(2)]
     copies = [
         pltpu.make_async_copy(source, target, sem.at[i])
         for i, (source, target) in enumerate(
             [
                 (cell_any, cell_ref),
-                *[(state_any.at[k, at], state_ref.at[k, at]) for at in state_rows for k in range(2)],
+                (state_any, state_ref),
                 (seg_any, seg_ref),
                 (trans_any, trans_ref),
                 (count_any, count_ref),
@@ -464,13 +463,11 @@
         hot_ref[:, at] = one_hot(col, columns)
         row_hot_ref[:, at] = one_hot(row, rows)
 
-    early = members // 2
-    for o in range(early):
+    for o in range(members):
         make_hots(o)
-    for copy in copies[1:5]:
-        copy.wait()
+    copies[1].wait()
     table = table_of([state_ref[0], state_ref[1]])
-    for copy in copies[5:]:
+    for copy in copies[2:]:
         copy.wait()
     frac = load_segs(frac_ref, 0)
     ends = ends_of(frac)
@@ -482,8 +479,6 @@
     for o in range(members):
         one = slice(o, o + 1)
         row, _ = cell_parts(cell_ref[one, :], columns)
-        if o >= early:
-            make_hots(o)
         cell_p, cell_s = pick(table, 2, rows, row, hot_ref[:, o * width : (o + 1) * width])
         live = iota((1, width), 1) < count_ref[0, o]
         out_ref[o, ROW_SEG : ROW_SEG + 1, :] = seg_ref[one, :].astype(F32)
@@ -513,32 +508,40 @@
     return pick(table, 2, fields, seg_parts(slot_ref, s)[0], hot_ref[:, s * width : (s + 1) * width])
 
 
-def cell_update(
-    members, t, hot_ref, row_hot_ref, sent_ref, cell_rows, seg_rows, pressure, saturation, perm, left_ref, ring
-):
+def cell_spread(t, o, row_hot_ref, sent_ref, cell_row, seg_row, left_ref):
+    seg_p, seg_s = seg_row
+    cell_p, cell_s = cell_row
+    weight, water = flow(
+        sent_ref[o, ROW_TRANS : ROW_TRANS + 1, :],
+        sent_ref[o, ROW_UP + t : ROW_UP + t + 1, :],
+        cell_p,
+        cell_s,
+        seg_p,
+        seg_s,
+    )
+    spread(left_ref, row_hot_ref, o, [weight, weight * seg_p, water])
+
+
+def cell_finish(hot_ref, pressure, saturation, perm, left_ref, ring):
     rows = pressure.shape[0]
-    for o in range(members):
-        seg_p, seg_s = seg_rows(o)
-        cell_p, cell_s = cell_rows(o)
-        weight, water = flow(
-            sent_ref[o, ROW_TRANS : ROW_TRANS + 1, :],
-            sent_ref[o, ROW_UP + t : ROW_UP + t + 1, :],
-            cell_p,
-            cell_s,
-            seg_p,
-            seg_s,
-        )
-        spread(left_ref, row_hot_ref, o, [weight, weight * seg_p, water])
     couple, source, lost = gathered_sum(left_ref, hot_ref, 3, rows)
     inverse = 1.0 / (4.0 + perm + couple)
     new_saturation = saturation - TAU_STEP * lost / (perm + couple)
     return new_saturation, partial_residual(pressure, couple, source, inverse, ring), inverse
 
 
+def cell_update(
+    members, t, hot_ref, row_hot_ref, sent_ref, cell_rows, seg_rows, pressure, saturation, perm, left_ref, ring
+):
+    for o in range(members):
+        cell_spread(t, o, row_hot_ref, sent_ref, cell_rows(o), seg_rows(o), left_ref)
+    return cell_finish(hot_ref, pressure, saturation, perm, left_ref, ring)
+
+
 def start_kernel(
     groups, members, size, slot_ref, sent_ref, cell_hot_ref, cell_row_hot_ref, frac_ref, aperture_ref,
     state_ref, perm_ref, out_ref, keep_ref, own_ref, new_ref, hot_ref, row_hot_ref,
-    left_seg_ref, left_ref, found_ref,
+    left_seg_ref, left_ref,
 ):
     width = slot_ref.shape[2]
     rows = new_ref.shape[1]
@@ -558,34 +561,29 @@
             seg_s,
         )
         spread(left_seg_ref, row_hot_ref, s, [weight * cell_p, weight, water])
+        o = s
+        row, lane = seg_parts(sent_ref, o)
+        whole = table_of([slot_ref[o, SUB : SUB + rows, :], slot_ref[o, SUB + rows :, :]])
+        seg_p, seg_s = pick(whole, 2, rows, row, one_hot(lane, SEG_COLUMNS))
+        cell_spread(
+            0,
+            o,
+            cell_row_hot_ref,
+            sent_ref,
+            (sent_ref[o, ROW_P : ROW_P + 1, :], sent_ref[o, ROW_S : ROW_S + 1, :]),
+            (seg_p, seg_s),
+            left_ref,
+        )
     inflow, total, gained = gathered_sum(left_seg_ref, hot_ref, 3, rows)
     before, after = chain_ends(slot_ref, ROW_ENDS, members)
     new_frac, new_sat = frac_step(frac, sat, load_segs(aperture_ref), before, after, inflow, total, gained)
     new_ref[0] = new_frac
     new_ref[1] = new_sat
     table = table_of([new_frac, new_sat])
-    for s in range(members):
-        seg_p, seg_s = seg_gather(slot_ref, hot_ref, rows, s, width, table)
-        own_ref[s, 0:1, :] = seg_p
-        own_ref[s, 1:2, :] = seg_s
-        at = (g * members + s) * size
-        send_slots(out_ref, at, seg_p, seg_s)
-    for o in range(members):
-        row, lane = seg_parts(sent_ref, o)
-        table = table_of([slot_ref[o, SUB : SUB + rows, :], slot_ref[o, SUB + rows :, :]])
-        seg_p, seg_s = pick(table, 2, rows, row, one_hot(lane, SEG_COLUMNS))
-        found_ref[o, 0:1, :] = seg_p
-        found_ref[o, 1:2, :] = seg_s
     me = lax.axis_index("frac")
     pressure = state_ref[0]
-    new_saturation, q, inv = cell_update(
-        members,
-        0,
+    new_saturation, q, inv = cell_finish(
         cell_hot_ref,
-        cell_row_hot_ref,
-        sent_ref,
-        lambda o: (sent_ref[o, ROW_P : ROW_P + 1, :], sent_ref[o, ROW_S : ROW_S + 1, :]),
-        lambda o: (found_ref[o, 0:1, :], found_ref[o, 1:2, :]),
         pressure,
         state_ref[1],
         perm_ref[...],
@@ -597,6 +595,12 @@
             members,
         ),
     )
+    for s in range(members):
+        seg_p, seg_s = seg_gather(slot_ref, hot_ref, rows, s, width, table)
+        own_ref[s, 0:1, :] = seg_p
+        own_ref[s, 1:2, :] = seg_s
+        at = (g * members + s) * size
+        send_slots(out_ref, at, seg_p, seg_s)
     keep_ref[0] = pressure
     keep_ref[1] = new_saturation
     keep_ref[2] = q
@@ -858,7 +862,7 @@
             pltpu.VMEM((ITERS, members, width), jnp.int32),
             pltpu.VMEM(matrix_state.shape, F32),
             pltpu.VMEM(frac.shape, F32),
-            pltpu.SemaphoreType.DMA((10,)),
+            pltpu.SemaphoreType.DMA((7,)),
         ],
         *[
             pltpu.with_memory_space_constraint(x, pltpu.HBM)
@@ -873,7 +877,7 @@
         start_kernel,
         both,
         [halo, (4, rows, columns), (members, 2, width), segs_wide] + hots(SEG_COLUMNS, seg_wide),
-        [left_seg, left_cell, pltpu.VMEM((members, 2, width), F32)],
+        [left_seg, left_cell],
         slot, sent, cell_hot, cell_row_hot, frac, aperture, matrix_state, matrix_perm,
     )
     before = to_all(edge)

time: 70.3 us -> 69.7 us (level)
  no operation moved by 1% of the time
where the time goes in v11:
time: 69.7 us; the launch traced here: 69.4 us
  blocking collectives  58.2 us (84%)
  Pallas kernels  10.4 us (15%)
  between operations  0.72 us (1%)
    all_to_all x3, blocking collectives, to_all(): lax.all_to_all(x, ('grp', 'frac'), split_axis=0, concat_axis=0, tiled=True)  35.3 us
    all_to_all x2, blocking collectives, to_group(): return lax.all_to_all(x, 'frac', split_axis=0, concat_axis=0, tiled=True)  22.9 us
    pallas_call x6, Pallas kernels, call(): pl.pallas_call(functools.partial(kernel, *statics), out_shape=outs, in_sp...  10.4 us

profile of v11, /device:TPU:0, one launch (start us, length us, event | category | flops | bytes accessed | tf_op | source)
XLA Modules:
  0.0 69.4 jit_solution(13718287414473778681)
XLA Ops:
  0.6 1.9 %first_kernel.1 = (f32[8,72,256]{2,1,0:T(8,128)S(1)}, bf16[256,2048]{1,0:T(8,128)(2,1)S(1)}, bf16[128,2048]{1,0:T(8,128)(2,1)S(1)}) custom-call(s32[8,256]{1,0:T(8,128)} %bitcast.13, s32[8,256]{1,0:T(8,128)} %bitcast.17, f32[8,256]{1,0:T(8,128)} %bitcast.18, s32[1,8]{1,0:T(1,128)} %bitcast.19, s32[3,8,256]{2,1,0:T(8,128)} %bitcast.16, ...), custom_call_target="tpu_custom_call" | custom-call | tf_op jit(solution)/shard_map/first_kernel/pallas_call | solution.py:799
  2.5 0.0 copy-start
  2.6 0.0 copy-start.1
  2.6 0.0 copy-start.2
  2.6 0.0 copy-start.3
  2.6 15.5 %all_to_all.25.slot_ref = f32[8,72,256]{2,1,0:T(8,128)S(1)} all-to-all(f32[8,72,256]{2,1,0:T(8,128)S(1)} %get-tuple-element.22.sent_ref), channel_id=1, replica_groups=mesh['grp'=4,'frac'=8] {'frac'}, dimensions={0} | all-to-all | bytes 1179648 | tf_op jit(solution)/shard_map/all_to_all | solution.py:845
  18.1 0.0 copy-done
  18.1 0.0 copy-done.1
  18.1 0.0 copy-done.2
  18.2 0.0 copy-done.3
  18.2 2.1 %start_kernel.1 = (f32[384,1,128]{2,1,0:T(1,128)S(1)}, f32[4,128,256]{2,1,0:T(8,128)S(1)}, f32[8,2,256]{2,1,0:T(2,128)S(1)}, f32[2,32,256]{2,1,0:T(8,128)S(1)}, ...) custom-call(f32[8,72,256]{2,1,0:T(8,128)S(1)} %all_to_all.25.slot_ref, ...), custom_call_target="tpu_custom_call" | custom-call | tf_op jit(solution)/shard_map/start_kernel/pallas_call | solution.py:799
  20.2 0.0 copy-start.4
  20.2 12.7 %all_to_all.26.halo_ref.ends_ref = f32[384,1,128]{2,1,0:T(1,128)S(1)} all-to-all(f32[384,1,128]{2,1,0:T(1,128)S(1)} %get-tuple-element.23), channel_id=1, replica_groups=mesh['grp'=4,'frac'=8] {'grp','frac'}, dimensions={0} | all-to-all | bytes 393216 | tf_op jit(solution)/shard_map/all_to_all | solution.py:848
  33.0 0.0 copy-done.4
  33.0 2.1 %middle_kernel.1 = (f32[416,1,128]{2,1,0:T(1,128)S(1)}, f32[4,128,256]{2,1,0:T(8,128)S(1)}) custom-call(f32[384,1,128]{2,1,0:T(1,128)S(1)} %all_to_all.26.halo_ref.ends_ref, s32[8,256]{1,0:T(8,128)S(1)} %bitcast.14, bf16[256,2048]{1,0:T(8,128)(2,1)S(1)} %get-tuple-element.20.cell_hot_ref.hot_ref, ...), custom_call_target="tpu_custom_call" | custom-call | tf_op jit(solution)/shard_map/middle_kernel/pallas_call | solution.py:799
  35.0 11.9 %all_to_all.27.halo_ref = f32[416,1,128]{2,1,0:T(1,128)S(1)} all-to-all(f32[416,1,128]{2,1,0:T(1,128)S(1)} %get-tuple-element.25), channel_id=1, replica_groups=mesh['grp'=4,'frac'=8] {'grp','frac'}, dimensions={0} | all-to-all | bytes 425984 | tf_op jit(solution)/shard_map/all_to_all | solution.py:848
  46.9 1.8 %exchange_kernel.1 = (f32[8,8,256]{2,1,0:T(8,128)S(1)}, f32[2,32,256]{2,1,0:T(8,128)S(1)}, f32[128,256]{1,0:T(8,128)S(1)}) custom-call(f32[416,1,128]{2,1,0:T(1,128)S(1)} %all_to_all.27.halo_ref, s32[8,256]{1,0:T(8,128)S(1)} %bitcast.15, bf16[256,2048]{1,0:T(8,128)(2,1)S(1)} %get-tuple-element.20.cell_hot_ref.hot_ref, ...), custom_call_target="tpu_custom_call" | custom-call | tf_op jit(solution)/shard_map/exchange_kernel/pallas_call | solution.py:799
  48.7 7.4 %all_to_all.28.seg_ref = f32[8,8,256]{2,1,0:T(8,128)S(1)} all-to-all(f32[8,8,256]{2,1,0:T(8,128)S(1)} %get-tuple-element.31.own_ref), channel_id=1, replica_groups=mesh['grp'=4,'frac'=8] {'frac'}, dimensions={0} | all-to-all | bytes 131072 | tf_op jit(solution)/shard_map/all_to_all | solution.py:845
  56.1 1.1 %source_last_kernel.1 = (f32[384,1,128]{2,1,0:T(1,128)S(1)}, f32[3,128,256]{2,1,0:T(8,128)S(1)}) custom-call(bf16[256,2048]{1,0:T(8,128)(2,1)S(1)} %get-tuple-element.20.cell_hot_ref.hot_ref, bf16[128,2048]{1,0:T(8,128)(2,1)S(1)} %get-tuple-element.21.cell_row_hot_ref.row_hot_ref, f32[8,72,256]{2,1,0:T(8,128)S(1)} %get-tuple-element.22.sent_ref, ...), custom_call_target="tpu_custom_call" | custom-call | tf_op jit(solution)/shard_map/source_last_kernel/pallas_call | solution.py:799
  57.2 10.7 %all_to_all.29.halo_ref = f32[384,1,128]{2,1,0:T(1,128)S(1)} all-to-all(f32[384,1,128]{2,1,0:T(1,128)S(1)} %get-tuple-element.33), channel_id=1, replica_groups=mesh['grp'=4,'frac'=8] {'grp','frac'}, dimensions={0} | all-to-all | bytes 393216 | tf_op jit(solution)/shard_map/all_to_all | solution.py:848
  67.9 1.4 %final_kernel.1 = (f32[2,128,256]{2,1,0:T(8,128)}, f32[2,64,128]{2,1,0:T(8,128)}) custom-call(f32[384,1,128]{2,1,0:T(1,128)S(1)} %all_to_all.29.halo_ref, f32[128,256]{1,0:T(8,128)S(1)} %get-tuple-element.32.pressure_ref, f32[3,128,256]{2,1,0:T(8,128)S(1)} %get-tuple-element.34.kept_ref, f32[8,72,256]{2,1,0:T(8,128)S(1)} %all_to_all.25.slot_ref, ...), custom_call_target="tpu_custom_call" | custom-call | tf_op jit(solution)/shard_map/final_kernel/pallas_call | solution.py:799
Async XLA Ops:
  2.5 15.6 %copy-start = (f32[128,256]{1,0:T(8,128)S(1)}, f32[128,256]{1,0:T(8,128)}, u32[]{:S(2)}) copy-start(f32[128,256]{1,0:T(8,128)} %perm_ref.5) | copy-start | bytes 393220
  2.6 15.6 %copy-start.1 = (f32[2,128,256]{2,1,0:T(8,128)S(1)}, f32[2,128,256]{2,1,0:T(8,128)}, u32[]{:S(2)}) copy-start(f32[2,128,256]{2,1,0:T(8,128)} %state_ref.1) | copy-start | bytes 786436
  2.6 15.6 %copy-start.2 = (f32[1,8192]{1,0:T(1,128)S(1)}, f32[1,8192]{1,0:T(1,128)}, u32[]{:S(2)}) copy-start(f32[1,8192]{1,0:T(1,128)} %param.12) | copy-start | bytes 98308
  2.6 15.6 %copy-start.3 = (f32[2,1,8192]{2,1,0:T(1,128)S(1)}, f32[2,1,8192]{2,1,0:T(1,128)}, u32[]{:S(2)}) copy-start(f32[2,1,8192]{2,1,0:T(1,128)} %param.11) | copy-start | bytes 196612
  20.2 12.7 %copy-start.4 = (s32[1,1,8,256]{3,2,1,0:T(8,128)S(1)}, s32[1,1,8,256]{3,2,1,0:T(8,128)}, u32[]{:S(2)}) copy-start(s32[1,1,8,256]{3,2,1,0:T(8,128)} %param.13) | copy-start | bytes 24580

commit v12 on v11

--- a/solution.py
+++ b/solution.py
@@ -634,33 +634,32 @@
     )
     pressure = keep_ref[0]
 
-    def put_p(o, cell_p):
-        slots_ref[o, 0:1, :] = cell_p
-        send_slots(out_ref, (g * members + o) * open_size, cell_p, slots_ref[o, 1:2, :])
-
-    cell_gather(members, cell_ref, hot_ref, [pressure], put_p)
-    new_saturation, q, inv = cell_update(
-        members,
-        1,
-        hot_ref,
-        row_hot_ref,
-        sent_ref,
-        lambda o: (slots_ref[o, 0:1, :], slots_ref[o, 1:2, :]),
-        lambda o: got_slots(halo_ref, (g * members + o) * size, cell_ref.shape[1]),
-        pressure,
-        saturation,
-        perm_ref[...],
-        left_ref,
-        None,
-    )
+    rows, columns = pressure.shape
+    width = cell_ref.shape[1]
+    table = table_of([pressure])
+    for o in range(members):
+        row, _ = cell_parts(cell_ref[o : o + 1, :], columns)
+        (cell_p,) = pick(table, 1, rows, row, hot_ref[:, o * width : (o + 1) * width])
+        cell_s = slots_ref[o, 1:2, :]
+        send_slots(out_ref, (g * members + o) * open_size, cell_p, cell_s)
+        cell_spread(
+            1,
+            o,
+            row_hot_ref,
+            sent_ref,
+            (cell_p, cell_s),
+            got_slots(halo_ref, (g * members + o) * size, width),
+            left_ref,
+        )
+    new_saturation, q, inv = cell_finish(hot_ref, pressure, saturation, perm_ref[...], left_ref, None)
     keep_ref[1] = new_saturation
     keep_ref[2] = q
     keep_ref[3] = inv
     send_halo(out_ref, q, inv, pressure, groups, members, open_size, False)
 
 
-def owner_spread(members, t, slot_ref, cell_rows, seg_rows, row_hot_ref, left_ref):
-    for s in range(members):
+def owner_spread(blocks, t, slot_ref, cell_rows, seg_rows, row_hot_ref, left_ref):
+    for s in blocks:
         cell_p, cell_s = cell_rows(s)
         weight, water = flow(
             slot_ref[s, ROW_TRANS : ROW_TRANS + 1, :],
@@ -675,7 +674,7 @@
 def owner_update(
     members, t, slot_ref, cell_rows, seg_rows, frac, sat, aperture, ends, hot_ref, row_hot_ref, left_ref
 ):
-    owner_spread(members, t, slot_ref, cell_rows, seg_rows, row_hot_ref, left_ref)
+    owner_spread(range(members), t, slot_ref, cell_rows, seg_rows, row_hot_ref, left_ref)
     inflow, total, gained = gathered_sum(left_ref, hot_ref, 3, frac.shape[0])
     return frac_step(frac, sat, aperture, *ends, inflow, total, gained)
 
@@ -699,7 +698,7 @@
     rows, columns = pressure_ref.shape
     seg_wide = frac_ref.shape[1]
     owner_spread(
-        members,
+        range(members),
         1,
         slot_ref,
         cell_rows,
@@ -707,9 +706,6 @@
         row_hot_ref,
         left_ref,
     )
-    chebyshev(
-        halo_ref, kept_ref.at[2], kept_ref.at[3], kept_ref.at[0], pressure_ref, scratch, groups, members, size, False
-    )
     inflow, total, gained = gathered_sum(left_ref, hot_ref, 3, seg_wide)
     new_frac, new_sat = frac_step(
         frac_ref[0], frac_ref[1], load_segs(aperture_ref), before, after, inflow, total, gained
@@ -718,18 +714,26 @@
     new_ref[1] = new_sat
     seg_table = table_of([new_frac, new_sat])
     ends = ends_of(new_frac)
-    table = table_of([pressure_ref[...], kept_ref[1]])
+    s_table = table_of([kept_ref[1]])
+    for o in range(members):
+        at = slice(o * width, (o + 1) * width)
+        row, _ = cell_parts(cell_ref[o : o + 1, :], columns)
+        (cell_s,) = pick(s_table, 1, rows, row, cell_hot_ref[:, at])
+        out_ref[o, 1:2, :] = cell_s
+    chebyshev(
+        halo_ref, kept_ref.at[2], kept_ref.at[3], kept_ref.at[0], pressure_ref, scratch, groups, members, size, False
+    )
+    p_table = table_of([pressure_ref[...]])
     columns_row = jnp.concatenate(edge_columns(pressure_ref[...]), axis=1)
     for o in range(members):
         at = slice(o * width, (o + 1) * width)
-        row, _ = cell_parts(cell_ref[o : o + 1, :], columns)
-        cell_p, cell_s = pick(table, 2, rows, row, cell_hot_ref[:, at])
-        out_ref[o, 0:1, :] = cell_p
-        out_ref[o, 1:2, :] = cell_s
         seg_p, seg_s = pick(seg_table, 2, seg_wide, seg_parts(slot_ref, o)[0], hot_ref[:, at])
         out_ref[o, 2:3, :] = seg_p
         out_ref[o, 3:4, :] = seg_s
         out_ref[o, 4:5, :] = ends
+        row, _ = cell_parts(cell_ref[o : o + 1, :], columns)
+        (cell_p,) = pick(p_table, 1, rows, row, cell_hot_ref[:, at])
+        out_ref[o, 0:1, :] = cell_p
         out_ref[o, 5:6, :] = columns_row
 
 

time: 69.7 us -> 69.4 us (level)
  no operation moved by 1% of the time
where the time goes in v12:
time: 69.4 us; the launch traced here: 69 us
  blocking collectives  58.2 us (84%)
  Pallas kernels  10.1 us (15%)
  between operations  0.72 us (1%)
    all_to_all x3, blocking collectives, to_all(): lax.all_to_all(x, ('grp', 'frac'), split_axis=0, concat_axis=0, tiled=True)  35.3 us
    all_to_all x2, blocking collectives, to_group(): return lax.all_to_all(x, 'frac', split_axis=0, concat_axis=0, tiled=True)  22.9 us
    pallas_call x6, Pallas kernels, call(): pl.pallas_call(functools.partial(kernel, *statics), out_shape=outs, in_sp...  10.1 us

profile of v12, /device:TPU:0, one launch (start us, length us, event | category | flops | bytes accessed | tf_op | source)
XLA Modules:
  0.0 69.0 jit_solution(7829386574849226965)
XLA Ops:
  0.6 1.9 %first_kernel.1 = (f32[8,72,256]{2,1,0:T(8,128)S(1)}, bf16[256,2048]{1,0:T(8,128)(2,1)S(1)}, bf16[128,2048]{1,0:T(8,128)(2,1)S(1)}) custom-call(s32[8,256]{1,0:T(8,128)} %bitcast.13, s32[8,256]{1,0:T(8,128)} %bitcast.17, f32[8,256]{1,0:T(8,128)} %bitcast.18, s32[1,8]{1,0:T(1,128)} %bitcast.19, s32[3,8,256]{2,1,0:T(8,128)} %bitcast.16, ...), custom_call_target="tpu_custom_call" | custom-call | tf_op jit(solution)/shard_map/first_kernel/pallas_call | solution.py:803
  2.5 0.0 copy-start
  2.6 0.0 copy-start.1
  2.6 0.0 copy-start.2
  2.6 0.0 copy-start.3
  2.6 15.5 %all_to_all.25.slot_ref = f32[8,72,256]{2,1,0:T(8,128)S(1)} all-to-all(f32[8,72,256]{2,1,0:T(8,128)S(1)} %get-tuple-element.22.sent_ref), channel_id=1, replica_groups=mesh['grp'=4,'frac'=8] {'frac'}, dimensions={0} | all-to-all | bytes 1179648 | tf_op jit(solution)/shard_map/all_to_all | solution.py:849
  18.1 0.0 copy-done
  18.1 0.0 copy-done.1
  18.1 0.0 copy-done.2
  18.2 0.0 copy-done.3
  18.2 2.1 %start_kernel.1 = (f32[384,1,128]{2,1,0:T(1,128)S(1)}, f32[4,128,256]{2,1,0:T(8,128)S(1)}, f32[8,2,256]{2,1,0:T(2,128)S(1)}, f32[2,32,256]{2,1,0:T(8,128)S(1)}, ...) custom-call(f32[8,72,256]{2,1,0:T(8,128)S(1)} %all_to_all.25.slot_ref, ...), custom_call_target="tpu_custom_call" | custom-call | tf_op jit(solution)/shard_map/start_kernel/pallas_call | solution.py:803
  20.2 0.0 copy-start.4
  20.2 12.7 %all_to_all.26.halo_ref.ends_ref = f32[384,1,128]{2,1,0:T(1,128)S(1)} all-to-all(f32[384,1,128]{2,1,0:T(1,128)S(1)} %get-tuple-element.23), channel_id=1, replica_groups=mesh['grp'=4,'frac'=8] {'grp','frac'}, dimensions={0} | all-to-all | bytes 393216 | tf_op jit(solution)/shard_map/all_to_all | solution.py:852
  33.0 0.0 copy-done.4
  33.0 2.1 %middle_kernel.1 = (f32[416,1,128]{2,1,0:T(1,128)S(1)}, f32[4,128,256]{2,1,0:T(8,128)S(1)}) custom-call(f32[384,1,128]{2,1,0:T(1,128)S(1)} %all_to_all.26.halo_ref.ends_ref, s32[8,256]{1,0:T(8,128)S(1)} %bitcast.14, bf16[256,2048]{1,0:T(8,128)(2,1)S(1)} %get-tuple-element.20.cell_hot_ref.hot_ref, ...), custom_call_target="tpu_custom_call" | custom-call | tf_op jit(solution)/shard_map/middle_kernel/pallas_call | solution.py:803
  35.0 11.9 %all_to_all.27.halo_ref = f32[416,1,128]{2,1,0:T(1,128)S(1)} all-to-all(f32[416,1,128]{2,1,0:T(1,128)S(1)} %get-tuple-element.25), channel_id=1, replica_groups=mesh['grp'=4,'frac'=8] {'grp','frac'}, dimensions={0} | all-to-all | bytes 425984 | tf_op jit(solution)/shard_map/all_to_all | solution.py:852
  46.9 1.5 %exchange_kernel.1 = (f32[8,8,256]{2,1,0:T(8,128)S(1)}, f32[2,32,256]{2,1,0:T(8,128)S(1)}, f32[128,256]{1,0:T(8,128)S(1)}) custom-call(f32[416,1,128]{2,1,0:T(1,128)S(1)} %all_to_all.27.halo_ref, s32[8,256]{1,0:T(8,128)S(1)} %bitcast.15, bf16[256,2048]{1,0:T(8,128)(2,1)S(1)} %get-tuple-element.20.cell_hot_ref.hot_ref, ...), custom_call_target="tpu_custom_call" | custom-call | tf_op jit(solution)/shard_map/exchange_kernel/pallas_call | solution.py:803
  48.4 7.4 %all_to_all.28.seg_ref = f32[8,8,256]{2,1,0:T(8,128)S(1)} all-to-all(f32[8,8,256]{2,1,0:T(8,128)S(1)} %get-tuple-element.31.own_ref), channel_id=1, replica_groups=mesh['grp'=4,'frac'=8] {'frac'}, dimensions={0} | all-to-all | bytes 131072 | tf_op jit(solution)/shard_map/all_to_all | solution.py:849
  55.8 1.1 %source_last_kernel.1 = (f32[384,1,128]{2,1,0:T(1,128)S(1)}, f32[3,128,256]{2,1,0:T(8,128)S(1)}) custom-call(bf16[256,2048]{1,0:T(8,128)(2,1)S(1)} %get-tuple-element.20.cell_hot_ref.hot_ref, bf16[128,2048]{1,0:T(8,128)(2,1)S(1)} %get-tuple-element.21.cell_row_hot_ref.row_hot_ref, f32[8,72,256]{2,1,0:T(8,128)S(1)} %get-tuple-element.22.sent_ref, ...), custom_call_target="tpu_custom_call" | custom-call | tf_op jit(solution)/shard_map/source_last_kernel/pallas_call | solution.py:803
  56.9 10.7 %all_to_all.29.halo_ref = f32[384,1,128]{2,1,0:T(1,128)S(1)} all-to-all(f32[384,1,128]{2,1,0:T(1,128)S(1)} %get-tuple-element.33), channel_id=1, replica_groups=mesh['grp'=4,'frac'=8] {'grp','frac'}, dimensions={0} | all-to-all | bytes 393216 | tf_op jit(solution)/shard_map/all_to_all | solution.py:852
  67.6 1.4 %final_kernel.1 = (f32[2,128,256]{2,1,0:T(8,128)}, f32[2,64,128]{2,1,0:T(8,128)}) custom-call(f32[384,1,128]{2,1,0:T(1,128)S(1)} %all_to_all.29.halo_ref, f32[128,256]{1,0:T(8,128)S(1)} %get-tuple-element.32.pressure_ref, f32[3,128,256]{2,1,0:T(8,128)S(1)} %get-tuple-element.34.kept_ref, f32[8,72,256]{2,1,0:T(8,128)S(1)} %all_to_all.25.slot_ref, ...), custom_call_target="tpu_custom_call" | custom-call | tf_op jit(solution)/shard_map/final_kernel/pallas_call | solution.py:803
Async XLA Ops:
  2.5 15.6 %copy-start = (f32[128,256]{1,0:T(8,128)S(1)}, f32[128,256]{1,0:T(8,128)}, u32[]{:S(2)}) copy-start(f32[128,256]{1,0:T(8,128)} %perm_ref.5) | copy-start | bytes 393220
  2.6 15.6 %copy-start.1 = (f32[2,128,256]{2,1,0:T(8,128)S(1)}, f32[2,128,256]{2,1,0:T(8,128)}, u32[]{:S(2)}) copy-start(f32[2,128,256]{2,1,0:T(8,128)} %state_ref.1) | copy-start | bytes 786436
  2.6 15.6 %copy-start.2 = (f32[1,8192]{1,0:T(1,128)S(1)}, f32[1,8192]{1,0:T(1,128)}, u32[]{:S(2)}) copy-start(f32[1,8192]{1,0:T(1,128)} %param.12) | copy-start | bytes 98308
  2.6 15.6 %copy-start.3 = (f32[2,1,8192]{2,1,0:T(1,128)S(1)}, f32[2,1,8192]{2,1,0:T(1,128)}, u32[]{:S(2)}) copy-start(f32[2,1,8192]{2,1,0:T(1,128)} %param.11) | copy-start | bytes 196612
  20.2 12.7 %copy-start.4 = (s32[1,1,8,256]{3,2,1,0:T(8,128)S(1)}, s32[1,1,8,256]{3,2,1,0:T(8,128)}, u32[]{:S(2)}) copy-start(s32[1,1,8,256]{3,2,1,0:T(8,128)} %param.13) | copy-start | bytes 24580

commit v13 on v12

--- a/solution.py
+++ b/solution.py
@@ -335,16 +335,25 @@
         )
     right, left = taker(0, 1)(0, SUB), taker(0, -1)(0, SUB)
     turned = jnp.transpose(
-        jnp.concatenate([right, jnp.zeros((LANES - 2 * SUB, rows), F32), left], axis=0)
+        jnp.concatenate(
+            [
+                right[:DEPTH],
+                jnp.zeros((LANES - 2 * SUB - DEPTH + 2, rows), F32),
+                left[:2],
+                right[2 * DEPTH :],
+                jnp.zeros((1, rows), F32),
+                left[2 : 2 + DEPTH],
+                right[DEPTH : 2 * DEPTH],
+                left[2 + DEPTH :],
+            ],
+            axis=0,
+        )
     )
     lane = iota((rows, LANES), 1)
     q_ext[side, 0:rows, :] = both(turned, turned, lane, DEPTH, LANES)
-    inv_ext[side, 0:rows, :] = both(
-        pltpu.roll(turned, LANES - DEPTH, 1), pltpu.roll(turned, DEPTH, 1), lane, DEPTH, LANES
-    )
-    p_ext[side, 0:rows, :] = both(
-        pltpu.roll(turned, LANES - 2 * DEPTH, 1), pltpu.roll(turned, 2 * DEPTH, 1), lane, 2, LANES
-    )
+    turned_inv, turned_p = pltpu.roll(turned, 2 * DEPTH, 1), pltpu.roll(turned, 4 * DEPTH, 1)
+    inv_ext[side, 0:rows, :] = both(turned_inv, turned_inv, lane, DEPTH, LANES)
+    p_ext[side, 0:rows, :] = both(turned_p, turned_p, lane, 2, LANES)
     lane = iota((DEPTH, LANES), 1)
     low_right, low_left, high_right, high_left = taker(1, 1), taker(1, -1), taker(-1, 1), taker(-1, -1)
     for i, ext in enumerate((q_ext, inv_ext, p_ext)):
@@ -550,17 +559,6 @@
     seg_hots(slot_ref, hot_ref, row_hot_ref, members, width)
     table = table_of([frac, sat])
     for s in range(members):
-        seg_p, seg_s = seg_gather(slot_ref, hot_ref, rows, s, width, table)
-        cell_p = slot_ref[s, ROW_P : ROW_P + 1, :]
-        weight, water = flow(
-            slot_ref[s, ROW_TRANS : ROW_TRANS + 1, :],
-            slot_ref[s, ROW_UP : ROW_UP + 1, :],
-            cell_p,
-            slot_ref[s, ROW_S : ROW_S + 1, :],
-            seg_p,
-            seg_s,
-        )
-        spread(left_seg_ref, row_hot_ref, s, [weight * cell_p, weight, water])
         o = s
         row, lane = seg_parts(sent_ref, o)
         whole = table_of([slot_ref[o, SUB : SUB + rows, :], slot_ref[o, SUB + rows :, :]])
@@ -574,6 +572,17 @@
             (seg_p, seg_s),
             left_ref,
         )
+        seg_p, seg_s = seg_gather(slot_ref, hot_ref, rows, s, width, table)
+        cell_p = slot_ref[s, ROW_P : ROW_P + 1, :]
+        weight, water = flow(
+            slot_ref[s, ROW_TRANS : ROW_TRANS + 1, :],
+            slot_ref[s, ROW_UP : ROW_UP + 1, :],
+            cell_p,
+            slot_ref[s, ROW_S : ROW_S + 1, :],
+            seg_p,
+            seg_s,
+        )
+        spread(left_seg_ref, row_hot_ref, s, [weight * cell_p, weight, water])
     inflow, total, gained = gathered_sum(left_seg_ref, hot_ref, 3, rows)
     before, after = chain_ends(slot_ref, ROW_ENDS, members)
     new_frac, new_sat = frac_step(frac, sat, load_segs(aperture_ref), before, after, inflow, total, gained)

time: 69.4 us -> 69.2 us (level)
  no operation moved by 1% of the time
where the time goes in v13:
time: 69.2 us; the launch traced here: 68.9 us
  blocking collectives  58.2 us (84%)
  Pallas kernels  9.97 us (14%)
  between operations  0.72 us (1%)
    all_to_all x3, blocking collectives, to_all(): lax.all_to_all(x, ('grp', 'frac'), split_axis=0, concat_axis=0, tiled=True)  35.3 us
    all_to_all x2, blocking collectives, to_group(): return lax.all_to_all(x, 'frac', split_axis=0, concat_axis=0, tiled=True)  22.9 us
    pallas_call x6, Pallas kernels, call(): pl.pallas_call(functools.partial(kernel, *statics), out_shape=outs, in_sp...  9.97 us

profile of v13, /device:TPU:0, one launch (start us, length us, event | category | flops | bytes accessed | tf_op | source)
XLA Modules:
  0.0 68.9 jit_solution(5584577543660108590)
XLA Ops:
  0.6 1.9 %first_kernel.1 = (f32[8,72,256]{2,1,0:T(8,128)S(1)}, bf16[256,2048]{1,0:T(8,128)(2,1)S(1)}, bf16[128,2048]{1,0:T(8,128)(2,1)S(1)}) custom-call(s32[8,256]{1,0:T(8,128)} %bitcast.13, s32[8,256]{1,0:T(8,128)} %bitcast.17, f32[8,256]{1,0:T(8,128)} %bitcast.18, s32[1,8]{1,0:T(1,128)} %bitcast.19, s32[3,8,256]{2,1,0:T(8,128)} %bitcast.16, ...), custom_call_target="tpu_custom_call" | custom-call | tf_op jit(solution)/shard_map/first_kernel/pallas_call | solution.py:812
  2.5 0.0 copy-start
  2.6 0.0 copy-start.1
  2.6 0.0 copy-start.2
  2.6 0.0 copy-start.3
  2.6 15.5 %all_to_all.25.slot_ref = f32[8,72,256]{2,1,0:T(8,128)S(1)} all-to-all(f32[8,72,256]{2,1,0:T(8,128)S(1)} %get-tuple-element.22.sent_ref), channel_id=1, replica_groups=mesh['grp'=4,'frac'=8] {'frac'}, dimensions={0} | all-to-all | bytes 1179648 | tf_op jit(solution)/shard_map/all_to_all | solution.py:858
  18.1 0.0 copy-done
  18.1 0.0 copy-done.1
  18.1 0.0 copy-done.2
  18.2 0.0 copy-done.3
  18.2 2.0 %start_kernel.1 = (f32[384,1,128]{2,1,0:T(1,128)S(1)}, f32[4,128,256]{2,1,0:T(8,128)S(1)}, f32[8,2,256]{2,1,0:T(2,128)S(1)}, f32[2,32,256]{2,1,0:T(8,128)S(1)}, ...) custom-call(f32[8,72,256]{2,1,0:T(8,128)S(1)} %all_to_all.25.slot_ref, ...), custom_call_target="tpu_custom_call" | custom-call | tf_op jit(solution)/shard_map/start_kernel/pallas_call | solution.py:812
  20.2 0.0 copy-start.4
  20.2 12.7 %all_to_all.26.halo_ref.ends_ref = f32[384,1,128]{2,1,0:T(1,128)S(1)} all-to-all(f32[384,1,128]{2,1,0:T(1,128)S(1)} %get-tuple-element.23), channel_id=1, replica_groups=mesh['grp'=4,'frac'=8] {'grp','frac'}, dimensions={0} | all-to-all | bytes 393216 | tf_op jit(solution)/shard_map/all_to_all | solution.py:861
  32.9 0.0 copy-done.4
  32.9 2.1 %middle_kernel.1 = (f32[416,1,128]{2,1,0:T(1,128)S(1)}, f32[4,128,256]{2,1,0:T(8,128)S(1)}) custom-call(f32[384,1,128]{2,1,0:T(1,128)S(1)} %all_to_all.26.halo_ref.ends_ref, s32[8,256]{1,0:T(8,128)S(1)} %bitcast.14, bf16[256,2048]{1,0:T(8,128)(2,1)S(1)} %get-tuple-element.20.cell_hot_ref.hot_ref, ...), custom_call_target="tpu_custom_call" | custom-call | tf_op jit(solution)/shard_map/middle_kernel/pallas_call | solution.py:812
  35.0 11.9 %all_to_all.27.halo_ref = f32[416,1,128]{2,1,0:T(1,128)S(1)} all-to-all(f32[416,1,128]{2,1,0:T(1,128)S(1)} %get-tuple-element.25), channel_id=1, replica_groups=mesh['grp'=4,'frac'=8] {'grp','frac'}, dimensions={0} | all-to-all | bytes 425984 | tf_op jit(solution)/shard_map/all_to_all | solution.py:861
  46.9 1.5 %exchange_kernel.1 = (f32[8,8,256]{2,1,0:T(8,128)S(1)}, f32[2,32,256]{2,1,0:T(8,128)S(1)}, f32[128,256]{1,0:T(8,128)S(1)}) custom-call(f32[416,1,128]{2,1,0:T(1,128)S(1)} %all_to_all.27.halo_ref, s32[8,256]{1,0:T(8,128)S(1)} %bitcast.15, bf16[256,2048]{1,0:T(8,128)(2,1)S(1)} %get-tuple-element.20.cell_hot_ref.hot_ref, ...), custom_call_target="tpu_custom_call" | custom-call | tf_op jit(solution)/shard_map/exchange_kernel/pallas_call | solution.py:812
  48.3 7.4 %all_to_all.28.seg_ref = f32[8,8,256]{2,1,0:T(8,128)S(1)} all-to-all(f32[8,8,256]{2,1,0:T(8,128)S(1)} %get-tuple-element.31.own_ref), channel_id=1, replica_groups=mesh['grp'=4,'frac'=8] {'frac'}, dimensions={0} | all-to-all | bytes 131072 | tf_op jit(solution)/shard_map/all_to_all | solution.py:858
  55.7 1.1 %source_last_kernel.1 = (f32[384,1,128]{2,1,0:T(1,128)S(1)}, f32[3,128,256]{2,1,0:T(8,128)S(1)}) custom-call(bf16[256,2048]{1,0:T(8,128)(2,1)S(1)} %get-tuple-element.20.cell_hot_ref.hot_ref, bf16[128,2048]{1,0:T(8,128)(2,1)S(1)} %get-tuple-element.21.cell_row_hot_ref.row_hot_ref, f32[8,72,256]{2,1,0:T(8,128)S(1)} %get-tuple-element.22.sent_ref, ...), custom_call_target="tpu_custom_call" | custom-call | tf_op jit(solution)/shard_map/source_last_kernel/pallas_call | solution.py:812
  56.8 10.7 %all_to_all.29.halo_ref = f32[384,1,128]{2,1,0:T(1,128)S(1)} all-to-all(f32[384,1,128]{2,1,0:T(1,128)S(1)} %get-tuple-element.33), channel_id=1, replica_groups=mesh['grp'=4,'frac'=8] {'grp','frac'}, dimensions={0} | all-to-all | bytes 393216 | tf_op jit(solution)/shard_map/all_to_all | solution.py:861
  67.5 1.4 %final_kernel.1 = (f32[2,128,256]{2,1,0:T(8,128)}, f32[2,64,128]{2,1,0:T(8,128)}) custom-call(f32[384,1,128]{2,1,0:T(1,128)S(1)} %all_to_all.29.halo_ref, f32[128,256]{1,0:T(8,128)S(1)} %get-tuple-element.32.pressure_ref, f32[3,128,256]{2,1,0:T(8,128)S(1)} %get-tuple-element.34.kept_ref, f32[8,72,256]{2,1,0:T(8,128)S(1)} %all_to_all.25.slot_ref, ...), custom_call_target="tpu_custom_call" | custom-call | tf_op jit(solution)/shard_map/final_kernel/pallas_call | solution.py:812
Async XLA Ops:
  2.5 15.6 %copy-start = (f32[128,256]{1,0:T(8,128)S(1)}, f32[128,256]{1,0:T(8,128)}, u32[]{:S(2)}) copy-start(f32[128,256]{1,0:T(8,128)} %perm_ref.5) | copy-start | bytes 393220
  2.6 15.6 %copy-start.1 = (f32[2,128,256]{2,1,0:T(8,128)S(1)}, f32[2,128,256]{2,1,0:T(8,128)}, u32[]{:S(2)}) copy-start(f32[2,128,256]{2,1,0:T(8,128)} %state_ref.1) | copy-start | bytes 786436
  2.6 15.6 %copy-start.2 = (f32[1,8192]{1,0:T(1,128)S(1)}, f32[1,8192]{1,0:T(1,128)}, u32[]{:S(2)}) copy-start(f32[1,8192]{1,0:T(1,128)} %param.12) | copy-start | bytes 98308
  2.6 15.6 %copy-start.3 = (f32[2,1,8192]{2,1,0:T(1,128)S(1)}, f32[2,1,8192]{2,1,0:T(1,128)}, u32[]{:S(2)}) copy-start(f32[2,1,8192]{2,1,0:T(1,128)} %param.11) | copy-start | bytes 196612
  20.2 12.7 %copy-start.4 = (s32[1,1,8,256]{3,2,1,0:T(8,128)S(1)}, s32[1,1,8,256]{3,2,1,0:T(8,128)}, u32[]{:S(2)}) copy-start(s32[1,1,8,256]{3,2,1,0:T(8,128)} %param.13) | copy-start | bytes 24580

commit v14 on v13

--- a/solution.py
+++ b/solution.py
@@ -462,8 +462,8 @@
             ]
         )
     ]
-    for copy in copies:
-        copy.start()
+    for i in (0, 1, 6, 2, 3, 4, 5):
+        copies[i].start()
     copies[0].wait()
 
     def make_hots(o):
@@ -476,8 +476,7 @@
         make_hots(o)
     copies[1].wait()
     table = table_of([state_ref[0], state_ref[1]])
-    for copy in copies[2:]:
-        copy.wait()
+    copies[6].wait()
     frac = load_segs(frac_ref, 0)
     ends = ends_of(frac)
     left, right = edge_columns(state_ref[0])
@@ -489,15 +488,19 @@
         one = slice(o, o + 1)
         row, _ = cell_parts(cell_ref[one, :], columns)
         cell_p, cell_s = pick(table, 2, rows, row, hot_ref[:, o * width : (o + 1) * width])
+        out_ref[o, ROW_P : ROW_P + 1, :] = cell_p
+        out_ref[o, ROW_S : ROW_S + 1, :] = cell_s
+        out_ref[o, ROW_ENDS : ROW_ENDS + 1, :] = jnp.where(me + 1 == o, to_right, to_left)
+        out_ref[o, SUB:, :] = whole
+    for copy in copies[2:6]:
+        copy.wait()
+    for o in range(members):
+        one = slice(o, o + 1)
         live = iota((1, width), 1) < count_ref[0, o]
         out_ref[o, ROW_SEG : ROW_SEG + 1, :] = seg_ref[one, :].astype(F32)
         out_ref[o, ROW_TRANS : ROW_TRANS + 1, :] = jnp.where(live, trans_ref[one, :], 0.0)
         for t in range(ITERS):
             out_ref[o, ROW_UP + t : ROW_UP + t + 1, :] = up_ref[t, one, :].astype(F32)
-        out_ref[o, ROW_P : ROW_P + 1, :] = cell_p
-        out_ref[o, ROW_S : ROW_S + 1, :] = cell_s
-        out_ref[o, ROW_ENDS : ROW_ENDS + 1, :] = jnp.where(me + 1 == o, to_right, to_left)
-        out_ref[o, SUB:, :] = whole
 
 
 def seg_parts(slot_ref, s):

time: 69.2 us -> 69.2 us (level)
  no operation moved by 1% of the time
where the time goes in v14:
time: 69.2 us; the launch traced here: 68.9 us
  blocking collectives  58.2 us (84%)
  Pallas kernels  9.96 us (14%)
  between operations  0.72 us (1%)
    all_to_all x3, blocking collectives, to_all(): lax.all_to_all(x, ('grp', 'frac'), split_axis=0, concat_axis=0, tiled=True)  35.3 us
    all_to_all x2, blocking collectives, to_group(): return lax.all_to_all(x, 'frac', split_axis=0, concat_axis=0, tiled=True)  22.9 us
    pallas_call x6, Pallas kernels, call(): pl.pallas_call(functools.partial(kernel, *statics), out_shape=outs, in_sp...  9.96 us

profile of v14, /device:TPU:0, one launch (start us, length us, event | category | flops | bytes accessed | tf_op | source)
XLA Modules:
  0.0 68.9 jit_solution(15625277886691750651)
XLA Ops:
  0.6 1.9 %first_kernel.1 = (f32[8,72,256]{2,1,0:T(8,128)S(1)}, bf16[256,2048]{1,0:T(8,128)(2,1)S(1)}, bf16[128,2048]{1,0:T(8,128)(2,1)S(1)}) custom-call(s32[8,256]{1,0:T(8,128)} %bitcast.13, s32[8,256]{1,0:T(8,128)} %bitcast.17, f32[8,256]{1,0:T(8,128)} %bitcast.18, s32[1,8]{1,0:T(1,128)} %bitcast.19, s32[3,8,256]{2,1,0:T(8,128)} %bitcast.16, ...), custom_call_target="tpu_custom_call" | custom-call | tf_op jit(solution)/shard_map/first_kernel/pallas_call | solution.py:815
  2.5 0.0 copy-start
  2.6 0.0 copy-start.1
  2.6 0.0 copy-start.2
  2.6 0.0 copy-start.3
  2.6 15.5 %all_to_all.25.slot_ref = f32[8,72,256]{2,1,0:T(8,128)S(1)} all-to-all(f32[8,72,256]{2,1,0:T(8,128)S(1)} %get-tuple-element.22.sent_ref), channel_id=1, replica_groups=mesh['grp'=4,'frac'=8] {'frac'}, dimensions={0} | all-to-all | bytes 1179648 | tf_op jit(solution)/shard_map/all_to_all | solution.py:861
  18.1 0.0 copy-done
  18.1 0.0 copy-done.1
  18.1 0.0 copy-done.2
  18.1 0.0 copy-done.3
  18.2 2.0 %start_kernel.1 = (f32[384,1,128]{2,1,0:T(1,128)S(1)}, f32[4,128,256]{2,1,0:T(8,128)S(1)}, f32[8,2,256]{2,1,0:T(2,128)S(1)}, f32[2,32,256]{2,1,0:T(8,128)S(1)}, ...) custom-call(f32[8,72,256]{2,1,0:T(8,128)S(1)} %all_to_all.25.slot_ref, ...), custom_call_target="tpu_custom_call" | custom-call | tf_op jit(solution)/shard_map/start_kernel/pallas_call | solution.py:815
  20.2 0.0 copy-start.4
  20.2 12.7 %all_to_all.26.halo_ref.ends_ref = f32[384,1,128]{2,1,0:T(1,128)S(1)} all-to-all(f32[384,1,128]{2,1,0:T(1,128)S(1)} %get-tuple-element.23), channel_id=1, replica_groups=mesh['grp'=4,'frac'=8] {'grp','frac'}, dimensions={0} | all-to-all | bytes 393216 | tf_op jit(solution)/shard_map/all_to_all | solution.py:864
  32.9 0.0 copy-done.4
  32.9 2.1 %middle_kernel.1 = (f32[416,1,128]{2,1,0:T(1,128)S(1)}, f32[4,128,256]{2,1,0:T(8,128)S(1)}) custom-call(f32[384,1,128]{2,1,0:T(1,128)S(1)} %all_to_all.26.halo_ref.ends_ref, s32[8,256]{1,0:T(8,128)S(1)} %bitcast.14, bf16[256,2048]{1,0:T(8,128)(2,1)S(1)} %get-tuple-element.20.cell_hot_ref.hot_ref, ...), custom_call_target="tpu_custom_call" | custom-call | tf_op jit(solution)/shard_map/middle_kernel/pallas_call | solution.py:815
  35.0 11.9 %all_to_all.27.halo_ref = f32[416,1,128]{2,1,0:T(1,128)S(1)} all-to-all(f32[416,1,128]{2,1,0:T(1,128)S(1)} %get-tuple-element.25), channel_id=1, replica_groups=mesh['grp'=4,'frac'=8] {'grp','frac'}, dimensions={0} | all-to-all | bytes 425984 | tf_op jit(solution)/shard_map/all_to_all | solution.py:864
  46.9 1.5 %exchange_kernel.1 = (f32[8,8,256]{2,1,0:T(8,128)S(1)}, f32[2,32,256]{2,1,0:T(8,128)S(1)}, f32[128,256]{1,0:T(8,128)S(1)}) custom-call(f32[416,1,128]{2,1,0:T(1,128)S(1)} %all_to_all.27.halo_ref, s32[8,256]{1,0:T(8,128)S(1)} %bitcast.15, bf16[256,2048]{1,0:T(8,128)(2,1)S(1)} %get-tuple-element.20.cell_hot_ref.hot_ref, ...), custom_call_target="tpu_custom_call" | custom-call | tf_op jit(solution)/shard_map/exchange_kernel/pallas_call | solution.py:815
  48.3 7.4 %all_to_all.28.seg_ref = f32[8,8,256]{2,1,0:T(8,128)S(1)} all-to-all(f32[8,8,256]{2,1,0:T(8,128)S(1)} %get-tuple-element.31.own_ref), channel_id=1, replica_groups=mesh['grp'=4,'frac'=8] {'frac'}, dimensions={0} | all-to-all | bytes 131072 | tf_op jit(solution)/shard_map/all_to_all | solution.py:861
  55.7 1.1 %source_last_kernel.1 = (f32[384,1,128]{2,1,0:T(1,128)S(1)}, f32[3,128,256]{2,1,0:T(8,128)S(1)}) custom-call(bf16[256,2048]{1,0:T(8,128)(2,1)S(1)} %get-tuple-element.20.cell_hot_ref.hot_ref, bf16[128,2048]{1,0:T(8,128)(2,1)S(1)} %get-tuple-element.21.cell_row_hot_ref.row_hot_ref, f32[8,72,256]{2,1,0:T(8,128)S(1)} %get-tuple-element.22.sent_ref, ...), custom_call_target="tpu_custom_call" | custom-call | tf_op jit(solution)/shard_map/source_last_kernel/pallas_call | solution.py:815
  56.8 10.7 %all_to_all.29.halo_ref = f32[384,1,128]{2,1,0:T(1,128)S(1)} all-to-all(f32[384,1,128]{2,1,0:T(1,128)S(1)} %get-tuple-element.33), channel_id=1, replica_groups=mesh['grp'=4,'frac'=8] {'grp','frac'}, dimensions={0} | all-to-all | bytes 393216 | tf_op jit(solution)/shard_map/all_to_all | solution.py:864
  67.5 1.4 %final_kernel.1 = (f32[2,128,256]{2,1,0:T(8,128)}, f32[2,64,128]{2,1,0:T(8,128)}) custom-call(f32[384,1,128]{2,1,0:T(1,128)S(1)} %all_to_all.29.halo_ref, f32[128,256]{1,0:T(8,128)S(1)} %get-tuple-element.32.pressure_ref, f32[3,128,256]{2,1,0:T(8,128)S(1)} %get-tuple-element.34.kept_ref, f32[8,72,256]{2,1,0:T(8,128)S(1)} %all_to_all.25.slot_ref, ...), custom_call_target="tpu_custom_call" | custom-call | tf_op jit(solution)/shard_map/final_kernel/pallas_call | solution.py:815
Async XLA Ops:
  2.5 15.6 %copy-start = (f32[128,256]{1,0:T(8,128)S(1)}, f32[128,256]{1,0:T(8,128)}, u32[]{:S(2)}) copy-start(f32[128,256]{1,0:T(8,128)} %perm_ref.5) | copy-start | bytes 393220
  2.6 15.6 %copy-start.1 = (f32[2,128,256]{2,1,0:T(8,128)S(1)}, f32[2,128,256]{2,1,0:T(8,128)}, u32[]{:S(2)}) copy-start(f32[2,128,256]{2,1,0:T(8,128)} %state_ref.1) | copy-start | bytes 786436
  2.6 15.6 %copy-start.2 = (f32[1,8192]{1,0:T(1,128)S(1)}, f32[1,8192]{1,0:T(1,128)}, u32[]{:S(2)}) copy-start(f32[1,8192]{1,0:T(1,128)} %param.12) | copy-start | bytes 98308
  2.6 15.6 %copy-start.3 = (f32[2,1,8192]{2,1,0:T(1,128)S(1)}, f32[2,1,8192]{2,1,0:T(1,128)}, u32[]{:S(2)}) copy-start(f32[2,1,8192]{2,1,0:T(1,128)} %param.11) | copy-start | bytes 196612
  20.2 12.7 %copy-start.4 = (s32[1,1,8,256]{3,2,1,0:T(8,128)S(1)}, s32[1,1,8,256]{3,2,1,0:T(8,128)}, u32[]{:S(2)}) copy-start(s32[1,1,8,256]{3,2,1,0:T(8,128)} %param.13) | copy-start | bytes 24580

commit v15 on v14

--- a/solution.py
+++ b/solution.py
@@ -782,8 +782,15 @@
 
 def final_kernel(
     groups, members, size, halo_ref, pressure_ref, kept_ref, slot_ref, hot_ref, row_hot_ref, own_ref, seg_ref,
-    frac_ref, aperture_ref, out_ref, new_ref, left_ref, *scratch,
+    frac_ref, aperture_ref, out_any, new_any, left_ref, field_ref, new_ref, sem, *scratch,
 ):
+    copies = [
+        pltpu.make_async_copy(source, target, sem.at[i])
+        for i, (source, target) in enumerate(
+            [(kept_ref.at[0], out_any.at[1]), (new_ref, new_any), (field_ref, out_any.at[0])]
+        )
+    ]
+    copies[0].start()
     new_frac, new_sat = owner_update(
         members,
         2,
@@ -800,23 +807,26 @@
     )
     store_segs(new_ref, 0, new_frac)
     store_segs(new_ref, 1, new_sat)
+    copies[1].start()
     chebyshev(
-        halo_ref, kept_ref.at[1], kept_ref.at[2], pressure_ref, out_ref.at[0], scratch, groups, members, size, True
-    )
-    out_ref[1] = kept_ref[0]
+        halo_ref, kept_ref.at[1], kept_ref.at[2], pressure_ref, field_ref, scratch, groups, members, size, True
+    )
+    copies[2].start()
+    for copy in copies:
+        copy.wait()
 
 
 VMEM = pl.BlockSpec(memory_space=pltpu.VMEM)
 HBM = pl.BlockSpec(memory_space=pltpu.HBM)
 
 
-def call(kernel, statics, outs, scratch, *args, spec=VMEM):
+def call(kernel, statics, outs, scratch, *args, spec=VMEM, out_spec=VMEM):
     outs = [o if hasattr(o, "dtype") else jax.ShapeDtypeStruct(o, F32) for o in outs]
     return pl.pallas_call(
         functools.partial(kernel, *statics),
         out_shape=outs,
         in_specs=[spec] * len(args),
-        out_specs=[VMEM] * len(outs),
+        out_specs=[out_spec] * len(outs),
         scratch_shapes=scratch,
         compiler_params=pltpu.CompilerParams(vmem_limit_bytes=32 * 1024 * 1024),
         name=kernel.__name__,
@@ -916,8 +926,9 @@
         final_kernel,
         both,
         [matrix_state.shape, frac.shape],
-        [left_seg] + ext,
+        [left_seg, pltpu.VMEM((rows, columns), F32), pltpu.VMEM(frac.shape, F32), pltpu.SemaphoreType.DMA((3,))] + ext,
         around, pressure, kept, slot, hot, row_hot, own, segs, frac2, aperture,
+        out_spec=HBM,
     )
     return matrix_out, frac3.reshape(frac_state.shape)
 

time: 69.2 us -> 69.2 us (level)
  no operation moved by 1% of the time
where the time goes in v15:
time: 69.2 us; the launch traced here: 68.9 us
  blocking collectives  58.2 us (84%)
  Pallas kernels  9.94 us (14%)
  between operations  0.72 us (1%)
    all_to_all x3, blocking collectives, to_all(): lax.all_to_all(x, ('grp', 'frac'), split_axis=0, concat_axis=0, tiled=True)  35.3 us
    all_to_all x2, blocking collectives, to_group(): return lax.all_to_all(x, 'frac', split_axis=0, concat_axis=0, tiled=True)  22.9 us
    pallas_call x6, Pallas kernels, call(): pl.pallas_call(functools.partial(kernel, *statics), out_shape=outs, in_sp...  9.94 us

profile of v15, /device:TPU:0, one launch (start us, length us, event | category | flops | bytes accessed | tf_op | source)
XLA Modules:
  0.0 68.9 jit_solution(11319654234946193183)
XLA Ops:
  0.6 1.9 %first_kernel.1 = (f32[8,72,256]{2,1,0:T(8,128)S(1)}, bf16[256,2048]{1,0:T(8,128)(2,1)S(1)}, bf16[128,2048]{1,0:T(8,128)(2,1)S(1)}) custom-call(s32[8,256]{1,0:T(8,128)} %bitcast.13, s32[8,256]{1,0:T(8,128)} %bitcast.17, f32[8,256]{1,0:T(8,128)} %bitcast.18, s32[1,8]{1,0:T(1,128)} %bitcast.19, s32[3,8,256]{2,1,0:T(8,128)} %bitcast.16, ...), custom_call_target="tpu_custom_call" | custom-call | tf_op jit(solution)/shard_map/first_kernel/pallas_call | solution.py:825
  2.5 0.0 copy-start
  2.6 0.0 copy-start.1
  2.6 0.0 copy-start.2
  2.6 0.0 copy-start.3
  2.6 15.5 %all_to_all.25.slot_ref = f32[8,72,256]{2,1,0:T(8,128)S(1)} all-to-all(f32[8,72,256]{2,1,0:T(8,128)S(1)} %get-tuple-element.22.sent_ref), channel_id=1, replica_groups=mesh['grp'=4,'frac'=8] {'frac'}, dimensions={0} | all-to-all | bytes 1179648 | tf_op jit(solution)/shard_map/all_to_all | solution.py:871
  18.1 0.0 copy-done
  18.1 0.0 copy-done.1
  18.1 0.0 copy-done.2
  18.1 0.0 copy-done.3
  18.2 2.0 %start_kernel.1 = (f32[384,1,128]{2,1,0:T(1,128)S(1)}, f32[4,128,256]{2,1,0:T(8,128)S(1)}, f32[8,2,256]{2,1,0:T(2,128)S(1)}, f32[2,32,256]{2,1,0:T(8,128)S(1)}, ...) custom-call(f32[8,72,256]{2,1,0:T(8,128)S(1)} %all_to_all.25.slot_ref, ...), custom_call_target="tpu_custom_call" | custom-call | tf_op jit(solution)/shard_map/start_kernel/pallas_call | solution.py:825
  20.2 0.0 copy-start.4
  20.2 12.7 %all_to_all.26.halo_ref.ends_ref = f32[384,1,128]{2,1,0:T(1,128)S(1)} all-to-all(f32[384,1,128]{2,1,0:T(1,128)S(1)} %get-tuple-element.23), channel_id=1, replica_groups=mesh['grp'=4,'frac'=8] {'grp','frac'}, dimensions={0} | all-to-all | bytes 393216 | tf_op jit(solution)/shard_map/all_to_all | solution.py:874
  32.9 0.0 copy-done.4
  32.9 2.1 %middle_kernel.1 = (f32[416,1,128]{2,1,0:T(1,128)S(1)}, f32[4,128,256]{2,1,0:T(8,128)S(1)}) custom-call(f32[384,1,128]{2,1,0:T(1,128)S(1)} %all_to_all.26.halo_ref.ends_ref, s32[8,256]{1,0:T(8,128)S(1)} %bitcast.14, bf16[256,2048]{1,0:T(8,128)(2,1)S(1)} %get-tuple-element.20.cell_hot_ref.hot_ref, ...), custom_call_target="tpu_custom_call" | custom-call | tf_op jit(solution)/shard_map/middle_kernel/pallas_call | solution.py:825
  35.0 11.9 %all_to_all.27.halo_ref = f32[416,1,128]{2,1,0:T(1,128)S(1)} all-to-all(f32[416,1,128]{2,1,0:T(1,128)S(1)} %get-tuple-element.25), channel_id=1, replica_groups=mesh['grp'=4,'frac'=8] {'grp','frac'}, dimensions={0} | all-to-all | bytes 425984 | tf_op jit(solution)/shard_map/all_to_all | solution.py:874
  46.9 1.5 %exchange_kernel.1 = (f32[8,8,256]{2,1,0:T(8,128)S(1)}, f32[2,32,256]{2,1,0:T(8,128)S(1)}, f32[128,256]{1,0:T(8,128)S(1)}) custom-call(f32[416,1,128]{2,1,0:T(1,128)S(1)} %all_to_all.27.halo_ref, s32[8,256]{1,0:T(8,128)S(1)} %bitcast.15, bf16[256,2048]{1,0:T(8,128)(2,1)S(1)} %get-tuple-element.20.cell_hot_ref.hot_ref, ...), custom_call_target="tpu_custom_call" | custom-call | tf_op jit(solution)/shard_map/exchange_kernel/pallas_call | solution.py:825
  48.3 7.4 %all_to_all.28.seg_ref = f32[8,8,256]{2,1,0:T(8,128)S(1)} all-to-all(f32[8,8,256]{2,1,0:T(8,128)S(1)} %get-tuple-element.31.own_ref), channel_id=1, replica_groups=mesh['grp'=4,'frac'=8] {'frac'}, dimensions={0} | all-to-all | bytes 131072 | tf_op jit(solution)/shard_map/all_to_all | solution.py:871
  55.7 1.1 %source_last_kernel.1 = (f32[384,1,128]{2,1,0:T(1,128)S(1)}, f32[3,128,256]{2,1,0:T(8,128)S(1)}) custom-call(bf16[256,2048]{1,0:T(8,128)(2,1)S(1)} %get-tuple-element.20.cell_hot_ref.hot_ref, bf16[128,2048]{1,0:T(8,128)(2,1)S(1)} %get-tuple-element.21.cell_row_hot_ref.row_hot_ref, f32[8,72,256]{2,1,0:T(8,128)S(1)} %get-tuple-element.22.sent_ref, ...), custom_call_target="tpu_custom_call" | custom-call | tf_op jit(solution)/shard_map/source_last_kernel/pallas_call | solution.py:825
  56.8 10.7 %all_to_all.29.halo_ref = f32[384,1,128]{2,1,0:T(1,128)S(1)} all-to-all(f32[384,1,128]{2,1,0:T(1,128)S(1)} %get-tuple-element.33), channel_id=1, replica_groups=mesh['grp'=4,'frac'=8] {'grp','frac'}, dimensions={0} | all-to-all | bytes 393216 | tf_op jit(solution)/shard_map/all_to_all | solution.py:874
  67.5 1.4 %final_kernel.1 = (f32[2,128,256]{2,1,0:T(8,128)}, f32[2,64,128]{2,1,0:T(8,128)}) custom-call(f32[384,1,128]{2,1,0:T(1,128)S(1)} %all_to_all.29.halo_ref, f32[128,256]{1,0:T(8,128)S(1)} %get-tuple-element.32.pressure_ref, f32[3,128,256]{2,1,0:T(8,128)S(1)} %get-tuple-element.34.kept_ref, f32[8,72,256]{2,1,0:T(8,128)S(1)} %all_to_all.25.slot_ref, ...), custom_call_target="tpu_custom_call" | custom-call | tf_op jit(solution)/shard_map/final_kernel/pallas_call | solution.py:825
Async XLA Ops:
  2.5 15.6 %copy-start = (f32[128,256]{1,0:T(8,128)S(1)}, f32[128,256]{1,0:T(8,128)}, u32[]{:S(2)}) copy-start(f32[128,256]{1,0:T(8,128)} %perm_ref.5) | copy-start | bytes 393220
  2.6 15.6 %copy-start.1 = (f32[2,128,256]{2,1,0:T(8,128)S(1)}, f32[2,128,256]{2,1,0:T(8,128)}, u32[]{:S(2)}) copy-start(f32[2,128,256]{2,1,0:T(8,128)} %state_ref.1) | copy-start | bytes 786436
  2.6 15.6 %copy-start.2 = (f32[1,8192]{1,0:T(1,128)S(1)}, f32[1,8192]{1,0:T(1,128)}, u32[]{:S(2)}) copy-start(f32[1,8192]{1,0:T(1,128)} %param.12) | copy-start | bytes 98308
  2.6 15.6 %copy-start.3 = (f32[2,1,8192]{2,1,0:T(1,128)S(1)}, f32[2,1,8192]{2,1,0:T(1,128)}, u32[]{:S(2)}) copy-start(f32[2,1,8192]{2,1,0:T(1,128)} %param.11) | copy-start | bytes 196612
  20.2 12.7 %copy-start.4 = (s32[1,1,8,256]{3,2,1,0:T(8,128)S(1)}, s32[1,1,8,256]{3,2,1,0:T(8,128)}, u32[]{:S(2)}) copy-start(s32[1,1,8,256]{3,2,1,0:T(8,128)} %param.13) | copy-start | bytes 24580
